TPU v7x, 128 devices: a whole 4x4x4 slice. The times are simulated.
128 devices in a mesh: dp: 32 (over x, z, y_lo), mp: 4 (over y_hi, core).
Axes of the slice: x: 4, y: 4 (y_hi: 2, y_lo: 2; y = y_hi * 2 + y_lo), z: 4, core: 2. Of those that a mesh axis runs over, the one named last changes fastest.
Arguments:
- tokens: bfloat16 [8192, 2048], P('dp'), may hold values from -6 to 6
- targets: bfloat16 [8192, 2048], P('dp'), may hold values from -6 to 6
- loss_weights: float32 [8192], P('dp'), may hold values from 0.4 to 14, as said below
- segments: int32 [32, 256], P('dp'), may hold values from 0 to 3, never falling along the last dimension, each value on 1 to 128 neighbouring positions
- probe_model: int32 [32, 2048], P('dp'), may hold values from 0 to 1
- probe_heads: int32 [32, 2, 2048], P('dp', None, 'mp'), may hold values from 0 to 1
- norm_gain: float32 [2048], replicated, may hold values from 0.5 to 1.5
- w_query: bfloat16 [2048, 2048], P(None, 'mp'), may hold values from -0.125 to 0.125
- w_key: bfloat16 [2048, 2048], P(None, 'mp'), may hold values from -0.125 to 0.125
- w_value: bfloat16 [2048, 2048], P(None, 'mp'), may hold values from -0.125 to 0.125
- w_out: bfloat16 [2048, 2048], P('mp'), may hold values from -0.125 to 0.125
Outputs:
- diag_query: float32 [2048, 2048], P('dp', 'mp')
- diag_key: float32 [2048, 2048], P('dp', 'mp')
- mean_diag: float32 [2], replicated
Inputs may be any that keep to these rules, and one draw needn't show every extreme that they name: `segments`: the documents of a sequence are runs of 1 to 128 tokens, numbered upwards from 0. `loss_weights`: positive weights.
All inputs are finite; a program needn't handle non-finite values.
Results may differ from a plain program's by a relative error of at most 0.0099.
Values may be sent and summed in bfloat16 or wider, within the bound.
No kernel may reach another device: no remote copies, remote signals or barrier semaphores. Data moves between devices by JAX's collectives and lax.ppermute only.
A program may use at most 128 MiB of HBM per device.

v0:
```python
import functools

import jax
import jax.numpy as jnp
import numpy as np
from jax import lax
from jax.experimental import pallas as pl
from jax.experimental.pallas import tpu as pltpu
from jax.sharding import Mesh
from jax.sharding import PartitionSpec as P


HEAD_DIM = 128
PRIME = 32749
EPSILON = 1e-06
SCALE = HEAD_DIM**-0.5
MIB = 1 << 20
DP = ("xh", "xl", "z", "yl")
MP = ("yh", "c")
bf16, f32, i32 = jnp.bfloat16, jnp.float32, jnp.int32
VMEM = pl.BlockSpec(memory_space=pltpu.VMEM)
ANY = pl.BlockSpec(memory_space=pl.ANY)
HBM = pl.BlockSpec(memory_space=pltpu.HBM)


def shape(dims, kind):
    return jax.ShapeDtypeStruct(dims, kind)


def call(body, outs, ins, scratch=(), flops=0, moved=0, limit=24, after=()):
    count = len(ins)

    def whole(*refs):
        return body(*refs[:count], *refs[count + len(after) :])

    kernel = pl.pallas_call(
        whole,
        out_shape=outs,
        in_specs=list(ins) + [ANY] * len(after),
        out_specs=jax.tree.map(lambda _: VMEM, outs),
        scratch_shapes=scratch,
        cost_estimate=pl.CostEstimate(flops=flops, bytes_accessed=moved, transcendentals=0),
        compiler_params=pltpu.CompilerParams(vmem_limit_bytes=limit * MIB),
    )

    def run(*args):
        return kernel(*args, *after)

    return run


def dot(a, b):
    return jnp.dot(a, b, preferred_element_type=f32)


def dot_nt(a, b):
    return lax.dot_general(a, b, (((1,), (1,)), ((), ())), preferred_element_type=f32)


def dot_tn(a, b):
    return lax.dot_general(a, b, (((0,), (0,)), ((), ())), preferred_element_type=f32)


def head(h):
    return slice(h * HEAD_DIM, (h + 1) * HEAD_DIM)


def rotate(x, cosine, sine):
    return x * cosine + pltpu.roll(x, HEAD_DIM // 2, 1) * sine


def rope_tables(length):
    position = np.arange(length, dtype=np.float32)
    exponent = np.arange(0, HEAD_DIM, 2, dtype=np.float32) / np.float32(HEAD_DIM)
    frequency = np.power(10000.0, -exponent.astype(np.float64)).astype(np.float32)
    angles = (position[:, None] * frequency[None, :]).astype(np.float64)
    cosine, sine = np.cos(angles), np.sin(angles)
    return (
        np.concatenate([cosine, cosine], axis=1).astype(np.float32),
        np.concatenate([-sine, sine], axis=1).astype(np.float32),
    )


def split3(value):
    high = value.astype(bf16)
    rest = value - high.astype(f32)
    middle = rest.astype(bf16)
    low = (rest - middle.astype(f32)).astype(bf16)
    return high, middle, low


def forward_body(
    tok_hbm, gain_hbm, wq_hbm, wk_hbm, table_hbm, seg_hbm, wv_hbm, wo_hbm,
    normed_out, q_out, k_out, v_out, p_out, send_out, own_out,
    tok, gain, wq, wk, table, seg, wv, wo, sems,
):
    sources = (tok_hbm, gain_hbm, wq_hbm, wk_hbm, table_hbm, seg_hbm, wv_hbm, wo_hbm)
    places = (tok, gain, wq, wk, table, seg, wv, wo)
    copies = [pltpu.make_async_copy(s, d, sems.at[i]) for i, (s, d) in enumerate(zip(sources, places))]
    for copy in copies:
        copy.start()
    length = tok.shape[0]
    heads = q_out.shape[1] // HEAD_DIM
    half = send_out.shape[1]
    core = lax.axis_index("c")
    copies[0].wait()
    copies[1].wait()
    tokens = tok[...].astype(f32)
    inverse = lax.rsqrt(jnp.mean(tokens * tokens, axis=1, keepdims=True) + EPSILON)
    normed = (tokens * inverse * gain[...]).astype(bf16)
    normed_out[...] = normed
    copies[2].wait()
    query = dot(normed, wq[...])
    copies[3].wait()
    keys = dot(normed, wk[...])
    for copy in copies[4:7]:
        copy.wait()
    values = dot(normed, wv[...]).astype(bf16)
    v_out[...] = values
    document = jnp.broadcast_to(seg[...].astype(f32), (length, length))
    row = lax.broadcasted_iota(i32, (length, length), 0)
    col = lax.broadcasted_iota(i32, (length, length), 1)
    allowed = (row >= col) & (document == document.T)
    attended = []
    for h in range(heads):
        q = rotate(query[:, head(h)], table[:length], table[length:])
        k = rotate(keys[:, head(h)], table[:length], table[length:])
        q_high, k_high = q.astype(bf16), k.astype(bf16)
        q_low = (q - q_high.astype(f32)).astype(bf16)
        k_low = (k - k_high.astype(f32)).astype(bf16)
        q_out[:, head(h)] = q_high
        k_out[:, head(h)] = k_high
        scores = dot_nt(
            jnp.concatenate([q_high, q_low], axis=1), jnp.concatenate([k_high, k_high], axis=1)
        ) + dot_nt(q_high, k_low)
        raised = jnp.where(allowed, jnp.exp(scores * SCALE), 0.0)
        weights = raised * (1.0 / jnp.sum(raised, axis=1, keepdims=True))
        p_out[h] = weights
        attended.append(dot(weights.astype(bf16), values[:, head(h)]).astype(bf16))
    attended = jnp.concatenate(attended, axis=1)
    copies[7].wait()
    mine = pl.multiple_of(core * half, half)
    other = pl.multiple_of((1 - core) * half, half)
    send_out[...] = dot(attended, wo[:, pl.ds(other, half)]).astype(bf16)
    own_out[...] = dot(attended, wo[:, pl.ds(mine, half)])


def small_mod(value):
    estimate = jnp.floor(value.astype(f32) * (1.0 / PRIME)).astype(i32)
    rest = value - estimate * PRIME
    rest = jnp.where(rest < 0, rest + PRIME, rest)
    return jnp.where(rest >= PRIME, rest - PRIME, rest)


def square_state(row0, col0, dims):
    row = row0 + lax.broadcasted_iota(i32, dims, 0)
    col = col0 + lax.broadcasted_iota(i32, dims, 1)
    mixed = small_mod(row * 1103 + col * 2713 + 7)
    return mixed, small_mod(mixed * mixed)


def sign_of(square):
    tenth = square * 0.1 + 0.05
    return jnp.where(tenth - jnp.floor(tenth) < 0.5, 1.0, -1.0)


STEP = 16
SHIFT = (1103 * STEP) % PRIME


def wrap(value):
    return jnp.where(value >= PRIME, value - PRIME, value)


def fill_pattern(col0, out):
    width, columns = out.shape
    mixed, square = square_state(0, col0, (STEP, columns))
    change = small_mod(mixed * (2 * SHIFT % PRIME) + SHIFT * SHIFT % PRIME)
    second = float(2 * SHIFT * SHIFT % PRIME)

    def step(i, state):
        square, change = state
        out[pl.ds(pl.multiple_of(i * STEP, STEP), STEP), :] = sign_of(square).astype(bf16)
        return wrap(square + change), wrap(change + second)

    lax.fori_loop(0, width // STEP, step, (square.astype(f32), change.astype(f32)))


def tangent_body(
    normed, model_bits, head_bits, table, q_ref, k_ref, v_ref, p_ref, wo,
    dq_out, dk_out, r_out, ds_out, send_out, own_out,
    pattern,
):
    heads = q_ref.shape[1] // HEAD_DIM
    half = send_out.shape[1]
    feat = q_ref.shape[1]
    core = lax.axis_index("c")
    fill_pattern((lax.axis_index("yh") * 2 + core) * feat, pattern)
    sign = (2 * model_bits[...] - 1).astype(f32).astype(bf16)
    product = dot(normed[...] * sign, pattern[...])
    r_out[...] = product
    signs = (2 * head_bits[...] - 1).astype(f32)
    d_query = product * signs[0:1, :]
    d_keys = product * signs[1:2, :]
    cosine, sine = table[: table.shape[0] // 2], table[table.shape[0] // 2 :]
    tangents = []
    for h in range(heads):
        dq = rotate(d_query[:, head(h)], cosine, sine).astype(bf16)
        dk = rotate(d_keys[:, head(h)], cosine, sine).astype(bf16)
        dq_out[:, head(h)] = dq
        dk_out[:, head(h)] = dk
        d_scores = dot_nt(
            jnp.concatenate([dq, q_ref[:, head(h)]], axis=1),
            jnp.concatenate([k_ref[:, head(h)], dk], axis=1),
        ) * SCALE
        weights = p_ref[h]
        centred = d_scores - jnp.sum(weights * d_scores, axis=1, keepdims=True)
        ds_out[h] = centred
        tangents.append(dot((weights * centred).astype(bf16), v_ref[:, head(h)]).astype(bf16))
    tangents = jnp.concatenate(tangents, axis=1)
    mine = pl.multiple_of(core * half, half)
    other = pl.multiple_of((1 - core) * half, half)
    send_out[...] = dot(tangents, wo[:, pl.ds(other, half)]).astype(bf16)
    own_out[...] = dot(tangents, wo[:, pl.ds(mine, half)])


def base_body(tokens, targets, loss_weights, base_out, weight_out):
    half = base_out.shape[1]
    length = base_out.shape[0]
    mine = pl.multiple_of(lax.axis_index("c") * half, half)
    base_out[...] = tokens[:, pl.ds(mine, half)].astype(f32) - targets[:, pl.ds(mine, half)].astype(f32)
    weight_out[...] = jnp.broadcast_to(loss_weights[...] * (1.0 / length), (HEAD_DIM, length)).T


def residual_body(near, far, base, weight, out):
    out[...] = ((near[...].astype(f32) + far[...].astype(f32) + base[...]) * weight[:, 0:1]).astype(bf16)


def d_residual_body(near, far, weight, out):
    out[...] = ((near[...].astype(f32) + far[...].astype(f32)) * weight[:, 0:1]).astype(bf16)


def back_of(res_own, res_mate, wo):
    half = res_own.shape[1]
    core = lax.axis_index("c")
    mine = pl.multiple_of(core * half, half)
    other = pl.multiple_of((1 - core) * half, half)
    return (
        dot_nt(res_own[...], wo[:, pl.ds(mine, half)])
        + dot_nt(res_mate[...], wo[:, pl.ds(other, half)])
    ).astype(bf16)


def second_body(res_own, res_mate, wo, q_ref, k_ref, v_ref, dq_ref, dk_ref, p_ref, ds_ref, hq_out, hk_out):
    back = back_of(res_own, res_mate, wo)
    for h in range(q_ref.shape[1] // HEAD_DIM):
        s = head(h)
        weights = p_ref[h]
        u = dot_nt(back[:, s], v_ref[:, s])
        first = weights * (u - jnp.sum(weights * u, axis=1, keepdims=True))
        curved = first * ds_ref[h]
        second = curved - weights * jnp.sum(curved, axis=1, keepdims=True)
        first, second = first.astype(bf16), second.astype(bf16)
        hq_out[:, s] = dot(first, dk_ref[:, s]) + dot(second, k_ref[:, s])
        hk_out[:, s] = dot_tn(first, dq_ref[:, s]) + dot_tn(second, q_ref[:, s])


def third_body(
    res_own, res_mate, wo, q_ref, k_ref, v_ref, p_ref, hq_ref, hk_ref, r_ref, head_bits, table,
    y_out, sum_out,
):
    feat = q_ref.shape[1]
    back = back_of(res_own, res_mate, wo)
    signs = (2 * head_bits[...] - 1).astype(f32)
    cosine, sine = table[: table.shape[0] // 2], table[table.shape[0] // 2 :]
    totals = [0.0, 0.0]
    for h in range(feat // HEAD_DIM):
        s = head(h)
        weights = p_ref[h]
        u = dot_nt(back[:, s], v_ref[:, s])
        first = (weights * (u - jnp.sum(weights * u, axis=1, keepdims=True))).astype(bf16)
        hq = (hq_ref[:, s] + dot(first, k_ref[:, s])) * SCALE
        hk = (hk_ref[:, s] + dot_tn(first, q_ref[:, s])) * SCALE
        product = r_ref[:, s]
        for i, gradient in enumerate((hq, hk)):
            y = rotate(gradient, cosine, -sine) * signs[i : i + 1, s]
            y = y.astype(bf16)
            y_out[:, i * feat + h * HEAD_DIM : i * feat + (h + 1) * HEAD_DIM] = y
            totals[i] = totals[i] + jnp.sum(product * y.astype(f32), axis=0, keepdims=True)
    pair = [jnp.sum(t, axis=1, keepdims=True) for t in totals]
    lane = lax.broadcasted_iota(i32, sum_out.shape, 1)
    sum_out[...] = jnp.where(lane == 0, pair[0], jnp.where(lane == 1, pair[1], 0.0))


def transpose_body(normed, model_bits, own_out, send_out, whole):
    sign = (2 * model_bits[...] - 1).astype(f32).astype(bf16)
    signed = normed[...] * sign
    for i in range(whole.shape[0] // HEAD_DIM):
        whole[i * HEAD_DIM : (i + 1) * HEAD_DIM, :] = signed[:, i * HEAD_DIM : (i + 1) * HEAD_DIM].T
    rows = whole.shape[0] // 32
    xh, xl, z, yl = (lax.axis_index(axis) for axis in DP)
    for out, low in ((own_out, xl), (send_out, 1 - xl)):
        for ez in range(4):
            for ex in range(2):
                for ey in range(2):
                    to_x = 2 * (xh if ex == 0 else 1 - xh) + low
                    to_z = lax.rem(z + ez, 4)
                    to_y = yl if ey == 0 else 1 - yl
                    start = pl.multiple_of(((to_x * 4 + to_z) * 2 + to_y) * rows, rows)
                    at = ((ez * 2 + ex) * 2 + ey) * rows
                    out[at : at + rows, :] = whole[pl.ds(start, rows), :]


def estimate_body(x_own, x_mate, y_own, y_mate, sums, a0, a1, a2, a3, b0, b1, b2, b3):
    group = b0.shape[0]
    rows = group // 4
    feat = b0.shape[1]
    pieces = jnp.concatenate(
        [part for part in split3(sums[...])] + [jnp.zeros((sums.shape[0], HEAD_DIM), bf16)], axis=1
    )
    for ez, out in enumerate((a0, a1, a2, a3)):
        at = slice(ez * group, (ez + 1) * group)
        part = dot(x_own[at, :], y_own[...]) + dot(x_mate[at, :], y_mate[...])
        if ez == 0:
            out[...] = part[:, :feat]
        else:
            out[:group, :] = part[:, :feat].astype(bf16)
            out[group:, :] = pieces
        for e, to in enumerate((b0, b1, b2, b3)):
            to[ez * rows : (ez + 1) * rows, :] = part[e * rows : (e + 1) * rows, feat:].astype(to.dtype)


def read_sums(part):
    return sum(part[:, i * HEAD_DIM : (i + 1) * HEAD_DIM].astype(f32) for i in range(3))


def middle_body(a0, a1, a2, a3, b0, b1, b2, b3, sums, *outs):
    group = b0.shape[0]
    rows = group // 4
    a = a0[...] + sum(r[:group, :].astype(f32) for r in (a1, a2, a3))
    b = b0[...] + sum(r[...].astype(f32) for r in (b1, b2, b3))
    total = sums[...] + sum(read_sums(r[group:, :]) for r in (a1, a2, a3))
    pieces = jnp.concatenate(list(split3(total)) + [jnp.zeros(total.shape, bf16)], axis=1)
    a_outs, b_outs, sum_out = outs[:4], outs[4:8], outs[8]
    for e, out in enumerate(a_outs):
        part = a[e * rows : (e + 1) * rows, :]
        if e == 0:
            out[...] = part
        else:
            out[:rows, :] = part.astype(bf16)
            out[rows:, :] = pieces
    for e, out in enumerate(b_outs):
        out[...] = b[e * rows : (e + 1) * rows, :].astype(out.dtype)
    sum_out[...] = total


def final_body(a0, a1, a2, a3, b0, b1, b2, b3, sums, diag_query, diag_key, mean_out, *, groups, entries):
    rows, feat = b0.shape
    xh, xl, z, yl = (lax.axis_index(axis) for axis in DP)
    row0 = (((xh * 2 + xl) * 4 + z) * 2 + yl) * rows
    col0 = (lax.axis_index("yh") * 2 + lax.axis_index("c")) * feat
    _, square = square_state(row0, col0, (rows, feat))
    sign = sign_of(square.astype(f32)) * (1.0 / groups)
    diag_query[...] = sign * (a0[...] + sum(r[:rows, :].astype(f32) for r in (a1, a2, a3)))
    diag_key[...] = sign * (b0[...] + sum(r[...].astype(f32) for r in (b1, b2, b3)))
    total = sums[...] + sum(read_sums(r[rows:, :]) for r in (a1, a2, a3))
    mean_out[...] = total * (1.0 / (groups * entries))


def flip(value, moves):
    axes = tuple(axis for axis, _ in moves)
    sizes = [lax.axis_size(axis) for axis in axes]

    def target(index):
        where = []
        for size in reversed(sizes):
            where.append(index % size)
            index //= size
        where = [f(w) for (_, f), w in zip(moves, reversed(where))]
        result = 0
        for w, size in zip(where, sizes):
            result = result * size + w
        return result

    count = int(np.prod(sizes))
    return lax.ppermute(value, axes if len(axes) > 1 else axes[0], [(i, target(i)) for i in range(count)])


def xor(axis, mask):
    return (axis, lambda i: i ^ mask)


def add(axis, k):
    return (axis, lambda i: (i + k) % lax.axis_size(axis))


def local(tokens, targets, loss_weights, segments, probe_model, probe_heads, norm_gain, w_query, w_key, w_value, w_out):
    length, width = tokens.shape
    feat = w_query.shape[1]
    heads = feat // HEAD_DIM
    half = width // 2
    groups = lax.axis_size(DP)
    entries = width * feat * lax.axis_size(MP)
    table = jnp.asarray(np.concatenate(rope_tables(length)))
    head_bits = probe_heads[0]
    mat = shape((length, feat), bf16)
    square = shape((heads, length, length), f32)
    half16, half32 = shape((length, half), bf16), shape((length, half), f32)
    product = 2 * length * width * feat
    small = 2 * length * length * HEAD_DIM * heads
    weight = pltpu.VMEM((width, feat), bf16)

    normed, q, k, v, p, send, own = call(
        forward_body,
        (shape((length, width), bf16), mat, mat, mat, square, half16, half32),
        [HBM] * 8,
        [
            pltpu.VMEM((length, width), bf16), pltpu.VMEM((1, width), f32), weight, weight,
            pltpu.VMEM((2 * length, HEAD_DIM), f32), pltpu.VMEM((1, length), i32),
            weight, pltpu.VMEM((feat, width), bf16), pltpu.SemaphoreType.DMA((8,)),
        ],
        4 * product + 4 * small, 12 * MIB, 50,
    )(tokens, norm_gain[None, :], w_query, w_key, table, segments, w_value, w_out)
    mate = [xor("c", 1)]
    far = [xor("yh", 1)]
    pair = [xor("xl", 1)]
    came = flip(send, mate)
    x_own, x_send = call(
        transpose_body,
        (shape((width // 2, length), bf16),) * 2,
        [VMEM] * 2,
        [pltpu.VMEM((width, length), bf16)],
        0, 3 * MIB, 16,
    )(normed, probe_model)
    x_mate = flip(x_send, pair)
    near = (own + came.astype(f32)).astype(bf16)
    there = flip(near, far)

    dq, dk, r, ds, d_send, d_own = call(
        tangent_body,
        (mat, mat, shape((length, feat), f32), square, half16, half32),
        [VMEM] * 9,
        [pltpu.VMEM((width, feat), bf16)],
        2 * product + 4 * small, 8 * MIB, 32, (near, x_send),
    )(normed, probe_model, head_bits, table, q, k, v, p, w_out)
    d_near = (d_own + flip(d_send, mate).astype(f32)).astype(bf16)
    d_there = flip(d_near, far)

    base, row_weight = call(
        base_body,
        (half32, shape((length, HEAD_DIM), f32)),
        [VMEM] * 3,
        (), 0, 3 * MIB, 16, (d_own,),
    )(tokens, targets, loss_weights[None, :])

    res_own = call(residual_body, half16, [VMEM] * 4, (), 0, 3 * MIB, 16, (d_near, x_mate))(near, there, base, row_weight)
    res_mate = flip(res_own, mate)
    hq, hk = call(
        second_body,
        (shape((length, feat), f32),) * 2,
        [VMEM] * 10,
        (), product + 5 * small, 6 * MIB, 24,
    )(res_own, res_mate, w_out, q, k, v, dq, dk, p, ds)

    d_res_own = call(d_residual_body, half16, [VMEM] * 3, (), 0, 2 * MIB, 16, (hq,))(d_near, d_there, row_weight)
    d_res_mate = flip(d_res_own, mate)
    y, sums = call(
        third_body,
        (shape((length, 2 * feat), bf16), shape((16, HEAD_DIM), f32)),
        [VMEM] * 12,
        (), product + 3 * small, 6 * MIB, 24,
    )(d_res_own, d_res_mate, w_out, q, k, v, p, hq, hk, r, head_bits, table)

    y_mate = flip(y, pair)
    sums = sums + flip(sums, mate)
    sums = sums + flip(sums, far) + flip(sums, pair) + flip(sums, pair + far)

    rows = width // 32
    group = 4 * rows
    a_out, b_out = shape((group + 16, feat), bf16), shape((group, feat), bf16)
    keep = shape((group, feat), f32)
    parts = call(
        estimate_body,
        (keep, a_out, a_out, a_out, keep, b_out, b_out, b_out),
        [VMEM] * 5,
        (), 2 * product, 6 * MIB, 24,
    )(x_own, x_mate, y, y_mate, sums)
    along = [[add("z", 1)], [add("z", 2)], [add("z", 3)]]
    across = [[xor("yl", 1)], [xor("xh", 1)], [xor("xh", 1), xor("yl", 1)]]
    a_in = [flip(m, where) for m, where in zip(parts[1:4], along)]
    b_in = [flip(m, where) for m, where in zip(parts[5:8], across)]
    a_out, b_out = shape((rows + 16, feat), bf16), shape((rows, feat), bf16)
    keep = shape((rows, feat), f32)
    parts = call(
        middle_body,
        (keep, a_out, a_out, a_out, keep, b_out, b_out, b_out, shape((16, HEAD_DIM), f32)),
        [VMEM] * 9,
        (), 0, 3 * MIB, 24,
    )(parts[0], *a_in, parts[4], *b_in, sums)
    a_in = [flip(m, where) for m, where in zip(parts[1:4], across)]
    b_in = [flip(m, where) for m, where in zip(parts[5:8], along)]
    diag_query, diag_key, mean = call(
        functools.partial(final_body, groups=groups, entries=entries),
        (keep, keep, shape((16, HEAD_DIM), f32)),
        [VMEM] * 9,
        (), 0, MIB, 16,
    )(parts[0], *a_in, parts[4], *b_in, parts[8])
    return diag_query, diag_key, mean[0, :2]


def solution(mesh):
    torus = Mesh(mesh.devices.reshape(2, 2, 4, 2, 2, 2), ("xh", "xl", "z", "yl", "yh", "c"))
    return jax.shard_map(
        local,
        mesh=torus,
        in_specs=(
            P(DP, None),
            P(DP, None),
            P(DP),
            P(DP, None),
            P(DP, None),
            P(DP, None, MP),
            P(),
            P(None, MP),
            P(None, MP),
            P(None, MP),
            P(MP, None),
        ),
        out_specs=(P(DP, MP), P(DP, MP), P()),
        check_vma=False,
    )
```

profile of v0, /device:TPU:0, one launch (start us, length us, event | category | flops | bytes accessed | tf_op | source)
XLA Modules:
  0.0 109.7 jit_solution(11596771331290011009)
XLA Ops:
  3.0 7.4 %shard_map.139 = (bf16[256,2048]{1,0:T(8,128)(2,1)S(1)}, bf16[256,512]{1,0:T(8,128)(2,1)S(1)}, bf16[256,512]{1,0:T(8,128)(2,1)S(1)}, bf16[256,512]{1,0:T(8,128)(...) custom-call(bf16[256,2048]{1,0:T(8,128)(2,1)} %refs_0_.3, ...), custom_call_target="tpu_custom_call" | custom-call | flops 2415919104 | bytes 12582912 | tf_op jit(solution)/shard_map/pallas_call | solution.py:47
  10.9 1.5 %collective-permute-done.1 = bf16[256,1024]{1,0:T(8,128)(2,1)S(1)} collective-permute-done((bf16[256,1024]{1,0:T(8,128)(2,1)S(1)}, bf16[256,1024]{1,0:T(8,128)(2,1)S(1)}, u32[]{:S(2)}, u32[]{:S(2)}) %collective-permute-start.1) | collective-permute-done | bytes 524320 | tf_op jit(solution)/shard_map/ppermute | solution.py:386
  12.3 1.4 %add_convert_fusion.1.refs_9_.refs_0_ = bf16[256,1024]{1,0:T(8,128)(2,1)S(1)} fusion(f32[256,1024]{1,0:T(8,128)} %get-tuple-element.51, bf16[256,1024]{1,0:T(8,128)(2,1)S(1)} %collective-permute-done.1), kind=kLoop, calls=%fused_computation.1 | loop fusion | flops 786432 | bytes 2097152 | tf_op jit(solution)/shard_map/convert_element_type | solution.py:436
  13.8 4.6 %shard_map.141 = (bf16[256,512]{1,0:T(8,128)(2,1)S(1)}, bf16[256,512]{1,0:T(8,128)(2,1)S(1)}, f32[256,512]{1,0:T(8,128)S(1)}, f32[4,256,256]{2,1,0:T(8,128)S(1)}...) custom-call(bf16[256,2048]{1,0:T(8,128)(2,1)S(1)} %get-tuple-element.44.refs_0_, s32[1,2048]{1,0:T(1,128)S(1)} %copy-done.4, ...), custom_call_target="tpu_custom_call" | custom-call | flops 1342177280 | bytes 8388608 | tf_op jit(solution)/shard_map/pallas_call | solution.py:47
  18.6 1.6 %collective-permute-start = (bf16[1024,256]{1,0:T(8,128)(2,1)S(1)}, bf16[1024,256]{1,0:T(8,128)(2,1)S(1)}, u32[]{:S(2)}, u32[]{:S(2)}) collective-permute-start(bf16[1024,256]{1,0:T(8,128)(2,1)S(1)} %get-tuple-element.46.refs_10_), channel_id=1, source_target_pairs={{0,32},{32,0},{1,33},{33,1},{2,34},{34,2},{3,35},{35,3},{4,36},{36... | collective-permute-start | bytes 1572872 | tf_op jit(solution)/shard_map/ppermute | solution.py:386
  20.2 3.2 %collective-permute-start.4 = (bf16[256,1024]{1,0:T(8,128)(2,1)S(1)}, bf16[256,1024]{1,0:T(8,128)(2,1)S(1)}, u32[]{:S(2)}, u32[]{:S(2)}) collective-permute-start(bf16[256,1024]{1,0:T(8,128)(2,1)S(1)} %add_convert_fusion.1.refs_9_.refs_0_), channel_id=1, source_target_pairs={{0,2},{2,0},{1,3},{3,1},{4,6},{6,4},{5,7},{7,5},{8,10},{10,8},{9,1... | collective-permute-start | bytes 1572872 | tf_op jit(solution)/shard_map/ppermute | solution.py:386
  23.8 9.0 %collective-permute-done.refs_5_.refs_1_ = bf16[1024,256]{1,0:T(8,128)(2,1)S(1)} collective-permute-done((bf16[1024,256]{1,0:T(8,128)(2,1)S(1)}, bf16[1024,256]{1,0:T(8,128)(2,1)S(1)}, u32[]{:S(2)}, u32[]{:S(2)}) %collective-permute-start) | collective-permute-done | bytes 524320 | tf_op jit(solution)/shard_map/ppermute | solution.py:386
  32.8 2.8 %collective-permute-done.4.refs_1_ = bf16[256,1024]{1,0:T(8,128)(2,1)S(1)} collective-permute-done((bf16[256,1024]{1,0:T(8,128)(2,1)S(1)}, bf16[256,1024]{1,0:T(8,128)(2,1)S(1)}, u32[]{:S(2)}, u32[]{:S(2)}) %collective-permute-start.4) | collective-permute-done | bytes 524320 | tf_op jit(solution)/shard_map/ppermute | solution.py:386
  35.9 3.3 %collective-permute-start.3 = (bf16[256,1024]{1,0:T(8,128)(2,1)S(1)}, bf16[256,1024]{1,0:T(8,128)(2,1)S(1)}, u32[]{:S(2)}, u32[]{:S(2)}) collective-permute-start(bf16[256,1024]{1,0:T(8,128)(2,1)S(1)} %add_convert_fusion.refs_4_.refs_0_), channel_id=1, source_target_pairs={{0,2},{2,0},{1,3},{3,1},{4,6},{6,4},{5,7},{7,5},{8,10},{10,8},{9,1... | collective-permute-start | bytes 1572872 | tf_op jit(solution)/shard_map/ppermute | solution.py:386
  39.2 2.8 %shard_map.144 = (f32[256,512]{1,0:T(8,128)S(1)}, f32[256,512]{1,0:T(8,128)S(1)}) custom-call(bf16[256,1024]{1,0:T(8,128)(2,1)S(1)} %shard_map.143.refs_0_, bf16[256,1024]{1,0:T(8,128)(2,1)S(1)} %collective-permute-done.5.refs_1_, bf16[512,2048]{1,0:T(8,128)(2,1)S(1)} %copy-done, bf16[256,512]{1,0:T(8,128)(2,1)S(1)} %get-tuple-element.47.refs_4_.refs_3_, ...), custom_call_target="tpu_custom_call" | custom-call | flops 872415232 | bytes 6291456 | tf_op jit(solution)/shard_map/pallas_call | solution.py:47
  42.0 9.8 %collective-permute-done.3.refs_1_ = bf16[256,1024]{1,0:T(8,128)(2,1)S(1)} collective-permute-done((bf16[256,1024]{1,0:T(8,128)(2,1)S(1)}, bf16[256,1024]{1,0:T(8,128)(2,1)S(1)}, u32[]{:S(2)}, u32[]{:S(2)}) %collective-permute-start.3) | collective-permute-done | bytes 524320 | tf_op jit(solution)/shard_map/ppermute | solution.py:386
  52.2 1.9 %collective-permute-done.6.refs_1_ = bf16[256,1024]{1,0:T(8,128)(2,1)S(1)} collective-permute-done((bf16[256,1024]{1,0:T(8,128)(2,1)S(1)}, bf16[256,1024]{1,0:T(8,128)(2,1)S(1)}, u32[]{:S(2)}, u32[]{:S(2)}) %collective-permute-start.6) | collective-permute-done | bytes 524320 | tf_op jit(solution)/shard_map/ppermute | solution.py:386
  54.1 2.3 %shard_map.146 = (bf16[256,1024]{1,0:T(8,128)(2,1)S(1)}, f32[16,128]{1,0:T(8,128)S(1)}) custom-call(bf16[256,1024]{1,0:T(8,128)(2,1)S(1)} %shard_map.145.refs_0_, bf16[256,1024]{1,0:T(8,128)(2,1)S(1)} %collective-permute-done.6.refs_1_, bf16[512,2048]{1,0:T(8,128)(2,1)S(1)} %copy-done, bf16[256,512]{1,0:T(8,128)(2,1)S(1)} %get-tuple-element.47.refs_4_.refs_3_, ...), custom_call_target="tpu_custom_call" | custom-call | flops 738197504 | bytes 6291456 | tf_op jit(solution)/shard_map/pallas_call | solution.py:47
  56.9 1.2 %collective-permute-done.8 = f32[16,128]{1,0:T(8,128)S(1)} collective-permute-done((f32[16,128]{1,0:T(8,128)S(1)}, f32[16,128]{1,0:T(8,128)S(1)}, u32[]{:S(2)}, u32[]{:S(2)}) %collective-permute-start.8) | collective-permute-done | bytes 8224 | tf_op jit(solution)/shard_map/ppermute | solution.py:386
  58.0 1.5 %collective-permute-start.10 = (f32[16,128]{1,0:T(8,128)S(1)}, f32[16,128]{1,0:T(8,128)S(1)}, u32[]{:S(2)}, u32[]{:S(2)}) collective-permute-start(f32[16,128]{1,0:T(8,128)S(1)} %add.20), channel_id=1, source_target_pairs={{0,32},{32,0},{1,33},{33,1},{2,34},{34,2},{3,35},{35,3},{4,36},{36... | collective-permute-start | bytes 24584 | tf_op jit(solution)/shard_map/ppermute | solution.py:386
  59.6 3.2 %collective-permute-start.11 = (f32[16,128]{1,0:T(8,128)S(1)}, f32[16,128]{1,0:T(8,128)S(1)}, u32[]{:S(2)}, u32[]{:S(2)}) collective-permute-start(f32[16,128]{1,0:T(8,128)S(1)} %add.20), channel_id=1, source_target_pairs={{0,34},{2,32},{32,2},{34,0},{1,35},{3,33},{33,3},{35,1},{4,38},{6,... | collective-permute-start | bytes 24584 | tf_op jit(solution)/shard_map/ppermute | solution.py:386
  63.0 7.6 %collective-permute-done.10 = f32[16,128]{1,0:T(8,128)S(1)} collective-permute-done((f32[16,128]{1,0:T(8,128)S(1)}, f32[16,128]{1,0:T(8,128)S(1)}, u32[]{:S(2)}, u32[]{:S(2)}) %collective-permute-start.10) | collective-permute-done | bytes 8224 | tf_op jit(solution)/shard_map/ppermute | solution.py:386
  70.6 2.7 %collective-permute-done.11 = f32[16,128]{1,0:T(8,128)S(1)} collective-permute-done((f32[16,128]{1,0:T(8,128)S(1)}, f32[16,128]{1,0:T(8,128)S(1)}, u32[]{:S(2)}, u32[]{:S(2)}) %collective-permute-start.11) | collective-permute-done | bytes 8224 | tf_op jit(solution)/shard_map/ppermute | solution.py:386
  73.3 1.3 %shard_map.147 = (f32[256,512]{1,0:T(8,128)S(1)}, bf16[272,512]{1,0:T(8,128)(2,1)S(1)}, bf16[272,512]{1,0:T(8,128)(2,1)S(1)}, bf16[272,512]{1,0:T(8,128)(2,1)S(1...) custom-call(bf16[1024,256]{1,0:T(8,128)(2,1)S(1)} %get-tuple-element, ...), custom_call_target="tpu_custom_call" | custom-call | flops 1073741824 | bytes 6291456 | tf_op jit(solution)/shard_map/pallas_call | solution.py:47
  75.4 1.9 %collective-permute-start.12 = (bf16[272,512]{1,0:T(8,128)(2,1)S(1)}, bf16[272,512]{1,0:T(8,128)(2,1)S(1)}, u32[]{:S(2)}, u32[]{:S(2)}) collective-permute-start(bf16[272,512]{1,0:T(8,128)(2,1)S(1)} %get-tuple-element.66), channel_id=1, source_target_pairs={{0,8},{8,16},{16,24},{24,0},{1,9},{9,17},{17,25},{25,1},{2,10},{10... | collective-permute-start | bytes 835592 | tf_op jit(solution)/shard_map/ppermute | solution.py:386
  77.3 3.6 %collective-permute-start.13 = (bf16[272,512]{1,0:T(8,128)(2,1)S(1)}, bf16[272,512]{1,0:T(8,128)(2,1)S(1)}, u32[]{:S(2)}, u32[]{:S(2)}) collective-permute-start(bf16[272,512]{1,0:T(8,128)(2,1)S(1)} %get-tuple-element.67), channel_id=1, source_target_pairs={{0,16},{8,24},{16,0},{24,8},{1,17},{9,25},{17,1},{25,9},{2,18},{10... | collective-permute-start | bytes 835592 | tf_op jit(solution)/shard_map/ppermute | solution.py:386
  80.9 1.0 collective-permute-start.14
  81.9 2.7 %collective-permute-start.16 = (bf16[256,512]{1,0:T(8,128)(2,1)S(1)}, bf16[256,512]{1,0:T(8,128)(2,1)S(1)}, u32[]{:S(2)}, u32[]{:S(2)}) collective-permute-start(bf16[256,512]{1,0:T(8,128)(2,1)S(1)} %get-tuple-element.71), channel_id=1, source_target_pairs={{0,64},{64,0},{1,65},{65,1},{2,66},{66,2},{3,67},{67,3},{4,68},{68... | collective-permute-start | bytes 786440 | tf_op jit(solution)/shard_map/ppermute | solution.py:386
  84.6 1.6 %collective-permute-start.17 = (bf16[256,512]{1,0:T(8,128)(2,1)S(1)}, bf16[256,512]{1,0:T(8,128)(2,1)S(1)}, u32[]{:S(2)}, u32[]{:S(2)}) collective-permute-start(bf16[256,512]{1,0:T(8,128)(2,1)S(1)} %get-tuple-element.72), channel_id=1, source_target_pairs={{0,68},{4,64},{64,4},{68,0},{1,69},{5,65},{65,5},{69,1},{2,70},{6,... | collective-permute-start | bytes 786440 | tf_op jit(solution)/shard_map/ppermute | solution.py:386
  86.2 6.2 %collective-permute-done.16.refs_6_ = bf16[256,512]{1,0:T(8,128)(2,1)S(1)} collective-permute-done((bf16[256,512]{1,0:T(8,128)(2,1)S(1)}, bf16[256,512]{1,0:T(8,128)(2,1)S(1)}, u32[]{:S(2)}, u32[]{:S(2)}) %collective-permute-start.16) | collective-permute-done | bytes 262176 | tf_op jit(solution)/shard_map/ppermute | solution.py:386
  92.5 3.4 %collective-permute-done.17.refs_7_ = bf16[256,512]{1,0:T(8,128)(2,1)S(1)} collective-permute-done((bf16[256,512]{1,0:T(8,128)(2,1)S(1)}, bf16[256,512]{1,0:T(8,128)(2,1)S(1)}, u32[]{:S(2)}, u32[]{:S(2)}) %collective-permute-start.17) | collective-permute-done | bytes 262176 | tf_op jit(solution)/shard_map/ppermute | solution.py:386
  96.1 1.1 collective-permute-start.21
  97.2 1.0 collective-permute-start.18
  98.2 2.4 %collective-permute-start.19 = (bf16[80,512]{1,0:T(8,128)(2,1)S(1)}, bf16[80,512]{1,0:T(8,128)(2,1)S(1)}, u32[]{:S(2)}, u32[]{:S(2)}) collective-permute-start(bf16[80,512]{1,0:T(8,128)(2,1)S(1)} %get-tuple-element.75), channel_id=1, source_target_pairs={{0,64},{64,0},{1,65},{65,1},{2,66},{66,2},{3,67},{67,3},{4,68},{68... | collective-permute-start | bytes 245768 | tf_op jit(solution)/shard_map/ppermute | solution.py:386
  100.6 1.6 %collective-permute-start.20 = (bf16[80,512]{1,0:T(8,128)(2,1)S(1)}, bf16[80,512]{1,0:T(8,128)(2,1)S(1)}, u32[]{:S(2)}, u32[]{:S(2)}) collective-permute-start(bf16[80,512]{1,0:T(8,128)(2,1)S(1)} %get-tuple-element.76), channel_id=1, source_target_pairs={{0,68},{4,64},{64,4},{68,0},{1,69},{5,65},{65,5},{69,1},{2,70},{6,... | collective-permute-start | bytes 245768 | tf_op jit(solution)/shard_map/ppermute | solution.py:386
  103.0 2.0 %collective-permute-start.23 = (bf16[64,512]{1,0:T(8,128)(2,1)S(1)}, bf16[64,512]{1,0:T(8,128)(2,1)S(1)}, u32[]{:S(2)}, u32[]{:S(2)}) collective-permute-start(bf16[64,512]{1,0:T(8,128)(2,1)S(1)} %get-tuple-element.80), channel_id=1, source_target_pairs={{0,24},{8,0},{16,8},{24,16},{1,25},{9,1},{17,9},{25,17},{2,26},{10... | collective-permute-start | bytes 196616 | tf_op jit(solution)/shard_map/ppermute | solution.py:386
  105.0 3.0 %collective-permute-done.22.refs_6_ = bf16[64,512]{1,0:T(8,128)(2,1)S(1)} collective-permute-done((bf16[64,512]{1,0:T(8,128)(2,1)S(1)}, bf16[64,512]{1,0:T(8,128)(2,1)S(1)}, u32[]{:S(2)}, u32[]{:S(2)}) %collective-permute-start.22) | collective-permute-done | bytes 65568 | tf_op jit(solution)/shard_map/ppermute | solution.py:386
  (50 shorter events, 8.4 us)
Async XLA Ops:
  0.6 1.0 copy-start.2
  1.6 0.7 copy-start.6
  3.0 7.5 %copy-start.4 = (s32[1,2048]{1,0:T(1,128)S(1)}, s32[1,2048]{1,0:T(1,128)}, u32[]{:S(2)}) copy-start(s32[1,2048]{1,0:T(1,128)} %refs_1_.4) | copy-start | bytes 24580
  10.3 3.4 %copy-start = (bf16[512,2048]{1,0:T(8,128)(2,1)S(1)}, bf16[512,2048]{1,0:T(8,128)(2,1)}, u32[]{:S(2)}) copy-start(bf16[512,2048]{1,0:T(8,128)(2,1)} %refs_2_.5) | copy-start | bytes 6291460
  10.3 3.4 %copy-start.5 = (s32[1,2,512]{2,1,0:T(2,128)S(1)}, s32[1,2,512]{2,1,0:T(2,128)}, u32[]{:S(2)}) copy-start(s32[1,2,512]{2,1,0:T(2,128)} %param.17) | copy-start | bytes 12292
  10.4 2.0 %collective-permute-start.1 = (bf16[256,1024]{1,0:T(8,128)(2,1)S(1)}, bf16[256,1024]{1,0:T(8,128)(2,1)S(1)}, u32[]{:S(2)}, u32[]{:S(2)}) collective-permute-start(bf16[256,1024]{1,0:T(8,128)(2,1)S(1)} %get-tuple-element.52), channel_id=1, source_target_pairs={{0,1},{1,0},{2,3},{3,2},{4,5},{5,4},{6,7},{7,6},{8,9},{9,8},{10,11... | collective-permute-start | bytes 1572872 | tf_op jit(solution)/shard_map/ppermute | solution.py:386
  13.7 9.7 %copy-start.1 = (bf16[256,2048]{1,0:T(8,128)(2,1)S(1)}, bf16[256,2048]{1,0:T(8,128)(2,1)}, u32[]{:S(2)}) copy-start(bf16[256,2048]{1,0:T(8,128)(2,1)} %refs_0_.3) | copy-start | bytes 3145732
  13.8 9.6 %copy-start.3 = (bf16[256,2048]{1,0:T(8,128)(2,1)S(1)}, bf16[256,2048]{1,0:T(8,128)(2,1)}, u32[]{:S(2)}) copy-start(bf16[256,2048]{1,0:T(8,128)(2,1)} %refs_1_.5) | copy-start | bytes 3145732
  13.8 9.6 %copy-start.8 = (f32[256]{0:T(256)S(1)}, f32[256]{0:T(256)}, u32[]{:S(2)}) copy-start(f32[256]{0:T(256)} %param.14) | copy-start | bytes 3076
  18.4 5.2 %collective-permute-start.2 = (bf16[256,1024]{1,0:T(8,128)(2,1)S(1)}, bf16[256,1024]{1,0:T(8,128)(2,1)S(1)}, u32[]{:S(2)}, u32[]{:S(2)}) collective-permute-start(bf16[256,1024]{1,0:T(8,128)(2,1)S(1)} %get-tuple-element.54), channel_id=1, source_target_pairs={{0,1},{1,0},{2,3},{3,2},{4,5},{5,4},{6,7},{7,6},{8,9},{9,8},{10,11... | collective-permute-start | bytes 1572872 | tf_op jit(solution)/shard_map/ppermute | solution.py:386
  18.6 14.2 %collective-permute-start = (bf16[1024,256]{1,0:T(8,128)(2,1)S(1)}, bf16[1024,256]{1,0:T(8,128)(2,1)S(1)}, u32[]{:S(2)}, u32[]{:S(2)}) collective-permute-start(bf16[1024,256]{1,0:T(8,128)(2,1)S(1)} %get-tuple-element.46.refs_10_), channel_id=1, source_target_pairs={{0,32},{32,0},{1,33},{33,1},{2,34},{34,2},{3,35},{35,3},{4,36},{36... | collective-permute-start | bytes 1572872 | tf_op jit(solution)/shard_map/ppermute | solution.py:386
  20.2 15.4 %collective-permute-start.4 = (bf16[256,1024]{1,0:T(8,128)(2,1)S(1)}, bf16[256,1024]{1,0:T(8,128)(2,1)S(1)}, u32[]{:S(2)}, u32[]{:S(2)}) collective-permute-start(bf16[256,1024]{1,0:T(8,128)(2,1)S(1)} %add_convert_fusion.1.refs_9_.refs_0_), channel_id=1, source_target_pairs={{0,2},{2,0},{1,3},{3,1},{4,6},{6,4},{5,7},{7,5},{8,10},{10,8},{9,1... | collective-permute-start | bytes 1572872 | tf_op jit(solution)/shard_map/ppermute | solution.py:386
  35.8 3.4 %collective-permute-start.5 = (bf16[256,1024]{1,0:T(8,128)(2,1)S(1)}, bf16[256,1024]{1,0:T(8,128)(2,1)S(1)}, u32[]{:S(2)}, u32[]{:S(2)}) collective-permute-start(bf16[256,1024]{1,0:T(8,128)(2,1)S(1)} %shard_map.143.refs_0_), channel_id=1, source_target_pairs={{0,1},{1,0},{2,3},{3,2},{4,5},{5,4},{6,7},{7,6},{8,9},{9,8},{10,11... | collective-permute-start | bytes 1572872 | tf_op jit(solution)/shard_map/ppermute | solution.py:386
  35.9 15.8 %collective-permute-start.3 = (bf16[256,1024]{1,0:T(8,128)(2,1)S(1)}, bf16[256,1024]{1,0:T(8,128)(2,1)S(1)}, u32[]{:S(2)}, u32[]{:S(2)}) collective-permute-start(bf16[256,1024]{1,0:T(8,128)(2,1)S(1)} %add_convert_fusion.refs_4_.refs_0_), channel_id=1, source_target_pairs={{0,2},{2,0},{1,3},{3,1},{4,6},{6,4},{5,7},{7,5},{8,10},{10,8},{9,1... | collective-permute-start | bytes 1572872 | tf_op jit(solution)/shard_map/ppermute | solution.py:386
  51.9 2.2 %collective-permute-start.6 = (bf16[256,1024]{1,0:T(8,128)(2,1)S(1)}, bf16[256,1024]{1,0:T(8,128)(2,1)S(1)}, u32[]{:S(2)}, u32[]{:S(2)}) collective-permute-start(bf16[256,1024]{1,0:T(8,128)(2,1)S(1)} %shard_map.145.refs_0_), channel_id=1, source_target_pairs={{0,1},{1,0},{2,3},{3,2},{4,5},{5,4},{6,7},{7,6},{8,9},{9,8},{10,11... | collective-permute-start | bytes 1572872 | tf_op jit(solution)/shard_map/ppermute | solution.py:386
  56.4 17.0 %collective-permute-start.7 = (bf16[256,1024]{1,0:T(8,128)(2,1)S(1)}, bf16[256,1024]{1,0:T(8,128)(2,1)S(1)}, u32[]{:S(2)}, u32[]{:S(2)}) collective-permute-start(bf16[256,1024]{1,0:T(8,128)(2,1)S(1)} %get-tuple-element.63.refs_2_), channel_id=1, source_target_pairs={{0,32},{32,0},{1,33},{33,1},{2,34},{34,2},{3,35},{35,3},{4,36},{36... | collective-permute-start | bytes 1572872 | tf_op jit(solution)/shard_map/ppermute | solution.py:386
  56.9 1.2 %collective-permute-start.8 = (f32[16,128]{1,0:T(8,128)S(1)}, f32[16,128]{1,0:T(8,128)S(1)}, u32[]{:S(2)}, u32[]{:S(2)}) collective-permute-start(f32[16,128]{1,0:T(8,128)S(1)} %get-tuple-element.64), channel_id=1, source_target_pairs={{0,1},{1,0},{2,3},{3,2},{4,5},{5,4},{6,7},{7,6},{8,9},{9,8},{10,11... | collective-permute-start | bytes 24584 | tf_op jit(solution)/shard_map/ppermute | solution.py:386
  58.0 12.6 %collective-permute-start.10 = (f32[16,128]{1,0:T(8,128)S(1)}, f32[16,128]{1,0:T(8,128)S(1)}, u32[]{:S(2)}, u32[]{:S(2)}) collective-permute-start(f32[16,128]{1,0:T(8,128)S(1)} %add.20), channel_id=1, source_target_pairs={{0,32},{32,0},{1,33},{33,1},{2,34},{34,2},{3,35},{35,3},{4,36},{36... | collective-permute-start | bytes 24584 | tf_op jit(solution)/shard_map/ppermute | solution.py:386
  59.6 13.7 %collective-permute-start.11 = (f32[16,128]{1,0:T(8,128)S(1)}, f32[16,128]{1,0:T(8,128)S(1)}, u32[]{:S(2)}, u32[]{:S(2)}) collective-permute-start(f32[16,128]{1,0:T(8,128)S(1)} %add.20), channel_id=1, source_target_pairs={{0,34},{2,32},{32,2},{34,0},{1,35},{3,33},{33,3},{35,1},{4,38},{6,... | collective-permute-start | bytes 24584 | tf_op jit(solution)/shard_map/ppermute | solution.py:386
  62.8 10.6 %collective-permute-start.9 = (f32[16,128]{1,0:T(8,128)S(1)}, f32[16,128]{1,0:T(8,128)S(1)}, u32[]{:S(2)}, u32[]{:S(2)}) collective-permute-start(f32[16,128]{1,0:T(8,128)S(1)} %add.20), channel_id=1, source_target_pairs={{0,2},{2,0},{1,3},{3,1},{4,6},{6,4},{5,7},{7,5},{8,10},{10,8},{9,1... | collective-permute-start | bytes 24584 | tf_op jit(solution)/shard_map/ppermute | solution.py:386
  74.6 10.0 %collective-permute-start.15 = (bf16[256,512]{1,0:T(8,128)(2,1)S(1)}, bf16[256,512]{1,0:T(8,128)(2,1)S(1)}, u32[]{:S(2)}, u32[]{:S(2)}) collective-permute-start(bf16[256,512]{1,0:T(8,128)(2,1)S(1)} %get-tuple-element.70), channel_id=1, source_target_pairs={{0,4},{4,0},{1,5},{5,1},{2,6},{6,2},{3,7},{7,3},{8,12},{12,8},{9,1... | collective-permute-start | bytes 786440 | tf_op jit(solution)/shard_map/ppermute | solution.py:386
  75.4 20.5 %collective-permute-start.12 = (bf16[272,512]{1,0:T(8,128)(2,1)S(1)}, bf16[272,512]{1,0:T(8,128)(2,1)S(1)}, u32[]{:S(2)}, u32[]{:S(2)}) collective-permute-start(bf16[272,512]{1,0:T(8,128)(2,1)S(1)} %get-tuple-element.66), channel_id=1, source_target_pairs={{0,8},{8,16},{16,24},{24,0},{1,9},{9,17},{17,25},{25,1},{2,10},{10... | collective-permute-start | bytes 835592 | tf_op jit(solution)/shard_map/ppermute | solution.py:386
  77.3 18.6 %collective-permute-start.13 = (bf16[272,512]{1,0:T(8,128)(2,1)S(1)}, bf16[272,512]{1,0:T(8,128)(2,1)S(1)}, u32[]{:S(2)}, u32[]{:S(2)}) collective-permute-start(bf16[272,512]{1,0:T(8,128)(2,1)S(1)} %get-tuple-element.67), channel_id=1, source_target_pairs={{0,16},{8,24},{16,0},{24,8},{1,17},{9,25},{17,1},{25,9},{2,18},{10... | collective-permute-start | bytes 835592 | tf_op jit(solution)/shard_map/ppermute | solution.py:386
  80.9 15.0 %collective-permute-start.14 = (bf16[272,512]{1,0:T(8,128)(2,1)S(1)}, bf16[272,512]{1,0:T(8,128)(2,1)S(1)}, u32[]{:S(2)}, u32[]{:S(2)}) collective-permute-start(bf16[272,512]{1,0:T(8,128)(2,1)S(1)} %get-tuple-element.68), channel_id=1, source_target_pairs={{0,24},{8,0},{16,8},{24,16},{1,25},{9,1},{17,9},{25,17},{2,26},{10... | collective-permute-start | bytes 835592 | tf_op jit(solution)/shard_map/ppermute | solution.py:386
  81.9 10.6 %collective-permute-start.16 = (bf16[256,512]{1,0:T(8,128)(2,1)S(1)}, bf16[256,512]{1,0:T(8,128)(2,1)S(1)}, u32[]{:S(2)}, u32[]{:S(2)}) collective-permute-start(bf16[256,512]{1,0:T(8,128)(2,1)S(1)} %get-tuple-element.71), channel_id=1, source_target_pairs={{0,64},{64,0},{1,65},{65,1},{2,66},{66,2},{3,67},{67,3},{4,68},{68... | collective-permute-start | bytes 786440 | tf_op jit(solution)/shard_map/ppermute | solution.py:386
  84.6 11.2 %collective-permute-start.17 = (bf16[256,512]{1,0:T(8,128)(2,1)S(1)}, bf16[256,512]{1,0:T(8,128)(2,1)S(1)}, u32[]{:S(2)}, u32[]{:S(2)}) collective-permute-start(bf16[256,512]{1,0:T(8,128)(2,1)S(1)} %get-tuple-element.72), channel_id=1, source_target_pairs={{0,68},{4,64},{64,4},{68,0},{1,69},{5,65},{65,5},{69,1},{2,70},{6,... | collective-permute-start | bytes 786440 | tf_op jit(solution)/shard_map/ppermute | solution.py:386
  96.1 6.8 %collective-permute-start.21 = (bf16[64,512]{1,0:T(8,128)(2,1)S(1)}, bf16[64,512]{1,0:T(8,128)(2,1)S(1)}, u32[]{:S(2)}, u32[]{:S(2)}) collective-permute-start(bf16[64,512]{1,0:T(8,128)(2,1)S(1)} %get-tuple-element.78), channel_id=1, source_target_pairs={{0,8},{8,16},{16,24},{24,0},{1,9},{9,17},{17,25},{25,1},{2,10},{10... | collective-permute-start | bytes 196616 | tf_op jit(solution)/shard_map/ppermute | solution.py:386
  97.2 11.0 %collective-permute-start.18 = (bf16[80,512]{1,0:T(8,128)(2,1)S(1)}, bf16[80,512]{1,0:T(8,128)(2,1)S(1)}, u32[]{:S(2)}, u32[]{:S(2)}) collective-permute-start(bf16[80,512]{1,0:T(8,128)(2,1)S(1)} %get-tuple-element.74), channel_id=1, source_target_pairs={{0,4},{4,0},{1,5},{5,1},{2,6},{6,2},{3,7},{7,3},{8,12},{12,8},{9,1... | collective-permute-start | bytes 245768 | tf_op jit(solution)/shard_map/ppermute | solution.py:386
  98.2 10.1 %collective-permute-start.19 = (bf16[80,512]{1,0:T(8,128)(2,1)S(1)}, bf16[80,512]{1,0:T(8,128)(2,1)S(1)}, u32[]{:S(2)}, u32[]{:S(2)}) collective-permute-start(bf16[80,512]{1,0:T(8,128)(2,1)S(1)} %get-tuple-element.75), channel_id=1, source_target_pairs={{0,64},{64,0},{1,65},{65,1},{2,66},{66,2},{3,67},{67,3},{4,68},{68... | collective-permute-start | bytes 245768 | tf_op jit(solution)/shard_map/ppermute | solution.py:386
  100.6 7.6 %collective-permute-start.20 = (bf16[80,512]{1,0:T(8,128)(2,1)S(1)}, bf16[80,512]{1,0:T(8,128)(2,1)S(1)}, u32[]{:S(2)}, u32[]{:S(2)}) collective-permute-start(bf16[80,512]{1,0:T(8,128)(2,1)S(1)} %get-tuple-element.76), channel_id=1, source_target_pairs={{0,68},{4,64},{64,4},{68,0},{1,69},{5,65},{65,5},{69,1},{2,70},{6,... | collective-permute-start | bytes 245768 | tf_op jit(solution)/shard_map/ppermute | solution.py:386
  102.2 5.8 %collective-permute-start.22 = (bf16[64,512]{1,0:T(8,128)(2,1)S(1)}, bf16[64,512]{1,0:T(8,128)(2,1)S(1)}, u32[]{:S(2)}, u32[]{:S(2)}) collective-permute-start(bf16[64,512]{1,0:T(8,128)(2,1)S(1)} %get-tuple-element.79), channel_id=1, source_target_pairs={{0,16},{8,24},{16,0},{24,8},{1,17},{9,25},{17,1},{25,9},{2,18},{10... | collective-permute-start | bytes 196616 | tf_op jit(solution)/shard_map/ppermute | solution.py:386
  103.0 5.3 %collective-permute-start.23 = (bf16[64,512]{1,0:T(8,128)(2,1)S(1)}, bf16[64,512]{1,0:T(8,128)(2,1)S(1)}, u32[]{:S(2)}, u32[]{:S(2)}) collective-permute-start(bf16[64,512]{1,0:T(8,128)(2,1)S(1)} %get-tuple-element.80), channel_id=1, source_target_pairs={{0,24},{8,0},{16,8},{24,16},{1,25},{9,1},{17,9},{25,17},{2,26},{10... | collective-permute-start | bytes 196616 | tf_op jit(solution)/shard_map/ppermute | solution.py:386
  (1 other events, 0.7 us)
where the time goes:
time: 110 us
  waiting for transfers between devices  49.4 us (45%)
  starting transfers between devices  34.6 us (31%)
  Pallas kernels  20.4 us (19%)
  local copies, waits for them, and re-layouts  2.87 us (3%)
  other arithmetic  1.53 us (1%)
    ppermute x24, waiting for transfers between devices, flip(): lax.ppermute(value, axes if len(axes) > 1 else axes[0], [(i, target(i)) f...  49.4 us
    ppermute x24, starting transfers between devices, flip(): lax.ppermute(value, axes if len(axes) > 1 else axes[0], [(i, target(i)) f...  34.6 us
    pallas_call x11, Pallas kernels, run(): return kernel(*args, *after)  20.4 us
    unnamed x18, local copies, waits for them, and re-layouts  2.36 us
  transfers between devices with their start and end apart: 24, of which 12 were waited for; matrix products, arithmetic and copies ran while one was open for 0% of the time, Pallas kernels for 3%

commit v1 on v0

--- a/solution.py
+++ b/solution.py
@@ -15,7 +15,7 @@
 EPSILON = 1e-06
 SCALE = HEAD_DIM**-0.5
 MIB = 1 << 20
-DP = ("xh", "xl", "z", "yl")
+DP = ("x", "z", "yl")
 MP = ("yh", "c")
 bf16, f32, i32 = jnp.bfloat16, jnp.float32, jnp.int32
 VMEM = pl.BlockSpec(memory_space=pltpu.VMEM)
@@ -47,6 +47,10 @@
         return kernel(*args, *after)
 
     return run
+
+
+def in_hbm(value):
+    return pltpu.with_memory_space_constraint(value, pltpu.HBM)
 
 
 def dot(a, b):
@@ -89,6 +93,18 @@
     return high, middle, low
 
 
+def pieces_of(value):
+    return jnp.concatenate(list(split3(value)) + [jnp.zeros(value.shape, bf16)], axis=1)
+
+
+def read_sums(part):
+    return sum(part[:, i * HEAD_DIM : (i + 1) * HEAD_DIM].astype(f32) for i in range(3))
+
+
+def in_pairs(own, first, second, third):
+    return (own + second) + (first + third)
+
+
 def forward_body(
     tok_hbm, gain_hbm, wq_hbm, wk_hbm, table_hbm, seg_hbm, wv_hbm, wo_hbm,
     normed_out, q_out, k_out, v_out, p_out, send_out, own_out,
@@ -97,13 +113,15 @@
     sources = (tok_hbm, gain_hbm, wq_hbm, wk_hbm, table_hbm, seg_hbm, wv_hbm, wo_hbm)
     places = (tok, gain, wq, wk, table, seg, wv, wo)
     copies = [pltpu.make_async_copy(s, d, sems.at[i]) for i, (s, d) in enumerate(zip(sources, places))]
-    for copy in copies:
+    for copy in copies[:3]:
         copy.start()
     length = tok.shape[0]
     heads = q_out.shape[1] // HEAD_DIM
     half = send_out.shape[1]
     core = lax.axis_index("c")
     copies[0].wait()
+    for copy in copies[3:]:
+        copy.start()
     copies[1].wait()
     tokens = tok[...].astype(f32)
     inverse = lax.rsqrt(jnp.mean(tokens * tokens, axis=1, keepdims=True) + EPSILON)
@@ -267,7 +285,7 @@
 
 def third_body(
     res_own, res_mate, wo, q_ref, k_ref, v_ref, p_ref, hq_ref, hk_ref, r_ref, head_bits, table,
-    y_out, sum_out,
+    yq_out, yk_out, sum_out,
 ):
     feat = q_ref.shape[1]
     back = back_of(res_own, res_mate, wo)
@@ -282,89 +300,86 @@
         hq = (hq_ref[:, s] + dot(first, k_ref[:, s])) * SCALE
         hk = (hk_ref[:, s] + dot_tn(first, q_ref[:, s])) * SCALE
         product = r_ref[:, s]
-        for i, gradient in enumerate((hq, hk)):
+        for i, (gradient, y_out) in enumerate(((hq, yq_out), (hk, yk_out))):
             y = rotate(gradient, cosine, -sine) * signs[i : i + 1, s]
             y = y.astype(bf16)
-            y_out[:, i * feat + h * HEAD_DIM : i * feat + (h + 1) * HEAD_DIM] = y
+            y_out[: y.shape[0], s] = y
             totals[i] = totals[i] + jnp.sum(product * y.astype(f32), axis=0, keepdims=True)
     pair = [jnp.sum(t, axis=1, keepdims=True) for t in totals]
     lane = lax.broadcasted_iota(i32, sum_out.shape, 1)
-    sum_out[...] = jnp.where(lane == 0, pair[0], jnp.where(lane == 1, pair[1], 0.0))
-
-
-def transpose_body(normed, model_bits, own_out, send_out, whole):
+    total = jnp.where(lane == 0, pair[0], jnp.where(lane == 1, pair[1], 0.0))
+    sum_out[...] = total
+    yq_out[yk_out.shape[0] :, :] = pieces_of(total)
+
+
+def transpose_body(normed, model_bits, *refs):
+    outs, whole = refs[:8], refs[8]
     sign = (2 * model_bits[...] - 1).astype(f32).astype(bf16)
     signed = normed[...] * sign
     for i in range(whole.shape[0] // HEAD_DIM):
         whole[i * HEAD_DIM : (i + 1) * HEAD_DIM, :] = signed[:, i * HEAD_DIM : (i + 1) * HEAD_DIM].T
     rows = whole.shape[0] // 32
-    xh, xl, z, yl = (lax.axis_index(axis) for axis in DP)
-    for out, low in ((own_out, xl), (send_out, 1 - xl)):
-        for ez in range(4):
-            for ex in range(2):
+    x, z, yl = (lax.axis_index(axis) for axis in DP)
+    for which in range(2):
+        for far in range(4):
+            for step in range(4):
+                to_x = lax.rem(x + (step if which == 0 else far), 4)
+                to_z = lax.rem(z + (far if which == 0 else step), 4)
                 for ey in range(2):
-                    to_x = 2 * (xh if ex == 0 else 1 - xh) + low
-                    to_z = lax.rem(z + ez, 4)
                     to_y = yl if ey == 0 else 1 - yl
                     start = pl.multiple_of(((to_x * 4 + to_z) * 2 + to_y) * rows, rows)
-                    at = ((ez * 2 + ex) * 2 + ey) * rows
-                    out[at : at + rows, :] = whole[pl.ds(start, rows), :]
-
-
-def estimate_body(x_own, x_mate, y_own, y_mate, sums, a0, a1, a2, a3, b0, b1, b2, b3):
-    group = b0.shape[0]
-    rows = group // 4
-    feat = b0.shape[1]
-    pieces = jnp.concatenate(
-        [part for part in split3(sums[...])] + [jnp.zeros((sums.shape[0], HEAD_DIM), bf16)], axis=1
-    )
-    for ez, out in enumerate((a0, a1, a2, a3)):
-        at = slice(ez * group, (ez + 1) * group)
-        part = dot(x_own[at, :], y_own[...]) + dot(x_mate[at, :], y_mate[...])
-        if ez == 0:
-            out[...] = part[:, :feat]
-        else:
-            out[:group, :] = part[:, :feat].astype(bf16)
-            out[group:, :] = pieces
-        for e, to in enumerate((b0, b1, b2, b3)):
-            to[ez * rows : (ez + 1) * rows, :] = part[e * rows : (e + 1) * rows, feat:].astype(to.dtype)
-
-
-def read_sums(part):
-    return sum(part[:, i * HEAD_DIM : (i + 1) * HEAD_DIM].astype(f32) for i in range(3))
-
-
-def middle_body(a0, a1, a2, a3, b0, b1, b2, b3, sums, *outs):
-    group = b0.shape[0]
-    rows = group // 4
+                    at = (step * 2 + ey) * rows
+                    outs[which * 4 + far][at : at + rows, :] = whole[pl.ds(start, rows), :]
+
+
+def rows_times(x_parts, y_parts):
+    length = x_parts[0].shape[1]
+    return sum(dot(a[...], b[:length, :]) for a, b in zip(x_parts, y_parts))
+
+
+def estimate_q_body(*refs):
+    y_parts, sums, outs, sum_out = refs[4:8], refs[8], refs[9:13], refs[13]
+    length = refs[0].shape[1]
+    group = outs[0].shape[0]
+    total = in_pairs(sums[...], *(read_sums(y[length:, :]) for y in y_parts[1:]))
+    sum_out[...] = total
+    whole = rows_times(refs[:4], y_parts)
+    for step, out in enumerate(outs):
+        out[:group, :] = whole[step * group : (step + 1) * group, :].astype(out.dtype)
+        if step > 0:
+            out[group:, :] = pieces_of(total)
+
+
+def estimate_k_body(*refs):
+    outs = refs[8:]
+    group = outs[0].shape[0]
+    whole = rows_times(refs[:4], refs[4:8])
+    for step, out in enumerate(outs):
+        out[...] = whole[step * group : (step + 1) * group, :].astype(out.dtype)
+
+
+def middle_body(a0, a1, a2, a3, b0, b1, b2, b3, sums, keep, send, sum_out):
+    group, feat = b0.shape
+    rows = group // 2
     a = a0[...] + sum(r[:group, :].astype(f32) for r in (a1, a2, a3))
     b = b0[...] + sum(r[...].astype(f32) for r in (b1, b2, b3))
-    total = sums[...] + sum(read_sums(r[group:, :]) for r in (a1, a2, a3))
-    pieces = jnp.concatenate(list(split3(total)) + [jnp.zeros(total.shape, bf16)], axis=1)
-    a_outs, b_outs, sum_out = outs[:4], outs[4:8], outs[8]
-    for e, out in enumerate(a_outs):
-        part = a[e * rows : (e + 1) * rows, :]
-        if e == 0:
-            out[...] = part
-        else:
-            out[:rows, :] = part.astype(bf16)
-            out[rows:, :] = pieces
-    for e, out in enumerate(b_outs):
-        out[...] = b[e * rows : (e + 1) * rows, :].astype(out.dtype)
-    sum_out[...] = total
-
-
-def final_body(a0, a1, a2, a3, b0, b1, b2, b3, sums, diag_query, diag_key, mean_out, *, groups, entries):
-    rows, feat = b0.shape
-    xh, xl, z, yl = (lax.axis_index(axis) for axis in DP)
-    row0 = (((xh * 2 + xl) * 4 + z) * 2 + yl) * rows
+    keep[:, :feat] = a[:rows, :]
+    keep[:, feat:] = b[:rows, :]
+    send[:, :feat] = a[rows:, :].astype(bf16)
+    send[:, feat:] = b[rows:, :].astype(bf16)
+    sum_out[...] = in_pairs(sums[...], *(read_sums(r[group:, :]) for r in (a1, a2, a3)))
+
+
+def final_body(keep, came, s0, s1, s2, s3, diag_query, diag_key, mean_out, *, groups, entries):
+    rows, feat = diag_query.shape
+    x, z, yl = (lax.axis_index(axis) for axis in DP)
+    row0 = ((x * 4 + z) * 2 + yl) * rows
     col0 = (lax.axis_index("yh") * 2 + lax.axis_index("c")) * feat
     _, square = square_state(row0, col0, (rows, feat))
     sign = sign_of(square.astype(f32)) * (1.0 / groups)
-    diag_query[...] = sign * (a0[...] + sum(r[:rows, :].astype(f32) for r in (a1, a2, a3)))
-    diag_key[...] = sign * (b0[...] + sum(r[...].astype(f32) for r in (b1, b2, b3)))
-    total = sums[...] + sum(read_sums(r[rows:, :]) for r in (a1, a2, a3))
-    mean_out[...] = total * (1.0 / (groups * entries))
+    diag_query[...] = sign * (keep[:, :feat] + came[:, :feat].astype(f32))
+    diag_key[...] = sign * (keep[:, feat:] + came[:, feat:].astype(f32))
+    mean_out[...] = in_pairs(s0[...], s1[...], s2[...], s3[...]) * (1.0 / (groups * entries))
 
 
 def flip(value, moves):
@@ -419,20 +434,19 @@
             pltpu.VMEM((2 * length, HEAD_DIM), f32), pltpu.VMEM((1, length), i32),
             weight, pltpu.VMEM((feat, width), bf16), pltpu.SemaphoreType.DMA((8,)),
         ],
-        4 * product + 4 * small, 12 * MIB, 50,
-    )(tokens, norm_gain[None, :], w_query, w_key, table, segments, w_value, w_out)
+        4 * product + 4 * small, 12 * MIB, 32,
+    )(*map(in_hbm, (tokens, norm_gain[None, :], w_query, w_key, table, segments, w_value, w_out)))
     mate = [xor("c", 1)]
     far = [xor("yh", 1)]
-    pair = [xor("xl", 1)]
     came = flip(send, mate)
-    x_own, x_send = call(
+    along_z, along_x = [[add("z", i)] for i in (1, 2, 3)], [[add("x", i)] for i in (1, 2, 3)]
+    sends = call(
         transpose_body,
-        (shape((width // 2, length), bf16),) * 2,
+        (shape((width // 4, length), bf16),) * 8,
         [VMEM] * 2,
         [pltpu.VMEM((width, length), bf16)],
         0, 3 * MIB, 16,
     )(normed, probe_model)
-    x_mate = flip(x_send, pair)
     near = (own + came.astype(f32)).astype(bf16)
     there = flip(near, far)
 
@@ -441,10 +455,12 @@
         (mat, mat, shape((length, feat), f32), square, half16, half32),
         [VMEM] * 9,
         [pltpu.VMEM((width, feat), bf16)],
-        2 * product + 4 * small, 8 * MIB, 32, (near, x_send),
+        2 * product + 4 * small, 8 * MIB, 32, (near, sends[0]),
     )(normed, probe_model, head_bits, table, q, k, v, p, w_out)
     d_near = (d_own + flip(d_send, mate).astype(f32)).astype(bf16)
     d_there = flip(d_near, far)
+    xq = [sends[0]] + [flip(m, where) for m, where in zip(sends[1:4], along_z)]
+    xk = [sends[4]] + [flip(m, where) for m, where in zip(sends[5:8], along_x)]
 
     base, row_weight = call(
         base_body,
@@ -453,7 +469,7 @@
         (), 0, 3 * MIB, 16, (d_own,),
     )(tokens, targets, loss_weights[None, :])
 
-    res_own = call(residual_body, half16, [VMEM] * 4, (), 0, 3 * MIB, 16, (d_near, x_mate))(near, there, base, row_weight)
+    res_own = call(residual_body, half16, [VMEM] * 4, (), 0, 3 * MIB, 16, (d_near,))(near, there, base, row_weight)
     res_mate = flip(res_own, mate)
     hq, hk = call(
         second_body,
@@ -464,52 +480,56 @@
 
     d_res_own = call(d_residual_body, half16, [VMEM] * 3, (), 0, 2 * MIB, 16, (hq,))(d_near, d_there, row_weight)
     d_res_mate = flip(d_res_own, mate)
-    y, sums = call(
+    yq, yk, sums = call(
         third_body,
-        (shape((length, 2 * feat), bf16), shape((16, HEAD_DIM), f32)),
+        (shape((length + 16, feat), bf16), mat, shape((16, HEAD_DIM), f32)),
         [VMEM] * 12,
         (), product + 3 * small, 6 * MIB, 24,
     )(d_res_own, d_res_mate, w_out, q, k, v, p, hq, hk, r, head_bits, table)
-
-    y_mate = flip(y, pair)
-    sums = sums + flip(sums, mate)
-    sums = sums + flip(sums, far) + flip(sums, pair) + flip(sums, pair + far)
+    yq_in = [yq] + [flip(yq, where) for where in along_z]
+    yk_in = [yk] + [flip(yk, where) for where in along_x]
 
     rows = width // 32
-    group = 4 * rows
+    group = 2 * rows
     a_out, b_out = shape((group + 16, feat), bf16), shape((group, feat), bf16)
     keep = shape((group, feat), f32)
-    parts = call(
-        estimate_body,
-        (keep, a_out, a_out, a_out, keep, b_out, b_out, b_out),
-        [VMEM] * 5,
-        (), 2 * product, 6 * MIB, 24,
-    )(x_own, x_mate, y, y_mate, sums)
-    along = [[add("z", 1)], [add("z", 2)], [add("z", 3)]]
-    across = [[xor("yl", 1)], [xor("xh", 1)], [xor("xh", 1), xor("yl", 1)]]
-    a_in = [flip(m, where) for m, where in zip(parts[1:4], along)]
-    b_in = [flip(m, where) for m, where in zip(parts[5:8], across)]
-    a_out, b_out = shape((rows + 16, feat), bf16), shape((rows, feat), bf16)
-    keep = shape((rows, feat), f32)
-    parts = call(
+    *parts, sums = call(
+        estimate_q_body,
+        (keep, a_out, a_out, a_out, shape((16, HEAD_DIM), f32)),
+        [VMEM] * 9,
+        (), product, 3 * MIB, 24,
+    )(*xq, *yq_in, sums)
+    parts += call(
+        estimate_k_body,
+        (keep, b_out, b_out, b_out),
+        [VMEM] * 8,
+        (), product, 3 * MIB, 24,
+    )(*xk, *yk_in)
+    a_in, b_in = [], []
+    for i in range(3):
+        a_in.append(flip(parts[1 + i], along_x[i]))
+        b_in.append(flip(parts[5 + i], along_z[i]))
+    keep, send, sums = call(
         middle_body,
-        (keep, a_out, a_out, a_out, keep, b_out, b_out, b_out, shape((16, HEAD_DIM), f32)),
+        (shape((rows, 2 * feat), f32), shape((rows, 2 * feat), bf16), shape((16, HEAD_DIM), f32)),
         [VMEM] * 9,
         (), 0, 3 * MIB, 24,
     )(parts[0], *a_in, parts[4], *b_in, sums)
-    a_in = [flip(m, where) for m, where in zip(parts[1:4], across)]
-    b_in = [flip(m, where) for m, where in zip(parts[5:8], along)]
+    side = [xor("yl", 1)]
+    came = flip(send, side)
+    sums = sums + flip(sums, mate)
+    sums = [sums] + [flip(sums, where) for where in (far, side, side + far)]
     diag_query, diag_key, mean = call(
         functools.partial(final_body, groups=groups, entries=entries),
-        (keep, keep, shape((16, HEAD_DIM), f32)),
-        [VMEM] * 9,
+        (shape((rows, feat), f32), shape((rows, feat), f32), shape((16, HEAD_DIM), f32)),
+        [VMEM] * 6,
         (), 0, MIB, 16,
-    )(parts[0], *a_in, parts[4], *b_in, parts[8])
+    )(keep, came, *sums)
     return diag_query, diag_key, mean[0, :2]
 
 
 def solution(mesh):
-    torus = Mesh(mesh.devices.reshape(2, 2, 4, 2, 2, 2), ("xh", "xl", "z", "yl", "yh", "c"))
+    torus = Mesh(mesh.devices.reshape(4, 4, 2, 2, 2), ("x", "z", "yl", "yh", "c"))
     return jax.shard_map(
         local,
         mesh=torus,

time: 110 us -> 119 us (1.082)
  starting transfers between devices: 34.6 us -> 43.2 us
  waiting for transfers between devices: 49.4 us -> 53.7 us
  local copies, waits for them, and re-layouts: 2.87 us -> 0.55 us
  other arithmetic: 1.53 us -> 0.3 us
    ppermute x24 -> x29, starting transfers between devices: 34.6 us -> 43.2 us  [flip(): lax.ppermute(value, axes if len(axes) > 1 else axes[0], [(i, target(i)) f...]
    ppermute x24 -> x29, waiting for transfers between devices: 49.4 us -> 53.7 us  [flip(): lax.ppermute(value, axes if len(axes) > 1 else axes[0], [(i, target(i)) f...]
    unnamed x18 -> x14, local copies, waits for them, and re-layouts: 2.36 us -> 0.04 us
    convert_element_type x1, other arithmetic: 1.37 us -> 0.15 us  [local(): near = (own + came.astype(f32)).astype(bf16)]
    pallas_call x11 -> x12, Pallas kernels: 20.4 us -> 19.9 us  [run(): return kernel(*args, *after)]
  transfers between devices with their start and end apart: 24 -> 29, of which waited for: 12 -> 13; matrix products, arithmetic and copies ran while one was open for 0% -> 0% of each run, Pallas kernels for 3% -> 6%
where the time goes in v1:
time: 119 us
  waiting for transfers between devices  53.7 us (45%)
  starting transfers between devices  43.2 us (36%)
  Pallas kernels  19.9 us (17%)
    ppermute x29, waiting for transfers between devices, flip(): lax.ppermute(value, axes if len(axes) > 1 else axes[0], [(i, target(i)) f...  53.7 us
    ppermute x29, starting transfers between devices, flip(): lax.ppermute(value, axes if len(axes) > 1 else axes[0], [(i, target(i)) f...  43.2 us
    pallas_call x12, Pallas kernels, run(): return kernel(*args, *after)  19.9 us
  transfers between devices with their start and end apart: 29, of which 13 were waited for; matrix products, arithmetic and copies ran while one was open for 0% of the time, Pallas kernels for 6%

profile of v1, /device:TPU:0, one launch (start us, length us, event | category | flops | bytes accessed | tf_op | source)
XLA Modules:
  0.0 118.5 jit_solution(13222225288239605405)
XLA Ops:
  0.6 6.7 %shard_map.139 = (bf16[256,2048]{1,0:T(8,128)(2,1)S(1)}, bf16[256,512]{1,0:T(8,128)(2,1)S(1)}, bf16[256,512]{1,0:T(8,128)(2,1)S(1)}, bf16[256,512]{1,0:T(8,128)(...) custom-call(bf16[256,2048]{1,0:T(8,128)(2,1)} %refs_0_.3, ...), custom_call_target="tpu_custom_call" | custom-call | flops 2415919104 | bytes 12582912 | tf_op jit(solution)/shard_map/pallas_call | solution.py:47
  8.0 1.4 %collective-permute-done.3 = bf16[256,1024]{1,0:T(8,128)(2,1)S(1)} collective-permute-done((bf16[256,1024]{1,0:T(8,128)(2,1)S(1)}, bf16[256,1024]{1,0:T(8,128)(2,1)S(1)}, u32[]{:S(2)}, u32[]{:S(2)}) %collective-permute-start.3) | collective-permute-done | bytes 524320 | tf_op jit(solution)/shard_map/ppermute | solution.py:401
  9.6 4.6 %shard_map.141 = (bf16[256,512]{1,0:T(8,128)(2,1)S(1)}, bf16[256,512]{1,0:T(8,128)(2,1)S(1)}, f32[256,512]{1,0:T(8,128)S(1)}, f32[4,256,256]{2,1,0:T(8,128)S(1)}...) custom-call(bf16[256,2048]{1,0:T(8,128)(2,1)S(1)} %get-tuple-element.46.refs_0_, s32[1,2048]{1,0:T(1,128)S(1)} %copy-done.4, ...), custom_call_target="tpu_custom_call" | custom-call | flops 1342177280 | bytes 8388608 | tf_op jit(solution)/shard_map/pallas_call | solution.py:47
  14.4 3.3 %collective-permute-start.6 = (bf16[256,1024]{1,0:T(8,128)(2,1)S(1)}, bf16[256,1024]{1,0:T(8,128)(2,1)S(1)}, u32[]{:S(2)}, u32[]{:S(2)}) collective-permute-start(bf16[256,1024]{1,0:T(8,128)(2,1)S(1)} %add_convert_fusion.1.refs_9_.refs_0_), channel_id=1, source_target_pairs={{0,2},{2,0},{1,3},{3,1},{4,6},{6,4},{5,7},{7,5},{8,10},{10,8},{9,1... | collective-permute-start | bytes 1572872 | tf_op jit(solution)/shard_map/ppermute | solution.py:401
  18.1 12.1 %collective-permute-done.6.refs_1_ = bf16[256,1024]{1,0:T(8,128)(2,1)S(1)} collective-permute-done((bf16[256,1024]{1,0:T(8,128)(2,1)S(1)}, bf16[256,1024]{1,0:T(8,128)(2,1)S(1)}, u32[]{:S(2)}, u32[]{:S(2)}) %collective-permute-start.6) | collective-permute-done | bytes 524320 | tf_op jit(solution)/shard_map/ppermute | solution.py:401
  30.5 3.3 %collective-permute-start.5 = (bf16[256,1024]{1,0:T(8,128)(2,1)S(1)}, bf16[256,1024]{1,0:T(8,128)(2,1)S(1)}, u32[]{:S(2)}, u32[]{:S(2)}) collective-permute-start(bf16[256,1024]{1,0:T(8,128)(2,1)S(1)} %add_convert_fusion.refs_4_.refs_0_), channel_id=1, source_target_pairs={{0,2},{2,0},{1,3},{3,1},{4,6},{6,4},{5,7},{7,5},{8,10},{10,8},{9,1... | collective-permute-start | bytes 1572872 | tf_op jit(solution)/shard_map/ppermute | solution.py:401
  33.8 2.8 %shard_map.144 = (f32[256,512]{1,0:T(8,128)S(1)}, f32[256,512]{1,0:T(8,128)S(1)}) custom-call(bf16[256,1024]{1,0:T(8,128)(2,1)S(1)} %shard_map.143.refs_0_, bf16[256,1024]{1,0:T(8,128)(2,1)S(1)} %collective-permute-done.7.refs_1_, bf16[512,2048]{1,0:T(8,128)(2,1)S(1)} %copy-done, bf16[256,512]{1,0:T(8,128)(2,1)S(1)} %get-tuple-element.51.refs_4_.refs_3_, ...), custom_call_target="tpu_custom_call" | custom-call | flops 872415232 | bytes 6291456 | tf_op jit(solution)/shard_map/pallas_call | solution.py:47
  36.6 9.7 %collective-permute-done.5.refs_1_ = bf16[256,1024]{1,0:T(8,128)(2,1)S(1)} collective-permute-done((bf16[256,1024]{1,0:T(8,128)(2,1)S(1)}, bf16[256,1024]{1,0:T(8,128)(2,1)S(1)}, u32[]{:S(2)}, u32[]{:S(2)}) %collective-permute-start.5) | collective-permute-done | bytes 524320 | tf_op jit(solution)/shard_map/ppermute | solution.py:401
  46.6 1.6 %collective-permute-start.15 = (bf16[512,256]{1,0:T(8,128)(2,1)S(1)}, bf16[512,256]{1,0:T(8,128)(2,1)S(1)}, u32[]{:S(2)}, u32[]{:S(2)}) collective-permute-start(bf16[512,256]{1,0:T(8,128)(2,1)S(1)} %get-tuple-element.74), channel_id=1, source_target_pairs={{0,32},{32,64},{64,96},{96,0},{1,33},{33,65},{65,97},{97,1},{2,34}... | collective-permute-start | bytes 786440 | tf_op jit(solution)/shard_map/ppermute | solution.py:401
  48.2 2.7 %collective-permute-start.16 = (bf16[512,256]{1,0:T(8,128)(2,1)S(1)}, bf16[512,256]{1,0:T(8,128)(2,1)S(1)}, u32[]{:S(2)}, u32[]{:S(2)}) collective-permute-start(bf16[512,256]{1,0:T(8,128)(2,1)S(1)} %get-tuple-element.75), channel_id=1, source_target_pairs={{0,64},{32,96},{64,0},{96,32},{1,65},{33,97},{65,1},{97,33},{2,66}... | collective-permute-start | bytes 786440 | tf_op jit(solution)/shard_map/ppermute | solution.py:401
  50.9 1.4 %collective-permute-start.17 = (bf16[512,256]{1,0:T(8,128)(2,1)S(1)}, bf16[512,256]{1,0:T(8,128)(2,1)S(1)}, u32[]{:S(2)}, u32[]{:S(2)}) collective-permute-start(bf16[512,256]{1,0:T(8,128)(2,1)S(1)} %get-tuple-element.76), channel_id=1, source_target_pairs={{0,96},{32,0},{64,32},{96,64},{1,97},{33,1},{65,33},{97,65},{2,98}... | collective-permute-start | bytes 786440 | tf_op jit(solution)/shard_map/ppermute | solution.py:401
  52.4 1.9 %collective-permute-start = (bf16[512,256]{1,0:T(8,128)(2,1)S(1)}, bf16[512,256]{1,0:T(8,128)(2,1)S(1)}, u32[]{:S(2)}, u32[]{:S(2)}) collective-permute-start(bf16[512,256]{1,0:T(8,128)(2,1)S(1)} %get-tuple-element.48), channel_id=1, source_target_pairs={{0,8},{8,16},{16,24},{24,0},{1,9},{9,17},{17,25},{25,1},{2,10},{10... | collective-permute-start | bytes 786440 | tf_op jit(solution)/shard_map/ppermute | solution.py:401
  54.3 2.3 %shard_map.146 = (bf16[272,512]{1,0:T(8,128)(2,1)S(1)}, bf16[256,512]{1,0:T(8,128)(2,1)S(1)}, f32[16,128]{1,0:T(8,128)S(1)}) custom-call(bf16[256,1024]{1,0:T(8,128)(2,1)S(1)} %shard_map.145.refs_0_, bf16[256,1024]{1,0:T(8,128)(2,1)S(1)} %collective-permute-done.8.refs_1_, bf16[512,2048]{1,0:T(8,128)(2,1)S(1)} %copy-done, ...), custom_call_target="tpu_custom_call" | custom-call | flops 738197504 | bytes 6291456 | tf_op jit(solution)/shard_map/pallas_call | solution.py:47
  57.2 1.8 %collective-permute-start.19 = (bf16[256,512]{1,0:T(8,128)(2,1)S(1)}, bf16[256,512]{1,0:T(8,128)(2,1)S(1)}, u32[]{:S(2)}, u32[]{:S(2)}) collective-permute-start(bf16[256,512]{1,0:T(8,128)(2,1)S(1)} %get-tuple-element.77.refs_4_), channel_id=1, source_target_pairs={{0,64},{32,96},{64,0},{96,32},{1,65},{33,97},{65,1},{97,33},{2,66}... | collective-permute-start | bytes 786440 | tf_op jit(solution)/shard_map/ppermute | solution.py:401
  58.9 4.8 %collective-permute-done.16.refs_2_ = bf16[512,256]{1,0:T(8,128)(2,1)S(1)} collective-permute-done((bf16[512,256]{1,0:T(8,128)(2,1)S(1)}, bf16[512,256]{1,0:T(8,128)(2,1)S(1)}, u32[]{:S(2)}, u32[]{:S(2)}) %collective-permute-start.16) | collective-permute-done | bytes 262176 | tf_op jit(solution)/shard_map/ppermute | solution.py:401
  63.8 3.9 %collective-permute-start.1 = (bf16[512,256]{1,0:T(8,128)(2,1)S(1)}, bf16[512,256]{1,0:T(8,128)(2,1)S(1)}, u32[]{:S(2)}, u32[]{:S(2)}) collective-permute-start(bf16[512,256]{1,0:T(8,128)(2,1)S(1)} %get-tuple-element.49), channel_id=1, source_target_pairs={{0,16},{8,24},{16,0},{24,8},{1,17},{9,25},{17,1},{25,9},{2,18},{10... | collective-permute-start | bytes 786440 | tf_op jit(solution)/shard_map/ppermute | solution.py:401
  67.7 1.5 %collective-permute-done.18.refs_5_ = bf16[256,512]{1,0:T(8,128)(2,1)S(1)} collective-permute-done((bf16[256,512]{1,0:T(8,128)(2,1)S(1)}, bf16[256,512]{1,0:T(8,128)(2,1)S(1)}, u32[]{:S(2)}, u32[]{:S(2)}) %collective-permute-start.18) | collective-permute-done | bytes 262176 | tf_op jit(solution)/shard_map/ppermute | solution.py:401
  69.3 4.0 %collective-permute-start.11 = (bf16[272,512]{1,0:T(8,128)(2,1)S(1)}, bf16[272,512]{1,0:T(8,128)(2,1)S(1)}, u32[]{:S(2)}, u32[]{:S(2)}) collective-permute-start(bf16[272,512]{1,0:T(8,128)(2,1)S(1)} %get-tuple-element.67.refs_4_), channel_id=1, source_target_pairs={{0,24},{8,0},{16,8},{24,16},{1,25},{9,1},{17,9},{25,17},{2,26},{10... | collective-permute-start | bytes 835592 | tf_op jit(solution)/shard_map/ppermute | solution.py:401
  73.3 1.2 collective-permute-done.19.refs_6_
  74.4 1.9 %collective-permute-start.9 = (bf16[272,512]{1,0:T(8,128)(2,1)S(1)}, bf16[272,512]{1,0:T(8,128)(2,1)S(1)}, u32[]{:S(2)}, u32[]{:S(2)}) collective-permute-start(bf16[272,512]{1,0:T(8,128)(2,1)S(1)} %get-tuple-element.67.refs_4_), channel_id=1, source_target_pairs={{0,8},{8,16},{16,24},{24,0},{1,9},{9,17},{17,25},{25,1},{2,10},{10... | collective-permute-start | bytes 835592 | tf_op jit(solution)/shard_map/ppermute | solution.py:401
  76.4 2.1 %collective-permute-start.2 = (bf16[512,256]{1,0:T(8,128)(2,1)S(1)}, bf16[512,256]{1,0:T(8,128)(2,1)S(1)}, u32[]{:S(2)}, u32[]{:S(2)}) collective-permute-start(bf16[512,256]{1,0:T(8,128)(2,1)S(1)} %get-tuple-element.50), channel_id=1, source_target_pairs={{0,24},{8,0},{16,8},{24,16},{1,25},{9,1},{17,9},{25,17},{2,26},{10... | collective-permute-start | bytes 786440 | tf_op jit(solution)/shard_map/ppermute | solution.py:401
  79.3 12.2 %collective-permute-done.2.refs_3_ = bf16[512,256]{1,0:T(8,128)(2,1)S(1)} collective-permute-done((bf16[512,256]{1,0:T(8,128)(2,1)S(1)}, bf16[512,256]{1,0:T(8,128)(2,1)S(1)}, u32[]{:S(2)}, u32[]{:S(2)}) %collective-permute-start.2) | collective-permute-done | bytes 262176 | tf_op jit(solution)/shard_map/ppermute | solution.py:401
  92.2 1.8 %collective-permute-start.12 = (bf16[144,512]{1,0:T(8,128)(2,1)S(1)}, bf16[144,512]{1,0:T(8,128)(2,1)S(1)}, u32[]{:S(2)}, u32[]{:S(2)}) collective-permute-start(bf16[144,512]{1,0:T(8,128)(2,1)S(1)} %get-tuple-element.70), channel_id=1, source_target_pairs={{0,32},{32,64},{64,96},{96,0},{1,33},{33,65},{65,97},{97,1},{2,34}... | collective-permute-start | bytes 442376 | tf_op jit(solution)/shard_map/ppermute | solution.py:401
  94.0 3.0 %collective-permute-start.13 = (bf16[144,512]{1,0:T(8,128)(2,1)S(1)}, bf16[144,512]{1,0:T(8,128)(2,1)S(1)}, u32[]{:S(2)}, u32[]{:S(2)}) collective-permute-start(bf16[144,512]{1,0:T(8,128)(2,1)S(1)} %get-tuple-element.71), channel_id=1, source_target_pairs={{0,64},{32,96},{64,0},{96,32},{1,65},{33,97},{65,1},{97,33},{2,66}... | collective-permute-start | bytes 442376 | tf_op jit(solution)/shard_map/ppermute | solution.py:401
  98.4 2.0 %collective-permute-start.23 = (bf16[128,512]{1,0:T(8,128)(2,1)S(1)}, bf16[128,512]{1,0:T(8,128)(2,1)S(1)}, u32[]{:S(2)}, u32[]{:S(2)}) collective-permute-start(bf16[128,512]{1,0:T(8,128)(2,1)S(1)} %get-tuple-element.81), channel_id=1, source_target_pairs={{0,24},{8,0},{16,8},{24,16},{1,25},{9,1},{17,9},{25,17},{2,26},{10... | collective-permute-start | bytes 393224 | tf_op jit(solution)/shard_map/ppermute | solution.py:401
  100.4 3.3 %collective-permute-done.22.refs_6_ = bf16[128,512]{1,0:T(8,128)(2,1)S(1)} collective-permute-done((bf16[128,512]{1,0:T(8,128)(2,1)S(1)}, bf16[128,512]{1,0:T(8,128)(2,1)S(1)}, u32[]{:S(2)}, u32[]{:S(2)}) %collective-permute-start.22) | collective-permute-done | bytes 131104 | tf_op jit(solution)/shard_map/ppermute | solution.py:401
  103.7 2.5 %collective-permute-done.23.refs_7_ = bf16[128,512]{1,0:T(8,128)(2,1)S(1)} collective-permute-done((bf16[128,512]{1,0:T(8,128)(2,1)S(1)}, bf16[128,512]{1,0:T(8,128)(2,1)S(1)}, u32[]{:S(2)}, u32[]{:S(2)}) %collective-permute-start.23) | collective-permute-done | bytes 131104 | tf_op jit(solution)/shard_map/ppermute | solution.py:401
  106.4 1.7 %collective-permute-start.24 = (bf16[64,1024]{1,0:T(8,128)(2,1)S(1)}, bf16[64,1024]{1,0:T(8,128)(2,1)S(1)}, u32[]{:S(2)}, u32[]{:S(2)}) collective-permute-start(bf16[64,1024]{1,0:T(8,128)(2,1)S(1)} %get-tuple-element.84), channel_id=1, source_target_pairs={{0,4},{4,0},{1,5},{5,1},{2,6},{6,2},{3,7},{7,3},{8,12},{12,8},{9,1... | collective-permute-start | bytes 393224 | tf_op jit(solution)/shard_map/ppermute | solution.py:401
  108.1 1.2 collective-permute-done.25
  109.2 2.9 %collective-permute-start.26 = (f32[16,128]{1,0:T(8,128)S(1)}, f32[16,128]{1,0:T(8,128)S(1)}, u32[]{:S(2)}, u32[]{:S(2)}) collective-permute-start(f32[16,128]{1,0:T(8,128)S(1)} %add.11.refs_2_), channel_id=1, source_target_pairs={{0,2},{2,0},{1,3},{3,1},{4,6},{6,4},{5,7},{7,5},{8,10},{10,8},{9,1... | collective-permute-start | bytes 24584 | tf_op jit(solution)/shard_map/ppermute | solution.py:401
  114.4 1.3 %collective-permute-done.27.refs_4_ = f32[16,128]{1,0:T(8,128)S(1)} collective-permute-done((f32[16,128]{1,0:T(8,128)S(1)}, f32[16,128]{1,0:T(8,128)S(1)}, u32[]{:S(2)}, u32[]{:S(2)}) %collective-permute-start.27) | collective-permute-done | bytes 8224 | tf_op jit(solution)/shard_map/ppermute | solution.py:401
  115.8 1.3 %collective-permute-done.28.refs_5_ = f32[16,128]{1,0:T(8,128)S(1)} collective-permute-done((f32[16,128]{1,0:T(8,128)S(1)}, f32[16,128]{1,0:T(8,128)S(1)}, u32[]{:S(2)}, u32[]{:S(2)}) %collective-permute-start.28) | collective-permute-done | bytes 8224 | tf_op jit(solution)/shard_map/ppermute | solution.py:401
  (56 shorter events, 9.3 us)
Async XLA Ops:
  7.4 2.0 %collective-permute-start.3 = (bf16[256,1024]{1,0:T(8,128)(2,1)S(1)}, bf16[256,1024]{1,0:T(8,128)(2,1)S(1)}, u32[]{:S(2)}, u32[]{:S(2)}) collective-permute-start(bf16[256,1024]{1,0:T(8,128)(2,1)S(1)} %get-tuple-element.56), channel_id=1, source_target_pairs={{0,1},{1,0},{2,3},{3,2},{4,5},{5,4},{6,7},{7,6},{8,9},{9,8},{10,11... | collective-permute-start | bytes 1572872 | tf_op jit(solution)/shard_map/ppermute | solution.py:401
  9.6 8.1 %copy-start.1 = (bf16[256,2048]{1,0:T(8,128)(2,1)S(1)}, bf16[256,2048]{1,0:T(8,128)(2,1)}, u32[]{:S(2)}) copy-start(bf16[256,2048]{1,0:T(8,128)(2,1)} %refs_0_.3) | copy-start | bytes 3145732
  9.6 8.1 %copy-start.3 = (bf16[256,2048]{1,0:T(8,128)(2,1)S(1)}, bf16[256,2048]{1,0:T(8,128)(2,1)}, u32[]{:S(2)}) copy-start(bf16[256,2048]{1,0:T(8,128)(2,1)} %refs_1_.5) | copy-start | bytes 3145732
  9.6 8.1 %copy-start.6 = (f32[256]{0:T(256)S(1)}, f32[256]{0:T(256)}, u32[]{:S(2)}) copy-start(f32[256]{0:T(256)} %param.14) | copy-start | bytes 3076
  14.2 3.7 %collective-permute-start.4 = (bf16[256,1024]{1,0:T(8,128)(2,1)S(1)}, bf16[256,1024]{1,0:T(8,128)(2,1)S(1)}, u32[]{:S(2)}, u32[]{:S(2)}) collective-permute-start(bf16[256,1024]{1,0:T(8,128)(2,1)S(1)} %get-tuple-element.58), channel_id=1, source_target_pairs={{0,1},{1,0},{2,3},{3,2},{4,5},{5,4},{6,7},{7,6},{8,9},{9,8},{10,11... | collective-permute-start | bytes 1572872 | tf_op jit(solution)/shard_map/ppermute | solution.py:401
  14.4 15.8 %collective-permute-start.6 = (bf16[256,1024]{1,0:T(8,128)(2,1)S(1)}, bf16[256,1024]{1,0:T(8,128)(2,1)S(1)}, u32[]{:S(2)}, u32[]{:S(2)}) collective-permute-start(bf16[256,1024]{1,0:T(8,128)(2,1)S(1)} %add_convert_fusion.1.refs_9_.refs_0_), channel_id=1, source_target_pairs={{0,2},{2,0},{1,3},{3,1},{4,6},{6,4},{5,7},{7,5},{8,10},{10,8},{9,1... | collective-permute-start | bytes 1572872 | tf_op jit(solution)/shard_map/ppermute | solution.py:401
  30.4 3.4 %collective-permute-start.7 = (bf16[256,1024]{1,0:T(8,128)(2,1)S(1)}, bf16[256,1024]{1,0:T(8,128)(2,1)S(1)}, u32[]{:S(2)}, u32[]{:S(2)}) collective-permute-start(bf16[256,1024]{1,0:T(8,128)(2,1)S(1)} %shard_map.143.refs_0_), channel_id=1, source_target_pairs={{0,1},{1,0},{2,3},{3,2},{4,5},{5,4},{6,7},{7,6},{8,9},{9,8},{10,11... | collective-permute-start | bytes 1572872 | tf_op jit(solution)/shard_map/ppermute | solution.py:401
  30.5 15.8 %collective-permute-start.5 = (bf16[256,1024]{1,0:T(8,128)(2,1)S(1)}, bf16[256,1024]{1,0:T(8,128)(2,1)S(1)}, u32[]{:S(2)}, u32[]{:S(2)}) collective-permute-start(bf16[256,1024]{1,0:T(8,128)(2,1)S(1)} %add_convert_fusion.refs_4_.refs_0_), channel_id=1, source_target_pairs={{0,2},{2,0},{1,3},{3,1},{4,6},{6,4},{5,7},{7,5},{8,10},{10,8},{9,1... | collective-permute-start | bytes 1572872 | tf_op jit(solution)/shard_map/ppermute | solution.py:401
  46.5 7.8 %collective-permute-start.8 = (bf16[256,1024]{1,0:T(8,128)(2,1)S(1)}, bf16[256,1024]{1,0:T(8,128)(2,1)S(1)}, u32[]{:S(2)}, u32[]{:S(2)}) collective-permute-start(bf16[256,1024]{1,0:T(8,128)(2,1)S(1)} %shard_map.145.refs_0_), channel_id=1, source_target_pairs={{0,1},{1,0},{2,3},{3,2},{4,5},{5,4},{6,7},{7,6},{8,9},{9,8},{10,11... | collective-permute-start | bytes 1572872 | tf_op jit(solution)/shard_map/ppermute | solution.py:401
  46.6 10.6 %collective-permute-start.15 = (bf16[512,256]{1,0:T(8,128)(2,1)S(1)}, bf16[512,256]{1,0:T(8,128)(2,1)S(1)}, u32[]{:S(2)}, u32[]{:S(2)}) collective-permute-start(bf16[512,256]{1,0:T(8,128)(2,1)S(1)} %get-tuple-element.74), channel_id=1, source_target_pairs={{0,32},{32,64},{64,96},{96,0},{1,33},{33,65},{65,97},{97,1},{2,34}... | collective-permute-start | bytes 786440 | tf_op jit(solution)/shard_map/ppermute | solution.py:401
  48.2 15.5 %collective-permute-start.16 = (bf16[512,256]{1,0:T(8,128)(2,1)S(1)}, bf16[512,256]{1,0:T(8,128)(2,1)S(1)}, u32[]{:S(2)}, u32[]{:S(2)}) collective-permute-start(bf16[512,256]{1,0:T(8,128)(2,1)S(1)} %get-tuple-element.75), channel_id=1, source_target_pairs={{0,64},{32,96},{64,0},{96,32},{1,65},{33,97},{65,1},{97,33},{2,66}... | collective-permute-start | bytes 786440 | tf_op jit(solution)/shard_map/ppermute | solution.py:401
  50.9 12.8 %collective-permute-start.17 = (bf16[512,256]{1,0:T(8,128)(2,1)S(1)}, bf16[512,256]{1,0:T(8,128)(2,1)S(1)}, u32[]{:S(2)}, u32[]{:S(2)}) collective-permute-start(bf16[512,256]{1,0:T(8,128)(2,1)S(1)} %get-tuple-element.76), channel_id=1, source_target_pairs={{0,96},{32,0},{64,32},{96,64},{1,97},{33,1},{65,33},{97,65},{2,98}... | collective-permute-start | bytes 786440 | tf_op jit(solution)/shard_map/ppermute | solution.py:401
  52.4 15.3 %collective-permute-start = (bf16[512,256]{1,0:T(8,128)(2,1)S(1)}, bf16[512,256]{1,0:T(8,128)(2,1)S(1)}, u32[]{:S(2)}, u32[]{:S(2)}) collective-permute-start(bf16[512,256]{1,0:T(8,128)(2,1)S(1)} %get-tuple-element.48), channel_id=1, source_target_pairs={{0,8},{8,16},{16,24},{24,0},{1,9},{9,17},{17,25},{25,1},{2,10},{10... | collective-permute-start | bytes 786440 | tf_op jit(solution)/shard_map/ppermute | solution.py:401
  56.6 12.7 %collective-permute-start.18 = (bf16[256,512]{1,0:T(8,128)(2,1)S(1)}, bf16[256,512]{1,0:T(8,128)(2,1)S(1)}, u32[]{:S(2)}, u32[]{:S(2)}) collective-permute-start(bf16[256,512]{1,0:T(8,128)(2,1)S(1)} %get-tuple-element.77.refs_4_), channel_id=1, source_target_pairs={{0,32},{32,64},{64,96},{96,0},{1,33},{33,65},{65,97},{97,1},{2,34}... | collective-permute-start | bytes 786440 | tf_op jit(solution)/shard_map/ppermute | solution.py:401
  57.2 17.3 %collective-permute-start.19 = (bf16[256,512]{1,0:T(8,128)(2,1)S(1)}, bf16[256,512]{1,0:T(8,128)(2,1)S(1)}, u32[]{:S(2)}, u32[]{:S(2)}) collective-permute-start(bf16[256,512]{1,0:T(8,128)(2,1)S(1)} %get-tuple-element.77.refs_4_), channel_id=1, source_target_pairs={{0,64},{32,96},{64,0},{96,32},{1,65},{33,97},{65,1},{97,33},{2,66}... | collective-permute-start | bytes 786440 | tf_op jit(solution)/shard_map/ppermute | solution.py:401
  63.8 12.6 %collective-permute-start.20 = (bf16[256,512]{1,0:T(8,128)(2,1)S(1)}, bf16[256,512]{1,0:T(8,128)(2,1)S(1)}, u32[]{:S(2)}, u32[]{:S(2)}) collective-permute-start(bf16[256,512]{1,0:T(8,128)(2,1)S(1)} %get-tuple-element.77.refs_4_), channel_id=1, source_target_pairs={{0,96},{32,0},{64,32},{96,64},{1,97},{33,1},{65,33},{97,65},{2,98}... | collective-permute-start | bytes 786440 | tf_op jit(solution)/shard_map/ppermute | solution.py:401
  63.8 15.5 %collective-permute-start.1 = (bf16[512,256]{1,0:T(8,128)(2,1)S(1)}, bf16[512,256]{1,0:T(8,128)(2,1)S(1)}, u32[]{:S(2)}, u32[]{:S(2)}) collective-permute-start(bf16[512,256]{1,0:T(8,128)(2,1)S(1)} %get-tuple-element.49), channel_id=1, source_target_pairs={{0,16},{8,24},{16,0},{24,8},{1,17},{9,25},{17,1},{25,9},{2,18},{10... | collective-permute-start | bytes 786440 | tf_op jit(solution)/shard_map/ppermute | solution.py:401
  67.6 23.8 %collective-permute-start.10 = (bf16[272,512]{1,0:T(8,128)(2,1)S(1)}, bf16[272,512]{1,0:T(8,128)(2,1)S(1)}, u32[]{:S(2)}, u32[]{:S(2)}) collective-permute-start(bf16[272,512]{1,0:T(8,128)(2,1)S(1)} %get-tuple-element.67.refs_4_), channel_id=1, source_target_pairs={{0,16},{8,24},{16,0},{24,8},{1,17},{9,25},{17,1},{25,9},{2,18},{10... | collective-permute-start | bytes 835592 | tf_op jit(solution)/shard_map/ppermute | solution.py:401
  69.3 22.2 %collective-permute-start.11 = (bf16[272,512]{1,0:T(8,128)(2,1)S(1)}, bf16[272,512]{1,0:T(8,128)(2,1)S(1)}, u32[]{:S(2)}, u32[]{:S(2)}) collective-permute-start(bf16[272,512]{1,0:T(8,128)(2,1)S(1)} %get-tuple-element.67.refs_4_), channel_id=1, source_target_pairs={{0,24},{8,0},{16,8},{24,16},{1,25},{9,1},{17,9},{25,17},{2,26},{10... | collective-permute-start | bytes 835592 | tf_op jit(solution)/shard_map/ppermute | solution.py:401
  74.4 17.0 %collective-permute-start.9 = (bf16[272,512]{1,0:T(8,128)(2,1)S(1)}, bf16[272,512]{1,0:T(8,128)(2,1)S(1)}, u32[]{:S(2)}, u32[]{:S(2)}) collective-permute-start(bf16[272,512]{1,0:T(8,128)(2,1)S(1)} %get-tuple-element.67.refs_4_), channel_id=1, source_target_pairs={{0,8},{8,16},{16,24},{24,0},{1,9},{9,17},{17,25},{25,1},{2,10},{10... | collective-permute-start | bytes 835592 | tf_op jit(solution)/shard_map/ppermute | solution.py:401
  76.4 15.1 %collective-permute-start.2 = (bf16[512,256]{1,0:T(8,128)(2,1)S(1)}, bf16[512,256]{1,0:T(8,128)(2,1)S(1)}, u32[]{:S(2)}, u32[]{:S(2)}) collective-permute-start(bf16[512,256]{1,0:T(8,128)(2,1)S(1)} %get-tuple-element.50), channel_id=1, source_target_pairs={{0,24},{8,0},{16,8},{24,16},{1,25},{9,1},{17,9},{25,17},{2,26},{10... | collective-permute-start | bytes 786440 | tf_op jit(solution)/shard_map/ppermute | solution.py:401
  79.2 19.2 %collective-permute-start.21 = (bf16[128,512]{1,0:T(8,128)(2,1)S(1)}, bf16[128,512]{1,0:T(8,128)(2,1)S(1)}, u32[]{:S(2)}, u32[]{:S(2)}) collective-permute-start(bf16[128,512]{1,0:T(8,128)(2,1)S(1)} %get-tuple-element.79), channel_id=1, source_target_pairs={{0,8},{8,16},{16,24},{24,0},{1,9},{9,17},{17,25},{25,1},{2,10},{10... | collective-permute-start | bytes 393224 | tf_op jit(solution)/shard_map/ppermute | solution.py:401
  92.2 14.0 %collective-permute-start.12 = (bf16[144,512]{1,0:T(8,128)(2,1)S(1)}, bf16[144,512]{1,0:T(8,128)(2,1)S(1)}, u32[]{:S(2)}, u32[]{:S(2)}) collective-permute-start(bf16[144,512]{1,0:T(8,128)(2,1)S(1)} %get-tuple-element.70), channel_id=1, source_target_pairs={{0,32},{32,64},{64,96},{96,0},{1,33},{33,65},{65,97},{97,1},{2,34}... | collective-permute-start | bytes 442376 | tf_op jit(solution)/shard_map/ppermute | solution.py:401
  94.0 12.2 %collective-permute-start.13 = (bf16[144,512]{1,0:T(8,128)(2,1)S(1)}, bf16[144,512]{1,0:T(8,128)(2,1)S(1)}, u32[]{:S(2)}, u32[]{:S(2)}) collective-permute-start(bf16[144,512]{1,0:T(8,128)(2,1)S(1)} %get-tuple-element.71), channel_id=1, source_target_pairs={{0,64},{32,96},{64,0},{96,32},{1,65},{33,97},{65,1},{97,33},{2,66}... | collective-permute-start | bytes 442376 | tf_op jit(solution)/shard_map/ppermute | solution.py:401
  97.1 9.2 %collective-permute-start.14 = (bf16[144,512]{1,0:T(8,128)(2,1)S(1)}, bf16[144,512]{1,0:T(8,128)(2,1)S(1)}, u32[]{:S(2)}, u32[]{:S(2)}) collective-permute-start(bf16[144,512]{1,0:T(8,128)(2,1)S(1)} %get-tuple-element.72), channel_id=1, source_target_pairs={{0,96},{32,0},{64,32},{96,64},{1,97},{33,1},{65,33},{97,65},{2,98}... | collective-permute-start | bytes 442376 | tf_op jit(solution)/shard_map/ppermute | solution.py:401
  97.2 6.5 %collective-permute-start.22 = (bf16[128,512]{1,0:T(8,128)(2,1)S(1)}, bf16[128,512]{1,0:T(8,128)(2,1)S(1)}, u32[]{:S(2)}, u32[]{:S(2)}) collective-permute-start(bf16[128,512]{1,0:T(8,128)(2,1)S(1)} %get-tuple-element.80), channel_id=1, source_target_pairs={{0,16},{8,24},{16,0},{24,8},{1,17},{9,25},{17,1},{25,9},{2,18},{10... | collective-permute-start | bytes 393224 | tf_op jit(solution)/shard_map/ppermute | solution.py:401
  98.4 7.9 %collective-permute-start.23 = (bf16[128,512]{1,0:T(8,128)(2,1)S(1)}, bf16[128,512]{1,0:T(8,128)(2,1)S(1)}, u32[]{:S(2)}, u32[]{:S(2)}) collective-permute-start(bf16[128,512]{1,0:T(8,128)(2,1)S(1)} %get-tuple-element.81), channel_id=1, source_target_pairs={{0,24},{8,0},{16,8},{24,16},{1,25},{9,1},{17,9},{25,17},{2,26},{10... | collective-permute-start | bytes 393224 | tf_op jit(solution)/shard_map/ppermute | solution.py:401
  106.4 10.7 %collective-permute-start.24 = (bf16[64,1024]{1,0:T(8,128)(2,1)S(1)}, bf16[64,1024]{1,0:T(8,128)(2,1)S(1)}, u32[]{:S(2)}, u32[]{:S(2)}) collective-permute-start(bf16[64,1024]{1,0:T(8,128)(2,1)S(1)} %get-tuple-element.84), channel_id=1, source_target_pairs={{0,4},{4,0},{1,5},{5,1},{2,6},{6,2},{3,7},{7,3},{8,12},{12,8},{9,1... | collective-permute-start | bytes 393224 | tf_op jit(solution)/shard_map/ppermute | solution.py:401
  108.1 1.2 collective-permute-start.25
  109.2 5.2 %collective-permute-start.26 = (f32[16,128]{1,0:T(8,128)S(1)}, f32[16,128]{1,0:T(8,128)S(1)}, u32[]{:S(2)}, u32[]{:S(2)}) collective-permute-start(f32[16,128]{1,0:T(8,128)S(1)} %add.11.refs_2_), channel_id=1, source_target_pairs={{0,2},{2,0},{1,3},{3,1},{4,6},{6,4},{5,7},{7,5},{8,10},{10,8},{9,1... | collective-permute-start | bytes 24584 | tf_op jit(solution)/shard_map/ppermute | solution.py:401
  112.1 3.7 %collective-permute-start.27 = (f32[16,128]{1,0:T(8,128)S(1)}, f32[16,128]{1,0:T(8,128)S(1)}, u32[]{:S(2)}, u32[]{:S(2)}) collective-permute-start(f32[16,128]{1,0:T(8,128)S(1)} %add.11.refs_2_), channel_id=1, source_target_pairs={{0,4},{4,0},{1,5},{5,1},{2,6},{6,2},{3,7},{7,3},{8,12},{12,8},{9,1... | collective-permute-start | bytes 24584 | tf_op jit(solution)/shard_map/ppermute | solution.py:401
  112.3 4.9 %collective-permute-start.28 = (f32[16,128]{1,0:T(8,128)S(1)}, f32[16,128]{1,0:T(8,128)S(1)}, u32[]{:S(2)}, u32[]{:S(2)}) collective-permute-start(f32[16,128]{1,0:T(8,128)S(1)} %add.11.refs_2_), channel_id=1, source_target_pairs={{0,6},{2,4},{4,2},{6,0},{1,7},{3,5},{5,3},{7,1},{8,14},{10,12},{12... | collective-permute-start | bytes 24584 | tf_op jit(solution)/shard_map/ppermute | solution.py:401
  (4 other events, 13.4 us)

commit v2 on v1

--- a/solution.py
+++ b/solution.py
@@ -21,6 +21,7 @@
 VMEM = pl.BlockSpec(memory_space=pltpu.VMEM)
 ANY = pl.BlockSpec(memory_space=pl.ANY)
 HBM = pl.BlockSpec(memory_space=pltpu.HBM)
+SMEM = pl.BlockSpec(memory_space=pltpu.SMEM)
 
 
 def shape(dims, kind):
@@ -37,7 +38,7 @@
         whole,
         out_shape=outs,
         in_specs=list(ins) + [ANY] * len(after),
-        out_specs=jax.tree.map(lambda _: VMEM, outs),
+        out_specs=jax.tree.map(lambda out: VMEM if len(out.shape) > 1 else SMEM, outs),
         scratch_shapes=scratch,
         cost_estimate=pl.CostEstimate(flops=flops, bytes_accessed=moved, transcendentals=0),
         compiler_params=pltpu.CompilerParams(vmem_limit_bytes=limit * MIB),
@@ -93,8 +94,10 @@
     return high, middle, low
 
 
-def pieces_of(value):
-    return jnp.concatenate(list(split3(value)) + [jnp.zeros(value.shape, bf16)], axis=1)
+def pieces_of(value, columns):
+    pieces = split3(value)
+    blank = columns // value.shape[1] - len(pieces)
+    return jnp.concatenate([*pieces] + [jnp.zeros(value.shape, bf16)] * blank, axis=1)
 
 
 def read_sums(part):
@@ -242,12 +245,18 @@
     own_out[...] = dot(tangents, wo[:, pl.ds(mine, half)])
 
 
-def base_body(tokens, targets, loss_weights, base_out, weight_out):
+def base_body(tokens, targets, loss_weights, base_out, weight_out, sign_out, *, groups):
     half = base_out.shape[1]
     length = base_out.shape[0]
     mine = pl.multiple_of(lax.axis_index("c") * half, half)
     base_out[...] = tokens[:, pl.ds(mine, half)].astype(f32) - targets[:, pl.ds(mine, half)].astype(f32)
     weight_out[...] = jnp.broadcast_to(loss_weights[...] * (1.0 / length), (HEAD_DIM, length)).T
+    rows, feat = sign_out.shape
+    x, z, yl = (lax.axis_index(axis) for axis in DP)
+    row0 = ((x * 4 + z) * 2 + yl) * rows
+    col0 = (lax.axis_index("yh") * 2 + lax.axis_index("c")) * feat
+    _, square = square_state(row0, col0, (rows, feat))
+    sign_out[...] = sign_of(square.astype(f32)) * (1.0 / groups)
 
 
 def residual_body(near, far, base, weight, out):
@@ -285,7 +294,7 @@
 
 def third_body(
     res_own, res_mate, wo, q_ref, k_ref, v_ref, p_ref, hq_ref, hk_ref, r_ref, head_bits, table,
-    yq_out, yk_out, sum_out,
+    ya_out, yb_out, sum_out,
 ):
     feat = q_ref.shape[1]
     back = back_of(res_own, res_mate, wo)
@@ -300,16 +309,27 @@
         hq = (hq_ref[:, s] + dot(first, k_ref[:, s])) * SCALE
         hk = (hk_ref[:, s] + dot_tn(first, q_ref[:, s])) * SCALE
         product = r_ref[:, s]
-        for i, (gradient, y_out) in enumerate(((hq, yq_out), (hk, yk_out))):
+        for i, gradient in enumerate((hq, hk)):
             y = rotate(gradient, cosine, -sine) * signs[i : i + 1, s]
             y = y.astype(bf16)
-            y_out[: y.shape[0], s] = y
+            column, cut = i * feat + h * HEAD_DIM, ya_out.shape[1]
+            if column < cut:
+                ya_out[:, column : column + HEAD_DIM] = y
+            else:
+                yb_out[:, column - cut : column - cut + HEAD_DIM] = y
             totals[i] = totals[i] + jnp.sum(product * y.astype(f32), axis=0, keepdims=True)
     pair = [jnp.sum(t, axis=1, keepdims=True) for t in totals]
     lane = lax.broadcasted_iota(i32, sum_out.shape, 1)
     total = jnp.where(lane == 0, pair[0], jnp.where(lane == 1, pair[1], 0.0))
     sum_out[...] = total
-    yq_out[yk_out.shape[0] :, :] = pieces_of(total)
+
+
+def stamp_body(y, near, far, out, sum_out):
+    length = y.shape[0]
+    total = near[...] + far[...]
+    sum_out[...] = total
+    out[:length, :] = y[...]
+    out[length:, :] = pieces_of(total, out.shape[1])
 
 
 def transpose_body(normed, model_bits, *refs):
@@ -337,7 +357,15 @@
     return sum(dot(a[...], b[:length, :]) for a, b in zip(x_parts, y_parts))
 
 
-def estimate_q_body(*refs):
+def estimate_a_body(*refs):
+    outs = refs[8:]
+    group = outs[0].shape[0]
+    whole = rows_times(refs[:4], refs[4:8])
+    for step, out in enumerate(outs):
+        out[...] = whole[step * group : (step + 1) * group, :].astype(out.dtype)
+
+
+def estimate_b_body(*refs):
     y_parts, sums, outs, sum_out = refs[4:8], refs[8], refs[9:13], refs[13]
     length = refs[0].shape[1]
     group = outs[0].shape[0]
@@ -347,39 +375,31 @@
     for step, out in enumerate(outs):
         out[:group, :] = whole[step * group : (step + 1) * group, :].astype(out.dtype)
         if step > 0:
-            out[group:, :] = pieces_of(total)
-
-
-def estimate_k_body(*refs):
-    outs = refs[8:]
-    group = outs[0].shape[0]
-    whole = rows_times(refs[:4], refs[4:8])
-    for step, out in enumerate(outs):
-        out[...] = whole[step * group : (step + 1) * group, :].astype(out.dtype)
+            out[group:, :] = pieces_of(total, out.shape[1])
 
 
 def middle_body(a0, a1, a2, a3, b0, b1, b2, b3, sums, keep, send, sum_out):
-    group, feat = b0.shape
+    group, cut = a0.shape
     rows = group // 2
-    a = a0[...] + sum(r[:group, :].astype(f32) for r in (a1, a2, a3))
-    b = b0[...] + sum(r[...].astype(f32) for r in (b1, b2, b3))
-    keep[:, :feat] = a[:rows, :]
-    keep[:, feat:] = b[:rows, :]
-    send[:, :feat] = a[rows:, :].astype(bf16)
-    send[:, feat:] = b[rows:, :].astype(bf16)
-    sum_out[...] = in_pairs(sums[...], *(read_sums(r[group:, :]) for r in (a1, a2, a3)))
-
-
-def final_body(keep, came, s0, s1, s2, s3, diag_query, diag_key, mean_out, *, groups, entries):
+    a = a0[...] + sum(r[...].astype(f32) for r in (a1, a2, a3))
+    b = b0[...] + sum(r[:group, :].astype(f32) for r in (b1, b2, b3))
+    keep[:, :cut] = a[:rows, :]
+    keep[:, cut:] = b[:rows, :]
+    send[:rows, :cut] = a[rows:, :].astype(bf16)
+    send[:rows, cut:] = b[rows:, :].astype(bf16)
+    total = in_pairs(sums[...], *(read_sums(r[group:, :]) for r in (b1, b2, b3)))
+    sum_out[...] = total
+    send[rows:, :] = pieces_of(total, send.shape[1])
+
+
+def final_body(keep, came, sums, sign, diag_query, diag_key, mean_out, *, count):
     rows, feat = diag_query.shape
-    x, z, yl = (lax.axis_index(axis) for axis in DP)
-    row0 = ((x * 4 + z) * 2 + yl) * rows
-    col0 = (lax.axis_index("yh") * 2 + lax.axis_index("c")) * feat
-    _, square = square_state(row0, col0, (rows, feat))
-    sign = sign_of(square.astype(f32)) * (1.0 / groups)
-    diag_query[...] = sign * (keep[:, :feat] + came[:, :feat].astype(f32))
-    diag_key[...] = sign * (keep[:, feat:] + came[:, feat:].astype(f32))
-    mean_out[...] = in_pairs(s0[...], s1[...], s2[...], s3[...]) * (1.0 / (groups * entries))
+    diag_query[...] = sign[...] * (keep[:, :feat] + came[:rows, :feat].astype(f32))
+    diag_key[...] = sign[...] * (keep[:, feat:] + came[:rows, feat:].astype(f32))
+    total = sums[...] + read_sums(came[rows:, :])
+    lane = lax.broadcasted_iota(i32, (1, total.shape[1]), 1)
+    for i in range(2):
+        mean_out[i] = jnp.sum(jnp.where(lane == i, total[0:1, :], 0.0)) * (1.0 / count)
 
 
 def flip(value, moves):
@@ -462,9 +482,10 @@
     xq = [sends[0]] + [flip(m, where) for m, where in zip(sends[1:4], along_z)]
     xk = [sends[4]] + [flip(m, where) for m, where in zip(sends[5:8], along_x)]
 
-    base, row_weight = call(
-        base_body,
-        (half32, shape((length, HEAD_DIM), f32)),
+    rows = width // 32
+    base, row_weight, sign = call(
+        functools.partial(base_body, groups=groups),
+        (half32, shape((length, HEAD_DIM), f32), shape((rows, feat), f32)),
         [VMEM] * 3,
         (), 0, 3 * MIB, 16, (d_own,),
     )(tokens, targets, loss_weights[None, :])
@@ -480,52 +501,52 @@
 
     d_res_own = call(d_residual_body, half16, [VMEM] * 3, (), 0, 2 * MIB, 16, (hq,))(d_near, d_there, row_weight)
     d_res_mate = flip(d_res_own, mate)
-    yq, yk, sums = call(
+    cut = 5 * feat // 4
+    rest = 2 * feat - cut
+    small_sums = shape((16, HEAD_DIM), f32)
+    ya, yb, sums = call(
         third_body,
-        (shape((length + 16, feat), bf16), mat, shape((16, HEAD_DIM), f32)),
+        (shape((length, cut), bf16), shape((length, rest), bf16), small_sums),
         [VMEM] * 12,
         (), product + 3 * small, 6 * MIB, 24,
     )(d_res_own, d_res_mate, w_out, q, k, v, p, hq, hk, r, head_bits, table)
-    yq_in = [yq] + [flip(yq, where) for where in along_z]
-    yk_in = [yk] + [flip(yk, where) for where in along_x]
-
-    rows = width // 32
+    ya_in = [ya] + [flip(ya, where) for where in along_z]
+    sums = sums + flip(sums, mate)
+    yb, sums = call(stamp_body, (shape((length + 16, rest), bf16), small_sums), [VMEM] * 3, (), 0, MIB, 16)(
+        yb, sums, flip(sums, far)
+    )
+    yb_in = [yb] + [flip(yb, where) for where in along_x]
+
     group = 2 * rows
-    a_out, b_out = shape((group + 16, feat), bf16), shape((group, feat), bf16)
-    keep = shape((group, feat), f32)
-    *parts, sums = call(
-        estimate_q_body,
-        (keep, a_out, a_out, a_out, shape((16, HEAD_DIM), f32)),
+    part, keep = shape((group, cut), bf16), shape((group, cut), f32)
+    a = call(
+        estimate_a_body,
+        (keep, part, part, part),
+        [VMEM] * 8,
+        (), product, 3 * MIB, 24,
+    )(*xq, *ya_in)
+    part, keep = shape((group + 16, rest), bf16), shape((group, rest), f32)
+    *b, sums = call(
+        estimate_b_body,
+        (keep, part, part, part, small_sums),
         [VMEM] * 9,
         (), product, 3 * MIB, 24,
-    )(*xq, *yq_in, sums)
-    parts += call(
-        estimate_k_body,
-        (keep, b_out, b_out, b_out),
-        [VMEM] * 8,
-        (), product, 3 * MIB, 24,
-    )(*xk, *yk_in)
-    a_in, b_in = [], []
-    for i in range(3):
-        a_in.append(flip(parts[1 + i], along_x[i]))
-        b_in.append(flip(parts[5 + i], along_z[i]))
+    )(*xk, *yb_in, sums)
+    a_in = [flip(part, where) for part, where in zip(a[1:], along_x)]
+    b_in = [flip(part, where) for part, where in zip(b[1:], along_z)]
     keep, send, sums = call(
         middle_body,
-        (shape((rows, 2 * feat), f32), shape((rows, 2 * feat), bf16), shape((16, HEAD_DIM), f32)),
+        (shape((rows, 2 * feat), f32), shape((rows + 16, 2 * feat), bf16), small_sums),
         [VMEM] * 9,
         (), 0, 3 * MIB, 24,
-    )(parts[0], *a_in, parts[4], *b_in, sums)
-    side = [xor("yl", 1)]
-    came = flip(send, side)
-    sums = sums + flip(sums, mate)
-    sums = [sums] + [flip(sums, where) for where in (far, side, side + far)]
+    )(a[0], *a_in, b[0], *b_in, sums)
     diag_query, diag_key, mean = call(
-        functools.partial(final_body, groups=groups, entries=entries),
-        (shape((rows, feat), f32), shape((rows, feat), f32), shape((16, HEAD_DIM), f32)),
-        [VMEM] * 6,
+        functools.partial(final_body, count=groups * entries),
+        (shape((rows, feat), f32), shape((rows, feat), f32), shape((2,), f32)),
+        [VMEM] * 4,
         (), 0, MIB, 16,
-    )(keep, came, *sums)
-    return diag_query, diag_key, mean[0, :2]
+    )(keep, flip(send, [xor("yl", 1)]), sums, sign)
+    return diag_query, diag_key, mean
 
 
 def solution(mesh):

time: 119 us -> 115 us (0.966)
  waiting for transfers between devices: 53.7 us -> 47.7 us
  starting transfers between devices: 43.2 us -> 45.4 us
    ppermute x29 -> x27, waiting for transfers between devices: 53.7 us -> 47.7 us  [flip(): lax.ppermute(value, axes if len(axes) > 1 else axes[0], [(i, target(i)) f...]
    ppermute x29 -> x27, starting transfers between devices: 43.2 us -> 45.4 us  [flip(): lax.ppermute(value, axes if len(axes) > 1 else axes[0], [(i, target(i)) f...]
    pallas_call x12 -> x13, Pallas kernels: 19.9 us -> 20.2 us  [run(): return kernel(*args, *after)]
  transfers between devices with their start and end apart: 29 -> 27, of which waited for: 13 -> 11; matrix products, arithmetic and copies ran while one was open for 0% -> 0% of each run, Pallas kernels for 6% -> 7%
where the time goes in v2:
time: 115 us
  waiting for transfers between devices  47.7 us (41%)
  starting transfers between devices  45.4 us (39%)
  Pallas kernels  20.2 us (18%)
    ppermute x27, waiting for transfers between devices, flip(): lax.ppermute(value, axes if len(axes) > 1 else axes[0], [(i, target(i)) f...  47.7 us
    ppermute x27, starting transfers between devices, flip(): lax.ppermute(value, axes if len(axes) > 1 else axes[0], [(i, target(i)) f...  45.4 us
    pallas_call x13, Pallas kernels, run(): return kernel(*args, *after)  20.2 us
  transfers between devices with their start and end apart: 27, of which 11 were waited for; matrix products, arithmetic and copies ran while one was open for 0% of the time, Pallas kernels for 7%

profile of v2, /device:TPU:0, one launch (start us, length us, event | category | flops | bytes accessed | tf_op | source)
XLA Modules:
  0.0 114.7 jit_solution(1162481006404417472)
XLA Ops:
  0.6 6.7 %shard_map.139 = (bf16[256,2048]{1,0:T(8,128)(2,1)S(1)}, bf16[256,512]{1,0:T(8,128)(2,1)S(1)}, bf16[256,512]{1,0:T(8,128)(2,1)S(1)}, bf16[256,512]{1,0:T(8,128)(...) custom-call(bf16[256,2048]{1,0:T(8,128)(2,1)} %refs_0_.3, ...), custom_call_target="tpu_custom_call" | custom-call | flops 2415919104 | bytes 12582912 | tf_op jit(solution)/shard_map/pallas_call | solution.py:48
  8.0 1.4 %collective-permute-done.3 = bf16[256,1024]{1,0:T(8,128)(2,1)S(1)} collective-permute-done((bf16[256,1024]{1,0:T(8,128)(2,1)S(1)}, bf16[256,1024]{1,0:T(8,128)(2,1)S(1)}, u32[]{:S(2)}, u32[]{:S(2)}) %collective-permute-start.3) | collective-permute-done | bytes 524320 | tf_op jit(solution)/shard_map/ppermute | solution.py:421
  9.6 4.6 %shard_map.141 = (bf16[256,512]{1,0:T(8,128)(2,1)S(1)}, bf16[256,512]{1,0:T(8,128)(2,1)S(1)}, f32[256,512]{1,0:T(8,128)S(1)}, f32[4,256,256]{2,1,0:T(8,128)S(1)}...) custom-call(bf16[256,2048]{1,0:T(8,128)(2,1)S(1)} %get-tuple-element.46.refs_0_, s32[1,2048]{1,0:T(1,128)S(1)} %copy-done.4, ...), custom_call_target="tpu_custom_call" | custom-call | flops 1342177280 | bytes 8388608 | tf_op jit(solution)/shard_map/pallas_call | solution.py:48
  14.4 3.3 %collective-permute-start.6 = (bf16[256,1024]{1,0:T(8,128)(2,1)S(1)}, bf16[256,1024]{1,0:T(8,128)(2,1)S(1)}, u32[]{:S(2)}, u32[]{:S(2)}) collective-permute-start(bf16[256,1024]{1,0:T(8,128)(2,1)S(1)} %add_convert_fusion.1.refs_9_.refs_0_), channel_id=1, source_target_pairs={{0,2},{2,0},{1,3},{3,1},{4,6},{6,4},{5,7},{7,5},{8,10},{10,8},{9,1... | collective-permute-start | bytes 1572872 | tf_op jit(solution)/shard_map/ppermute | solution.py:421
  18.3 11.9 %collective-permute-done.6.refs_1_ = bf16[256,1024]{1,0:T(8,128)(2,1)S(1)} collective-permute-done((bf16[256,1024]{1,0:T(8,128)(2,1)S(1)}, bf16[256,1024]{1,0:T(8,128)(2,1)S(1)}, u32[]{:S(2)}, u32[]{:S(2)}) %collective-permute-start.6) | collective-permute-done | bytes 524320 | tf_op jit(solution)/shard_map/ppermute | solution.py:421
  30.5 3.3 %collective-permute-start.5 = (bf16[256,1024]{1,0:T(8,128)(2,1)S(1)}, bf16[256,1024]{1,0:T(8,128)(2,1)S(1)}, u32[]{:S(2)}, u32[]{:S(2)}) collective-permute-start(bf16[256,1024]{1,0:T(8,128)(2,1)S(1)} %add_convert_fusion.refs_4_.refs_0_), channel_id=1, source_target_pairs={{0,2},{2,0},{1,3},{3,1},{4,6},{6,4},{5,7},{7,5},{8,10},{10,8},{9,1... | collective-permute-start | bytes 1572872 | tf_op jit(solution)/shard_map/ppermute | solution.py:421
  33.8 2.8 %shard_map.144 = (f32[256,512]{1,0:T(8,128)S(1)}, f32[256,512]{1,0:T(8,128)S(1)}) custom-call(bf16[256,1024]{1,0:T(8,128)(2,1)S(1)} %shard_map.143.refs_0_, bf16[256,1024]{1,0:T(8,128)(2,1)S(1)} %collective-permute-done.7.refs_1_, bf16[512,2048]{1,0:T(8,128)(2,1)S(1)} %copy-done, bf16[256,512]{1,0:T(8,128)(2,1)S(1)} %get-tuple-element.51.refs_4_.refs_3_, ...), custom_call_target="tpu_custom_call" | custom-call | flops 872415232 | bytes 6291456 | tf_op jit(solution)/shard_map/pallas_call | solution.py:48
  36.6 9.7 %collective-permute-done.5.refs_1_ = bf16[256,1024]{1,0:T(8,128)(2,1)S(1)} collective-permute-done((bf16[256,1024]{1,0:T(8,128)(2,1)S(1)}, bf16[256,1024]{1,0:T(8,128)(2,1)S(1)}, u32[]{:S(2)}, u32[]{:S(2)}) %collective-permute-start.5) | collective-permute-done | bytes 524320 | tf_op jit(solution)/shard_map/ppermute | solution.py:421
  46.6 1.6 %collective-permute-start.15 = (bf16[512,256]{1,0:T(8,128)(2,1)S(1)}, bf16[512,256]{1,0:T(8,128)(2,1)S(1)}, u32[]{:S(2)}, u32[]{:S(2)}) collective-permute-start(bf16[512,256]{1,0:T(8,128)(2,1)S(1)} %get-tuple-element.73), channel_id=1, source_target_pairs={{0,32},{32,64},{64,96},{96,0},{1,33},{33,65},{65,97},{97,1},{2,34}... | collective-permute-start | bytes 786440 | tf_op jit(solution)/shard_map/ppermute | solution.py:421
  48.2 2.7 %collective-permute-start.16 = (bf16[512,256]{1,0:T(8,128)(2,1)S(1)}, bf16[512,256]{1,0:T(8,128)(2,1)S(1)}, u32[]{:S(2)}, u32[]{:S(2)}) collective-permute-start(bf16[512,256]{1,0:T(8,128)(2,1)S(1)} %get-tuple-element.74), channel_id=1, source_target_pairs={{0,64},{32,96},{64,0},{96,32},{1,65},{33,97},{65,1},{97,33},{2,66}... | collective-permute-start | bytes 786440 | tf_op jit(solution)/shard_map/ppermute | solution.py:421
  50.9 1.4 %collective-permute-start.17 = (bf16[512,256]{1,0:T(8,128)(2,1)S(1)}, bf16[512,256]{1,0:T(8,128)(2,1)S(1)}, u32[]{:S(2)}, u32[]{:S(2)}) collective-permute-start(bf16[512,256]{1,0:T(8,128)(2,1)S(1)} %get-tuple-element.75), channel_id=1, source_target_pairs={{0,96},{32,0},{64,32},{96,64},{1,97},{33,1},{65,33},{97,65},{2,98}... | collective-permute-start | bytes 786440 | tf_op jit(solution)/shard_map/ppermute | solution.py:421
  52.4 1.9 %collective-permute-start = (bf16[512,256]{1,0:T(8,128)(2,1)S(1)}, bf16[512,256]{1,0:T(8,128)(2,1)S(1)}, u32[]{:S(2)}, u32[]{:S(2)}) collective-permute-start(bf16[512,256]{1,0:T(8,128)(2,1)S(1)} %get-tuple-element.48), channel_id=1, source_target_pairs={{0,8},{8,16},{16,24},{24,0},{1,9},{9,17},{17,25},{25,1},{2,10},{10... | collective-permute-start | bytes 786440 | tf_op jit(solution)/shard_map/ppermute | solution.py:421
  54.3 2.3 %shard_map.146 = (bf16[256,640]{1,0:T(8,128)(2,1)S(1)}, bf16[256,384]{1,0:T(8,128)(2,1)S(1)}, f32[16,128]{1,0:T(8,128)S(1)}) custom-call(bf16[256,1024]{1,0:T(8,128)(2,1)S(1)} %shard_map.145.refs_0_, bf16[256,1024]{1,0:T(8,128)(2,1)S(1)} %collective-permute-done.8.refs_1_, bf16[512,2048]{1,0:T(8,128)(2,1)S(1)} %copy-done, ...), custom_call_target="tpu_custom_call" | custom-call | flops 738197504 | bytes 6291456 | tf_op jit(solution)/shard_map/pallas_call | solution.py:48
  57.8 3.2 %collective-permute-start.19 = (f32[16,128]{1,0:T(8,128)S(1)}, f32[16,128]{1,0:T(8,128)S(1)}, u32[]{:S(2)}, u32[]{:S(2)}) collective-permute-start(f32[16,128]{1,0:T(8,128)S(1)} %add.11.refs_1_), channel_id=1, source_target_pairs={{0,2},{2,0},{1,3},{3,1},{4,6},{6,4},{5,7},{7,5},{8,10},{10,8},{9,1... | collective-permute-start | bytes 24584 | tf_op jit(solution)/shard_map/ppermute | solution.py:421
  60.9 2.0 %collective-permute-done.19.refs_2_ = f32[16,128]{1,0:T(8,128)S(1)} collective-permute-done((f32[16,128]{1,0:T(8,128)S(1)}, f32[16,128]{1,0:T(8,128)S(1)}, u32[]{:S(2)}, u32[]{:S(2)}) %collective-permute-start.19) | collective-permute-done | bytes 8224 | tf_op jit(solution)/shard_map/ppermute | solution.py:421
  64.5 1.9 %collective-permute-start.22 = (bf16[272,384]{1,0:T(8,128)(2,1)S(1)}, bf16[272,384]{1,0:T(8,128)(2,1)S(1)}, u32[]{:S(2)}, u32[]{:S(2)}) collective-permute-start(bf16[272,384]{1,0:T(8,128)(2,1)S(1)} %get-tuple-element.78.refs_4_), channel_id=1, source_target_pairs={{0,96},{32,0},{64,32},{96,64},{1,97},{33,1},{65,33},{97,65},{2,98}... | collective-permute-start | bytes 626696 | tf_op jit(solution)/shard_map/ppermute | solution.py:421
  66.4 3.6 %collective-permute-start.10 = (bf16[256,640]{1,0:T(8,128)(2,1)S(1)}, bf16[256,640]{1,0:T(8,128)(2,1)S(1)}, u32[]{:S(2)}, u32[]{:S(2)}) collective-permute-start(bf16[256,640]{1,0:T(8,128)(2,1)S(1)} %get-tuple-element.67.refs_4_), channel_id=1, source_target_pairs={{0,16},{8,24},{16,0},{24,8},{1,17},{9,25},{17,1},{25,9},{2,18},{10... | collective-permute-start | bytes 983048 | tf_op jit(solution)/shard_map/ppermute | solution.py:421
  71.0 4.1 %collective-permute-done.20.refs_5_ = bf16[272,384]{1,0:T(8,128)(2,1)S(1)} collective-permute-done((bf16[272,384]{1,0:T(8,128)(2,1)S(1)}, bf16[272,384]{1,0:T(8,128)(2,1)S(1)}, u32[]{:S(2)}, u32[]{:S(2)}) %collective-permute-start.20) | collective-permute-done | bytes 208928 | tf_op jit(solution)/shard_map/ppermute | solution.py:421
  75.1 1.9 %collective-permute-start.9 = (bf16[256,640]{1,0:T(8,128)(2,1)S(1)}, bf16[256,640]{1,0:T(8,128)(2,1)S(1)}, u32[]{:S(2)}, u32[]{:S(2)}) collective-permute-start(bf16[256,640]{1,0:T(8,128)(2,1)S(1)} %get-tuple-element.67.refs_4_), channel_id=1, source_target_pairs={{0,8},{8,16},{16,24},{24,0},{1,9},{9,17},{17,25},{25,1},{2,10},{10... | collective-permute-start | bytes 983048 | tf_op jit(solution)/shard_map/ppermute | solution.py:421
  77.0 1.7 %collective-permute-start.1 = (bf16[512,256]{1,0:T(8,128)(2,1)S(1)}, bf16[512,256]{1,0:T(8,128)(2,1)S(1)}, u32[]{:S(2)}, u32[]{:S(2)}) collective-permute-start(bf16[512,256]{1,0:T(8,128)(2,1)S(1)} %get-tuple-element.49), channel_id=1, source_target_pairs={{0,16},{8,24},{16,0},{24,8},{1,17},{9,25},{17,1},{25,9},{2,18},{10... | collective-permute-start | bytes 786440 | tf_op jit(solution)/shard_map/ppermute | solution.py:421
  78.7 2.6 %collective-permute-start.2 = (bf16[512,256]{1,0:T(8,128)(2,1)S(1)}, bf16[512,256]{1,0:T(8,128)(2,1)S(1)}, u32[]{:S(2)}, u32[]{:S(2)}) collective-permute-start(bf16[512,256]{1,0:T(8,128)(2,1)S(1)} %get-tuple-element.50), channel_id=1, source_target_pairs={{0,24},{8,0},{16,8},{24,16},{1,25},{9,1},{17,9},{25,17},{2,26},{10... | collective-permute-start | bytes 786440 | tf_op jit(solution)/shard_map/ppermute | solution.py:421
  82.0 9.2 %collective-permute-done.1.refs_2_ = bf16[512,256]{1,0:T(8,128)(2,1)S(1)} collective-permute-done((bf16[512,256]{1,0:T(8,128)(2,1)S(1)}, bf16[512,256]{1,0:T(8,128)(2,1)S(1)}, u32[]{:S(2)}, u32[]{:S(2)}) %collective-permute-start.1) | collective-permute-done | bytes 262176 | tf_op jit(solution)/shard_map/ppermute | solution.py:421
  91.2 1.9 %collective-permute-start.23 = (bf16[144,384]{1,0:T(8,128)(2,1)S(1)}, bf16[144,384]{1,0:T(8,128)(2,1)S(1)}, u32[]{:S(2)}, u32[]{:S(2)}) collective-permute-start(bf16[144,384]{1,0:T(8,128)(2,1)S(1)} %get-tuple-element.81), channel_id=1, source_target_pairs={{0,8},{8,16},{16,24},{24,0},{1,9},{9,17},{17,25},{25,1},{2,10},{10... | collective-permute-start | bytes 331784 | tf_op jit(solution)/shard_map/ppermute | solution.py:421
  95.0 1.4 %collective-permute-start.12 = (bf16[128,640]{1,0:T(8,128)(2,1)S(1)}, bf16[128,640]{1,0:T(8,128)(2,1)S(1)}, u32[]{:S(2)}, u32[]{:S(2)}) collective-permute-start(bf16[128,640]{1,0:T(8,128)(2,1)S(1)} %get-tuple-element.69), channel_id=1, source_target_pairs={{0,32},{32,64},{64,96},{96,0},{1,33},{33,65},{65,97},{97,1},{2,34}... | collective-permute-start | bytes 491528 | tf_op jit(solution)/shard_map/ppermute | solution.py:421
  96.4 2.4 %collective-permute-start.13 = (bf16[128,640]{1,0:T(8,128)(2,1)S(1)}, bf16[128,640]{1,0:T(8,128)(2,1)S(1)}, u32[]{:S(2)}, u32[]{:S(2)}) collective-permute-start(bf16[128,640]{1,0:T(8,128)(2,1)S(1)} %get-tuple-element.70), channel_id=1, source_target_pairs={{0,64},{32,96},{64,0},{96,32},{1,65},{33,97},{65,1},{97,33},{2,66}... | collective-permute-start | bytes 491528 | tf_op jit(solution)/shard_map/ppermute | solution.py:421
  98.8 1.4 %collective-permute-start.14 = (bf16[128,640]{1,0:T(8,128)(2,1)S(1)}, bf16[128,640]{1,0:T(8,128)(2,1)S(1)}, u32[]{:S(2)}, u32[]{:S(2)}) collective-permute-start(bf16[128,640]{1,0:T(8,128)(2,1)S(1)} %get-tuple-element.71), channel_id=1, source_target_pairs={{0,96},{32,0},{64,32},{96,64},{1,97},{33,1},{65,33},{97,65},{2,98}... | collective-permute-start | bytes 491528 | tf_op jit(solution)/shard_map/ppermute | solution.py:421
  100.2 3.1 %collective-permute-start.24 = (bf16[144,384]{1,0:T(8,128)(2,1)S(1)}, bf16[144,384]{1,0:T(8,128)(2,1)S(1)}, u32[]{:S(2)}, u32[]{:S(2)}) collective-permute-start(bf16[144,384]{1,0:T(8,128)(2,1)S(1)} %get-tuple-element.82), channel_id=1, source_target_pairs={{0,16},{8,24},{16,0},{24,8},{1,17},{9,25},{17,1},{25,9},{2,18},{10... | collective-permute-start | bytes 331784 | tf_op jit(solution)/shard_map/ppermute | solution.py:421
  103.3 1.3 %collective-permute-start.25 = (bf16[144,384]{1,0:T(8,128)(2,1)S(1)}, bf16[144,384]{1,0:T(8,128)(2,1)S(1)}, u32[]{:S(2)}, u32[]{:S(2)}) collective-permute-start(bf16[144,384]{1,0:T(8,128)(2,1)S(1)} %get-tuple-element.83), channel_id=1, source_target_pairs={{0,24},{8,0},{16,8},{24,16},{1,25},{9,1},{17,9},{25,17},{2,26},{10... | collective-permute-start | bytes 331784 | tf_op jit(solution)/shard_map/ppermute | solution.py:421
  104.6 1.9 %collective-permute-done.24.refs_6_ = bf16[144,384]{1,0:T(8,128)(2,1)S(1)} collective-permute-done((bf16[144,384]{1,0:T(8,128)(2,1)S(1)}, bf16[144,384]{1,0:T(8,128)(2,1)S(1)}, u32[]{:S(2)}, u32[]{:S(2)}) %collective-permute-start.24) | collective-permute-done | bytes 110624 | tf_op jit(solution)/shard_map/ppermute | solution.py:421
  106.5 1.7 %collective-permute-done.25.refs_7_ = bf16[144,384]{1,0:T(8,128)(2,1)S(1)} collective-permute-done((bf16[144,384]{1,0:T(8,128)(2,1)S(1)}, bf16[144,384]{1,0:T(8,128)(2,1)S(1)}, u32[]{:S(2)}, u32[]{:S(2)}) %collective-permute-start.25) | collective-permute-done | bytes 110624 | tf_op jit(solution)/shard_map/ppermute | solution.py:421
  108.4 1.7 %collective-permute-start.26 = (bf16[80,1024]{1,0:T(8,128)(2,1)S(1)}, bf16[80,1024]{1,0:T(8,128)(2,1)S(1)}, u32[]{:S(2)}, u32[]{:S(2)}) collective-permute-start(bf16[80,1024]{1,0:T(8,128)(2,1)S(1)} %get-tuple-element.86), channel_id=1, source_target_pairs={{0,4},{4,0},{1,5},{5,1},{2,6},{6,2},{3,7},{7,3},{8,12},{12,8},{9,1... | collective-permute-start | bytes 491528 | tf_op jit(solution)/shard_map/ppermute | solution.py:421
  110.0 3.7 %collective-permute-done.26.refs_1_ = bf16[80,1024]{1,0:T(8,128)(2,1)S(1)} collective-permute-done((bf16[80,1024]{1,0:T(8,128)(2,1)S(1)}, bf16[80,1024]{1,0:T(8,128)(2,1)S(1)}, u32[]{:S(2)}, u32[]{:S(2)}) %collective-permute-start.26) | collective-permute-done | bytes 163872 | tf_op jit(solution)/shard_map/ppermute | solution.py:421
  (52 shorter events, 9.3 us)
Async XLA Ops:
  0.6 6.9 %copy-start.4 = (s32[1,2048]{1,0:T(1,128)S(1)}, s32[1,2048]{1,0:T(1,128)}, u32[]{:S(2)}) copy-start(s32[1,2048]{1,0:T(1,128)} %refs_1_.4) | copy-start | bytes 24580
  7.4 2.2 %copy-start = (bf16[512,2048]{1,0:T(8,128)(2,1)S(1)}, bf16[512,2048]{1,0:T(8,128)(2,1)}, u32[]{:S(2)}) copy-start(bf16[512,2048]{1,0:T(8,128)(2,1)} %refs_2_.5) | copy-start | bytes 6291460
  7.4 2.0 %collective-permute-start.3 = (bf16[256,1024]{1,0:T(8,128)(2,1)S(1)}, bf16[256,1024]{1,0:T(8,128)(2,1)S(1)}, u32[]{:S(2)}, u32[]{:S(2)}) collective-permute-start(bf16[256,1024]{1,0:T(8,128)(2,1)S(1)} %get-tuple-element.56), channel_id=1, source_target_pairs={{0,1},{1,0},{2,3},{3,2},{4,5},{5,4},{6,7},{7,6},{8,9},{9,8},{10,11... | collective-permute-start | bytes 1572872 | tf_op jit(solution)/shard_map/ppermute | solution.py:421
  9.6 8.1 %copy-start.1 = (bf16[256,2048]{1,0:T(8,128)(2,1)S(1)}, bf16[256,2048]{1,0:T(8,128)(2,1)}, u32[]{:S(2)}) copy-start(bf16[256,2048]{1,0:T(8,128)(2,1)} %refs_0_.3) | copy-start | bytes 3145732
  9.6 8.1 %copy-start.3 = (bf16[256,2048]{1,0:T(8,128)(2,1)S(1)}, bf16[256,2048]{1,0:T(8,128)(2,1)}, u32[]{:S(2)}) copy-start(bf16[256,2048]{1,0:T(8,128)(2,1)} %refs_1_.5) | copy-start | bytes 3145732
  9.6 8.1 %copy-start.6 = (f32[256]{0:T(256)S(1)}, f32[256]{0:T(256)}, u32[]{:S(2)}) copy-start(f32[256]{0:T(256)} %param.14) | copy-start | bytes 3076
  14.2 3.9 %collective-permute-start.4 = (bf16[256,1024]{1,0:T(8,128)(2,1)S(1)}, bf16[256,1024]{1,0:T(8,128)(2,1)S(1)}, u32[]{:S(2)}, u32[]{:S(2)}) collective-permute-start(bf16[256,1024]{1,0:T(8,128)(2,1)S(1)} %get-tuple-element.58), channel_id=1, source_target_pairs={{0,1},{1,0},{2,3},{3,2},{4,5},{5,4},{6,7},{7,6},{8,9},{9,8},{10,11... | collective-permute-start | bytes 1572872 | tf_op jit(solution)/shard_map/ppermute | solution.py:421
  14.4 15.8 %collective-permute-start.6 = (bf16[256,1024]{1,0:T(8,128)(2,1)S(1)}, bf16[256,1024]{1,0:T(8,128)(2,1)S(1)}, u32[]{:S(2)}, u32[]{:S(2)}) collective-permute-start(bf16[256,1024]{1,0:T(8,128)(2,1)S(1)} %add_convert_fusion.1.refs_9_.refs_0_), channel_id=1, source_target_pairs={{0,2},{2,0},{1,3},{3,1},{4,6},{6,4},{5,7},{7,5},{8,10},{10,8},{9,1... | collective-permute-start | bytes 1572872 | tf_op jit(solution)/shard_map/ppermute | solution.py:421
  30.4 3.4 %collective-permute-start.7 = (bf16[256,1024]{1,0:T(8,128)(2,1)S(1)}, bf16[256,1024]{1,0:T(8,128)(2,1)S(1)}, u32[]{:S(2)}, u32[]{:S(2)}) collective-permute-start(bf16[256,1024]{1,0:T(8,128)(2,1)S(1)} %shard_map.143.refs_0_), channel_id=1, source_target_pairs={{0,1},{1,0},{2,3},{3,2},{4,5},{5,4},{6,7},{7,6},{8,9},{9,8},{10,11... | collective-permute-start | bytes 1572872 | tf_op jit(solution)/shard_map/ppermute | solution.py:421
  30.5 15.8 %collective-permute-start.5 = (bf16[256,1024]{1,0:T(8,128)(2,1)S(1)}, bf16[256,1024]{1,0:T(8,128)(2,1)S(1)}, u32[]{:S(2)}, u32[]{:S(2)}) collective-permute-start(bf16[256,1024]{1,0:T(8,128)(2,1)S(1)} %add_convert_fusion.refs_4_.refs_0_), channel_id=1, source_target_pairs={{0,2},{2,0},{1,3},{3,1},{4,6},{6,4},{5,7},{7,5},{8,10},{10,8},{9,1... | collective-permute-start | bytes 1572872 | tf_op jit(solution)/shard_map/ppermute | solution.py:421
  46.5 7.8 %collective-permute-start.8 = (bf16[256,1024]{1,0:T(8,128)(2,1)S(1)}, bf16[256,1024]{1,0:T(8,128)(2,1)S(1)}, u32[]{:S(2)}, u32[]{:S(2)}) collective-permute-start(bf16[256,1024]{1,0:T(8,128)(2,1)S(1)} %shard_map.145.refs_0_), channel_id=1, source_target_pairs={{0,1},{1,0},{2,3},{3,2},{4,5},{5,4},{6,7},{7,6},{8,9},{9,8},{10,11... | collective-permute-start | bytes 1572872 | tf_op jit(solution)/shard_map/ppermute | solution.py:421
  46.6 17.0 %collective-permute-start.15 = (bf16[512,256]{1,0:T(8,128)(2,1)S(1)}, bf16[512,256]{1,0:T(8,128)(2,1)S(1)}, u32[]{:S(2)}, u32[]{:S(2)}) collective-permute-start(bf16[512,256]{1,0:T(8,128)(2,1)S(1)} %get-tuple-element.73), channel_id=1, source_target_pairs={{0,32},{32,64},{64,96},{96,0},{1,33},{33,65},{65,97},{97,1},{2,34}... | collective-permute-start | bytes 786440 | tf_op jit(solution)/shard_map/ppermute | solution.py:421
  48.2 16.3 %collective-permute-start.16 = (bf16[512,256]{1,0:T(8,128)(2,1)S(1)}, bf16[512,256]{1,0:T(8,128)(2,1)S(1)}, u32[]{:S(2)}, u32[]{:S(2)}) collective-permute-start(bf16[512,256]{1,0:T(8,128)(2,1)S(1)} %get-tuple-element.74), channel_id=1, source_target_pairs={{0,64},{32,96},{64,0},{96,32},{1,65},{33,97},{65,1},{97,33},{2,66}... | collective-permute-start | bytes 786440 | tf_op jit(solution)/shard_map/ppermute | solution.py:421
  50.9 15.5 %collective-permute-start.17 = (bf16[512,256]{1,0:T(8,128)(2,1)S(1)}, bf16[512,256]{1,0:T(8,128)(2,1)S(1)}, u32[]{:S(2)}, u32[]{:S(2)}) collective-permute-start(bf16[512,256]{1,0:T(8,128)(2,1)S(1)} %get-tuple-element.75), channel_id=1, source_target_pairs={{0,96},{32,0},{64,32},{96,64},{1,97},{33,1},{65,33},{97,65},{2,98}... | collective-permute-start | bytes 786440 | tf_op jit(solution)/shard_map/ppermute | solution.py:421
  52.4 17.6 %collective-permute-start = (bf16[512,256]{1,0:T(8,128)(2,1)S(1)}, bf16[512,256]{1,0:T(8,128)(2,1)S(1)}, u32[]{:S(2)}, u32[]{:S(2)}) collective-permute-start(bf16[512,256]{1,0:T(8,128)(2,1)S(1)} %get-tuple-element.48), channel_id=1, source_target_pairs={{0,8},{8,16},{16,24},{24,0},{1,9},{9,17},{17,25},{25,1},{2,10},{10... | collective-permute-start | bytes 786440 | tf_op jit(solution)/shard_map/ppermute | solution.py:421
  56.6 1.2 %collective-permute-start.18 = (f32[16,128]{1,0:T(8,128)S(1)}, f32[16,128]{1,0:T(8,128)S(1)}, u32[]{:S(2)}, u32[]{:S(2)}) collective-permute-start(f32[16,128]{1,0:T(8,128)S(1)} %get-tuple-element.77), channel_id=1, source_target_pairs={{0,1},{1,0},{2,3},{3,2},{4,5},{5,4},{6,7},{7,6},{8,9},{9,8},{10,11... | collective-permute-start | bytes 24584 | tf_op jit(solution)/shard_map/ppermute | solution.py:421
  57.8 5.2 %collective-permute-start.19 = (f32[16,128]{1,0:T(8,128)S(1)}, f32[16,128]{1,0:T(8,128)S(1)}, u32[]{:S(2)}, u32[]{:S(2)}) collective-permute-start(f32[16,128]{1,0:T(8,128)S(1)} %add.11.refs_1_), channel_id=1, source_target_pairs={{0,2},{2,0},{1,3},{3,1},{4,6},{6,4},{5,7},{7,5},{8,10},{10,8},{9,1... | collective-permute-start | bytes 24584 | tf_op jit(solution)/shard_map/ppermute | solution.py:421
  62.9 12.1 %collective-permute-start.20 = (bf16[272,384]{1,0:T(8,128)(2,1)S(1)}, bf16[272,384]{1,0:T(8,128)(2,1)S(1)}, u32[]{:S(2)}, u32[]{:S(2)}) collective-permute-start(bf16[272,384]{1,0:T(8,128)(2,1)S(1)} %get-tuple-element.78.refs_4_), channel_id=1, source_target_pairs={{0,32},{32,64},{64,96},{96,0},{1,33},{33,65},{65,97},{97,1},{2,34}... | collective-permute-start | bytes 626696 | tf_op jit(solution)/shard_map/ppermute | solution.py:421
  63.6 13.4 %collective-permute-start.21 = (bf16[272,384]{1,0:T(8,128)(2,1)S(1)}, bf16[272,384]{1,0:T(8,128)(2,1)S(1)}, u32[]{:S(2)}, u32[]{:S(2)}) collective-permute-start(bf16[272,384]{1,0:T(8,128)(2,1)S(1)} %get-tuple-element.78.refs_4_), channel_id=1, source_target_pairs={{0,64},{32,96},{64,0},{96,32},{1,65},{33,97},{65,1},{97,33},{2,66}... | collective-permute-start | bytes 626696 | tf_op jit(solution)/shard_map/ppermute | solution.py:421
  64.5 14.2 %collective-permute-start.22 = (bf16[272,384]{1,0:T(8,128)(2,1)S(1)}, bf16[272,384]{1,0:T(8,128)(2,1)S(1)}, u32[]{:S(2)}, u32[]{:S(2)}) collective-permute-start(bf16[272,384]{1,0:T(8,128)(2,1)S(1)} %get-tuple-element.78.refs_4_), channel_id=1, source_target_pairs={{0,96},{32,0},{64,32},{96,64},{1,97},{33,1},{65,33},{97,65},{2,98}... | collective-permute-start | bytes 626696 | tf_op jit(solution)/shard_map/ppermute | solution.py:421
  66.4 27.6 %collective-permute-start.10 = (bf16[256,640]{1,0:T(8,128)(2,1)S(1)}, bf16[256,640]{1,0:T(8,128)(2,1)S(1)}, u32[]{:S(2)}, u32[]{:S(2)}) collective-permute-start(bf16[256,640]{1,0:T(8,128)(2,1)S(1)} %get-tuple-element.67.refs_4_), channel_id=1, source_target_pairs={{0,16},{8,24},{16,0},{24,8},{1,17},{9,25},{17,1},{25,9},{2,18},{10... | collective-permute-start | bytes 983048 | tf_op jit(solution)/shard_map/ppermute | solution.py:421
  70.0 24.0 %collective-permute-start.11 = (bf16[256,640]{1,0:T(8,128)(2,1)S(1)}, bf16[256,640]{1,0:T(8,128)(2,1)S(1)}, u32[]{:S(2)}, u32[]{:S(2)}) collective-permute-start(bf16[256,640]{1,0:T(8,128)(2,1)S(1)} %get-tuple-element.67.refs_4_), channel_id=1, source_target_pairs={{0,24},{8,0},{16,8},{24,16},{1,25},{9,1},{17,9},{25,17},{2,26},{10... | collective-permute-start | bytes 983048 | tf_op jit(solution)/shard_map/ppermute | solution.py:421
  75.1 18.9 %collective-permute-start.9 = (bf16[256,640]{1,0:T(8,128)(2,1)S(1)}, bf16[256,640]{1,0:T(8,128)(2,1)S(1)}, u32[]{:S(2)}, u32[]{:S(2)}) collective-permute-start(bf16[256,640]{1,0:T(8,128)(2,1)S(1)} %get-tuple-element.67.refs_4_), channel_id=1, source_target_pairs={{0,8},{8,16},{16,24},{24,0},{1,9},{9,17},{17,25},{25,1},{2,10},{10... | collective-permute-start | bytes 983048 | tf_op jit(solution)/shard_map/ppermute | solution.py:421
  77.0 14.2 %collective-permute-start.1 = (bf16[512,256]{1,0:T(8,128)(2,1)S(1)}, bf16[512,256]{1,0:T(8,128)(2,1)S(1)}, u32[]{:S(2)}, u32[]{:S(2)}) collective-permute-start(bf16[512,256]{1,0:T(8,128)(2,1)S(1)} %get-tuple-element.49), channel_id=1, source_target_pairs={{0,16},{8,24},{16,0},{24,8},{1,17},{9,25},{17,1},{25,9},{2,18},{10... | collective-permute-start | bytes 786440 | tf_op jit(solution)/shard_map/ppermute | solution.py:421
  78.7 15.3 %collective-permute-start.2 = (bf16[512,256]{1,0:T(8,128)(2,1)S(1)}, bf16[512,256]{1,0:T(8,128)(2,1)S(1)}, u32[]{:S(2)}, u32[]{:S(2)}) collective-permute-start(bf16[512,256]{1,0:T(8,128)(2,1)S(1)} %get-tuple-element.50), channel_id=1, source_target_pairs={{0,24},{8,0},{16,8},{24,16},{1,25},{9,1},{17,9},{25,17},{2,26},{10... | collective-permute-start | bytes 786440 | tf_op jit(solution)/shard_map/ppermute | solution.py:421
  91.2 12.1 %collective-permute-start.23 = (bf16[144,384]{1,0:T(8,128)(2,1)S(1)}, bf16[144,384]{1,0:T(8,128)(2,1)S(1)}, u32[]{:S(2)}, u32[]{:S(2)}) collective-permute-start(bf16[144,384]{1,0:T(8,128)(2,1)S(1)} %get-tuple-element.81), channel_id=1, source_target_pairs={{0,8},{8,16},{16,24},{24,0},{1,9},{9,17},{17,25},{25,1},{2,10},{10... | collective-permute-start | bytes 331784 | tf_op jit(solution)/shard_map/ppermute | solution.py:421
  95.0 13.2 %collective-permute-start.12 = (bf16[128,640]{1,0:T(8,128)(2,1)S(1)}, bf16[128,640]{1,0:T(8,128)(2,1)S(1)}, u32[]{:S(2)}, u32[]{:S(2)}) collective-permute-start(bf16[128,640]{1,0:T(8,128)(2,1)S(1)} %get-tuple-element.69), channel_id=1, source_target_pairs={{0,32},{32,64},{64,96},{96,0},{1,33},{33,65},{65,97},{97,1},{2,34}... | collective-permute-start | bytes 491528 | tf_op jit(solution)/shard_map/ppermute | solution.py:421
  96.4 11.8 %collective-permute-start.13 = (bf16[128,640]{1,0:T(8,128)(2,1)S(1)}, bf16[128,640]{1,0:T(8,128)(2,1)S(1)}, u32[]{:S(2)}, u32[]{:S(2)}) collective-permute-start(bf16[128,640]{1,0:T(8,128)(2,1)S(1)} %get-tuple-element.70), channel_id=1, source_target_pairs={{0,64},{32,96},{64,0},{96,32},{1,65},{33,97},{65,1},{97,33},{2,66}... | collective-permute-start | bytes 491528 | tf_op jit(solution)/shard_map/ppermute | solution.py:421
  98.8 9.4 %collective-permute-start.14 = (bf16[128,640]{1,0:T(8,128)(2,1)S(1)}, bf16[128,640]{1,0:T(8,128)(2,1)S(1)}, u32[]{:S(2)}, u32[]{:S(2)}) collective-permute-start(bf16[128,640]{1,0:T(8,128)(2,1)S(1)} %get-tuple-element.71), channel_id=1, source_target_pairs={{0,96},{32,0},{64,32},{96,64},{1,97},{33,1},{65,33},{97,65},{2,98}... | collective-permute-start | bytes 491528 | tf_op jit(solution)/shard_map/ppermute | solution.py:421
  100.2 6.3 %collective-permute-start.24 = (bf16[144,384]{1,0:T(8,128)(2,1)S(1)}, bf16[144,384]{1,0:T(8,128)(2,1)S(1)}, u32[]{:S(2)}, u32[]{:S(2)}) collective-permute-start(bf16[144,384]{1,0:T(8,128)(2,1)S(1)} %get-tuple-element.82), channel_id=1, source_target_pairs={{0,16},{8,24},{16,0},{24,8},{1,17},{9,25},{17,1},{25,9},{2,18},{10... | collective-permute-start | bytes 331784 | tf_op jit(solution)/shard_map/ppermute | solution.py:421
  103.3 4.9 %collective-permute-start.25 = (bf16[144,384]{1,0:T(8,128)(2,1)S(1)}, bf16[144,384]{1,0:T(8,128)(2,1)S(1)}, u32[]{:S(2)}, u32[]{:S(2)}) collective-permute-start(bf16[144,384]{1,0:T(8,128)(2,1)S(1)} %get-tuple-element.83), channel_id=1, source_target_pairs={{0,24},{8,0},{16,8},{24,16},{1,25},{9,1},{17,9},{25,17},{2,26},{10... | collective-permute-start | bytes 331784 | tf_op jit(solution)/shard_map/ppermute | solution.py:421
  108.4 5.4 %collective-permute-start.26 = (bf16[80,1024]{1,0:T(8,128)(2,1)S(1)}, bf16[80,1024]{1,0:T(8,128)(2,1)S(1)}, u32[]{:S(2)}, u32[]{:S(2)}) collective-permute-start(bf16[80,1024]{1,0:T(8,128)(2,1)S(1)} %get-tuple-element.86), channel_id=1, source_target_pairs={{0,4},{4,0},{1,5},{5,1},{2,6},{6,2},{3,7},{7,3},{8,12},{12,8},{9,1... | collective-permute-start | bytes 491528 | tf_op jit(solution)/shard_map/ppermute | solution.py:421
  (2 other events, 4.4 us)

commit v3 on v2

--- a/solution.py
+++ b/solution.py
@@ -108,10 +108,15 @@
     return (own + second) + (first + third)
 
 
+def columns_of(half, own):
+    core = lax.axis_index("c")
+    return pl.ds(pl.multiple_of((core if own else 1 - core) * half, half), half)
+
+
 def forward_body(
     tok_hbm, gain_hbm, wq_hbm, wk_hbm, table_hbm, seg_hbm, wv_hbm, wo_hbm,
-    normed_out, q_out, k_out, v_out, p_out, send_out, own_out,
-    tok, gain, wq, wk, table, seg, wv, wo, sems,
+    normed_out, q_out, k_out, v_out, p_out, send_out, attended_out, wo,
+    tok, gain, wq, wk, table, seg, wv, sems,
 ):
     sources = (tok_hbm, gain_hbm, wq_hbm, wk_hbm, table_hbm, seg_hbm, wv_hbm, wo_hbm)
     places = (tok, gain, wq, wk, table, seg, wv, wo)
@@ -121,7 +126,6 @@
     length = tok.shape[0]
     heads = q_out.shape[1] // HEAD_DIM
     half = send_out.shape[1]
-    core = lax.axis_index("c")
     copies[0].wait()
     for copy in copies[3:]:
         copy.start()
@@ -160,10 +164,12 @@
         attended.append(dot(weights.astype(bf16), values[:, head(h)]).astype(bf16))
     attended = jnp.concatenate(attended, axis=1)
     copies[7].wait()
-    mine = pl.multiple_of(core * half, half)
-    other = pl.multiple_of((1 - core) * half, half)
-    send_out[...] = dot(attended, wo[:, pl.ds(other, half)]).astype(bf16)
-    own_out[...] = dot(attended, wo[:, pl.ds(mine, half)])
+    attended_out[...] = attended
+    send_out[...] = dot(attended, wo[:, columns_of(half, False)]).astype(bf16)
+
+
+def out_own_body(attended, wo, out):
+    out[...] = dot(attended[...], wo[:, columns_of(out.shape[1], True)])
 
 
 def small_mod(value):
@@ -269,13 +275,12 @@
 
 def back_of(res_own, res_mate, wo):
     half = res_own.shape[1]
-    core = lax.axis_index("c")
-    mine = pl.multiple_of(core * half, half)
-    other = pl.multiple_of((1 - core) * half, half)
-    return (
-        dot_nt(res_own[...], wo[:, pl.ds(mine, half)])
-        + dot_nt(res_mate[...], wo[:, pl.ds(other, half)])
-    ).astype(bf16)
+    own = dot_nt(res_own[...], wo[:, columns_of(half, True)])
+    return (own + dot_nt(res_mate[...], wo[:, columns_of(half, False)])).astype(bf16)
+
+
+def back_own_body(res_own, wo, out):
+    out[...] = dot_nt(res_own[...], wo[:, columns_of(res_own.shape[1], True)])
 
 
 def second_body(res_own, res_mate, wo, q_ref, k_ref, v_ref, dq_ref, dk_ref, p_ref, ds_ref, hq_out, hk_out):
@@ -293,11 +298,11 @@
 
 
 def third_body(
-    res_own, res_mate, wo, q_ref, k_ref, v_ref, p_ref, hq_ref, hk_ref, r_ref, head_bits, table,
+    back_own, res_mate, wo, q_ref, k_ref, v_ref, p_ref, hq_ref, hk_ref, r_ref, head_bits, table,
     ya_out, yb_out, sum_out,
 ):
     feat = q_ref.shape[1]
-    back = back_of(res_own, res_mate, wo)
+    back = (back_own[...] + dot_nt(res_mate[...], wo[:, columns_of(res_mate.shape[1], False)])).astype(bf16)
     signs = (2 * head_bits[...] - 1).astype(f32)
     cosine, sine = table[: table.shape[0] // 2], table[table.shape[0] // 2 :]
     totals = [0.0, 0.0]
@@ -378,24 +383,37 @@
             out[group:, :] = pieces_of(total, out.shape[1])
 
 
-def middle_body(a0, a1, a2, a3, b0, b1, b2, b3, sums, keep, send, sum_out):
-    group, cut = a0.shape
-    rows = group // 2
+def middle_a_body(a0, a1, a2, a3, keep, send):
+    rows = keep.shape[0]
     a = a0[...] + sum(r[...].astype(f32) for r in (a1, a2, a3))
+    keep[...] = a[:rows, :]
+    send[...] = a[rows:, :].astype(bf16)
+
+
+def middle_b_body(b0, b1, b2, b3, sums, keep, send, sum_out):
+    rows = keep.shape[0]
+    group = 2 * rows
     b = b0[...] + sum(r[:group, :].astype(f32) for r in (b1, b2, b3))
-    keep[:, :cut] = a[:rows, :]
-    keep[:, cut:] = b[:rows, :]
-    send[:rows, :cut] = a[rows:, :].astype(bf16)
-    send[:rows, cut:] = b[rows:, :].astype(bf16)
+    keep[...] = b[:rows, :]
+    send[:rows, :] = b[rows:, :].astype(bf16)
     total = in_pairs(sums[...], *(read_sums(r[group:, :]) for r in (b1, b2, b3)))
     sum_out[...] = total
     send[rows:, :] = pieces_of(total, send.shape[1])
 
 
-def final_body(keep, came, sums, sign, diag_query, diag_key, mean_out, *, count):
-    rows, feat = diag_query.shape
-    diag_query[...] = sign[...] * (keep[:, :feat] + came[:rows, :feat].astype(f32))
-    diag_key[...] = sign[...] * (keep[:, feat:] + came[:rows, feat:].astype(f32))
+def final_a_body(keep, came, sign, diag_query, more_out):
+    feat = diag_query.shape[1]
+    more = more_out.shape[1]
+    a = keep[...] + came[...].astype(f32)
+    diag_query[...] = sign[...] * a[:, :feat]
+    more_out[...] = sign[:, :more] * a[:, feat:]
+
+
+def final_b_body(more_in, keep, came, sums, sign, diag_key, mean_out, *, count):
+    rows = diag_key.shape[0]
+    more = more_in.shape[1]
+    diag_key[:, :more] = more_in[...]
+    diag_key[:, more:] = sign[:, more:] * (keep[...] + came[:rows, :].astype(f32))
     total = sums[...] + read_sums(came[rows:, :])
     lane = lax.broadcasted_iota(i32, (1, total.shape[1]), 1)
     for i in range(2):
@@ -445,14 +463,14 @@
     small = 2 * length * length * HEAD_DIM * heads
     weight = pltpu.VMEM((width, feat), bf16)
 
-    normed, q, k, v, p, send, own = call(
+    normed, q, k, v, p, send, attended, w_out = call(
         forward_body,
-        (shape((length, width), bf16), mat, mat, mat, square, half16, half32),
+        (shape((length, width), bf16), mat, mat, mat, square, half16, mat, shape((feat, width), bf16)),
         [HBM] * 8,
         [
             pltpu.VMEM((length, width), bf16), pltpu.VMEM((1, width), f32), weight, weight,
             pltpu.VMEM((2 * length, HEAD_DIM), f32), pltpu.VMEM((1, length), i32),
-            weight, pltpu.VMEM((feat, width), bf16), pltpu.SemaphoreType.DMA((8,)),
+            weight, pltpu.SemaphoreType.DMA((8,)),
         ],
         4 * product + 4 * small, 12 * MIB, 32,
     )(*map(in_hbm, (tokens, norm_gain[None, :], w_query, w_key, table, segments, w_value, w_out)))
@@ -467,6 +485,7 @@
         [pltpu.VMEM((width, length), bf16)],
         0, 3 * MIB, 16,
     )(normed, probe_model)
+    own = call(out_own_body, half32, [VMEM] * 2, (), product // 2, 2 * MIB, 16)(attended, w_out)
     near = (own + came.astype(f32)).astype(bf16)
     there = flip(near, far)
 
@@ -501,6 +520,9 @@
 
     d_res_own = call(d_residual_body, half16, [VMEM] * 3, (), 0, 2 * MIB, 16, (hq,))(d_near, d_there, row_weight)
     d_res_mate = flip(d_res_own, mate)
+    back_own = call(
+        back_own_body, shape((length, feat), f32), [VMEM] * 2, (), product // 2, 2 * MIB, 16
+    )(d_res_own, w_out)
     cut = 5 * feat // 4
     rest = 2 * feat - cut
     small_sums = shape((16, HEAD_DIM), f32)
@@ -509,7 +531,7 @@
         (shape((length, cut), bf16), shape((length, rest), bf16), small_sums),
         [VMEM] * 12,
         (), product + 3 * small, 6 * MIB, 24,
-    )(d_res_own, d_res_mate, w_out, q, k, v, p, hq, hk, r, head_bits, table)
+    )(back_own, d_res_mate, w_out, q, k, v, p, hq, hk, r, head_bits, table)
     ya_in = [ya] + [flip(ya, where) for where in along_z]
     sums = sums + flip(sums, mate)
     yb, sums = call(stamp_body, (shape((length + 16, rest), bf16), small_sums), [VMEM] * 3, (), 0, MIB, 16)(
@@ -534,18 +556,27 @@
     )(*xk, *yb_in, sums)
     a_in = [flip(part, where) for part, where in zip(a[1:], along_x)]
     b_in = [flip(part, where) for part, where in zip(b[1:], along_z)]
-    keep, send, sums = call(
-        middle_body,
-        (shape((rows, 2 * feat), f32), shape((rows + 16, 2 * feat), bf16), small_sums),
-        [VMEM] * 9,
-        (), 0, 3 * MIB, 24,
-    )(a[0], *a_in, b[0], *b_in, sums)
-    diag_query, diag_key, mean = call(
-        functools.partial(final_body, count=groups * entries),
-        (shape((rows, feat), f32), shape((rows, feat), f32), shape((2,), f32)),
-        [VMEM] * 4,
+    keep_a, send_a = call(
+        middle_a_body, (shape((rows, cut), f32), shape((rows, cut), bf16)), [VMEM] * 4, (), 0, MIB, 16
+    )(a[0], *a_in)
+    keep_b, send_b, sums = call(
+        middle_b_body,
+        (shape((rows, rest), f32), shape((rows + 16, rest), bf16), small_sums),
+        [VMEM] * 5,
         (), 0, MIB, 16,
-    )(keep, flip(send, [xor("yl", 1)]), sums, sign)
+    )(b[0], *b_in, sums)
+    side = [xor("yl", 1)]
+    block = shape((rows, feat), f32)
+    came_a, came_b = flip(send_a, side), flip(send_b, side)
+    diag_query, more = call(
+        final_a_body, (block, shape((rows, cut - feat), f32)), [VMEM] * 3, (), 0, MIB, 16
+    )(keep_a, came_a, sign)
+    diag_key, mean = call(
+        functools.partial(final_b_body, count=groups * entries),
+        (block, shape((2,), f32)),
+        [VMEM] * 5,
+        (), 0, MIB, 16,
+    )(more, keep_b, came_b, sums, sign)
     return diag_query, diag_key, mean
 
 

time: 115 us -> 116 us (level); the launches traced: 115 us -> 114 us
  waiting for transfers between devices: 47.7 us -> 41.2 us
  starting transfers between devices: 45.4 us -> 50.1 us
    ppermute x27 -> x28, waiting for transfers between devices: 47.7 us -> 41.2 us  [flip(): lax.ppermute(value, axes if len(axes) > 1 else axes[0], [(i, target(i)) f...]
    ppermute x27 -> x28, starting transfers between devices: 45.4 us -> 50.1 us  [flip(): lax.ppermute(value, axes if len(axes) > 1 else axes[0], [(i, target(i)) f...]
    pallas_call x13 -> x17, Pallas kernels: 20.2 us -> 21.2 us  [run(): return kernel(*args, *after)]
  transfers between devices with their start and end apart: 27 -> 28, of which waited for: 11 -> 10; matrix products, arithmetic and copies ran while one was open for 0% -> 0% of each run, Pallas kernels for 7% -> 8%
where the time goes in v3:
time: 116 us; the launch traced here: 114 us
  starting transfers between devices  50.1 us (43%)
  waiting for transfers between devices  41.2 us (36%)
  Pallas kernels  21.2 us (18%)
    ppermute x28, starting transfers between devices, flip(): lax.ppermute(value, axes if len(axes) > 1 else axes[0], [(i, target(i)) f...  50.1 us
    ppermute x28, waiting for transfers between devices, flip(): lax.ppermute(value, axes if len(axes) > 1 else axes[0], [(i, target(i)) f...  41.2 us
    pallas_call x17, Pallas kernels, run(): return kernel(*args, *after)  21.2 us
  transfers between devices with their start and end apart: 28, of which 10 were waited for; matrix products, arithmetic and copies ran while one was open for 0% of the time, Pallas kernels for 8%

profile of v3, /device:TPU:0, one launch (start us, length us, event | category | flops | bytes accessed | tf_op | source)
XLA Modules:
  0.0 113.9 jit_solution(14089267133950945160)
XLA Ops:
  0.6 6.5 %shard_map.139 = (bf16[256,2048]{1,0:T(8,128)(2,1)S(1)}, bf16[256,512]{1,0:T(8,128)(2,1)S(1)}, bf16[256,512]{1,0:T(8,128)(2,1)S(1)}, bf16[256,512]{1,0:T(8,128)(...) custom-call(bf16[256,2048]{1,0:T(8,128)(2,1)} %refs_0_.3, ...), custom_call_target="tpu_custom_call" | custom-call | flops 2415919104 | bytes 12582912 | tf_op jit(solution)/shard_map/pallas_call | solution.py:48
  8.2 0.9 collective-permute-done.3
  9.3 4.5 %shard_map.142 = (bf16[256,512]{1,0:T(8,128)(2,1)S(1)}, bf16[256,512]{1,0:T(8,128)(2,1)S(1)}, f32[256,512]{1,0:T(8,128)S(1)}, f32[4,256,256]{2,1,0:T(8,128)S(1)}...) custom-call(bf16[256,2048]{1,0:T(8,128)(2,1)S(1)} %get-tuple-element.53.refs_0_, s32[1,2048]{1,0:T(1,128)S(1)} %copy-done.3, ...), custom_call_target="tpu_custom_call" | custom-call | flops 1342177280 | bytes 8388608 | tf_op jit(solution)/shard_map/pallas_call | solution.py:48
  14.1 3.3 %collective-permute-start.6 = (bf16[256,1024]{1,0:T(8,128)(2,1)S(1)}, bf16[256,1024]{1,0:T(8,128)(2,1)S(1)}, u32[]{:S(2)}, u32[]{:S(2)}) collective-permute-start(bf16[256,1024]{1,0:T(8,128)(2,1)S(1)} %add_convert_fusion.1.refs_9_.refs_0_), channel_id=1, source_target_pairs={{0,2},{2,0},{1,3},{3,1},{4,6},{6,4},{5,7},{7,5},{8,10},{10,8},{9,1... | collective-permute-start | bytes 1572872 | tf_op jit(solution)/shard_map/ppermute | solution.py:439
  17.9 11.9 %collective-permute-done.6.refs_1_ = bf16[256,1024]{1,0:T(8,128)(2,1)S(1)} collective-permute-done((bf16[256,1024]{1,0:T(8,128)(2,1)S(1)}, bf16[256,1024]{1,0:T(8,128)(2,1)S(1)}, u32[]{:S(2)}, u32[]{:S(2)}) %collective-permute-start.6) | collective-permute-done | bytes 524320 | tf_op jit(solution)/shard_map/ppermute | solution.py:439
  30.2 3.3 %collective-permute-start.5 = (bf16[256,1024]{1,0:T(8,128)(2,1)S(1)}, bf16[256,1024]{1,0:T(8,128)(2,1)S(1)}, u32[]{:S(2)}, u32[]{:S(2)}) collective-permute-start(bf16[256,1024]{1,0:T(8,128)(2,1)S(1)} %add_convert_fusion.refs_4_.refs_0_), channel_id=1, source_target_pairs={{0,2},{2,0},{1,3},{3,1},{4,6},{6,4},{5,7},{7,5},{8,10},{10,8},{9,1... | collective-permute-start | bytes 1572872 | tf_op jit(solution)/shard_map/ppermute | solution.py:439
  33.5 2.8 %shard_map.145 = (f32[256,512]{1,0:T(8,128)S(1)}, f32[256,512]{1,0:T(8,128)S(1)}) custom-call(bf16[256,1024]{1,0:T(8,128)(2,1)S(1)} %shard_map.144.refs_0_, bf16[256,1024]{1,0:T(8,128)(2,1)S(1)} %collective-permute-done.7.refs_1_, bf16[512,2048]{1,0:T(8,128)(2,1)S(1)} %get-tuple-element.62.refs_1_.refs_8_.refs_2_, ...), custom_call_target="tpu_custom_call" | custom-call | flops 872415232 | bytes 6291456 | tf_op jit(solution)/shard_map/pallas_call | solution.py:48
  36.3 9.7 %collective-permute-done.5.refs_1_ = bf16[256,1024]{1,0:T(8,128)(2,1)S(1)} collective-permute-done((bf16[256,1024]{1,0:T(8,128)(2,1)S(1)}, bf16[256,1024]{1,0:T(8,128)(2,1)S(1)}, u32[]{:S(2)}, u32[]{:S(2)}) %collective-permute-start.5) | collective-permute-done | bytes 524320 | tf_op jit(solution)/shard_map/ppermute | solution.py:439
  46.2 1.6 %collective-permute-start.16 = (bf16[512,256]{1,0:T(8,128)(2,1)S(1)}, bf16[512,256]{1,0:T(8,128)(2,1)S(1)}, u32[]{:S(2)}, u32[]{:S(2)}) collective-permute-start(bf16[512,256]{1,0:T(8,128)(2,1)S(1)} %get-tuple-element.86), channel_id=1, source_target_pairs={{0,32},{32,64},{64,96},{96,0},{1,33},{33,65},{65,97},{97,1},{2,34}... | collective-permute-start | bytes 786440 | tf_op jit(solution)/shard_map/ppermute | solution.py:439
  47.9 1.9 %collective-permute-start = (bf16[512,256]{1,0:T(8,128)(2,1)S(1)}, bf16[512,256]{1,0:T(8,128)(2,1)S(1)}, u32[]{:S(2)}, u32[]{:S(2)}) collective-permute-start(bf16[512,256]{1,0:T(8,128)(2,1)S(1)} %get-tuple-element.55), channel_id=1, source_target_pairs={{0,8},{8,16},{16,24},{24,0},{1,9},{9,17},{17,25},{25,1},{2,10},{10... | collective-permute-start | bytes 786440 | tf_op jit(solution)/shard_map/ppermute | solution.py:439
  49.8 3.6 %collective-permute-start.1 = (bf16[512,256]{1,0:T(8,128)(2,1)S(1)}, bf16[512,256]{1,0:T(8,128)(2,1)S(1)}, u32[]{:S(2)}, u32[]{:S(2)}) collective-permute-start(bf16[512,256]{1,0:T(8,128)(2,1)S(1)} %get-tuple-element.56), channel_id=1, source_target_pairs={{0,16},{8,24},{16,0},{24,8},{1,17},{9,25},{17,1},{25,9},{2,18},{10... | collective-permute-start | bytes 786440 | tf_op jit(solution)/shard_map/ppermute | solution.py:439
  53.9 2.0 %shard_map.148 = (bf16[256,640]{1,0:T(8,128)(2,1)S(1)}, bf16[256,384]{1,0:T(8,128)(2,1)S(1)}, f32[16,128]{1,0:T(8,128)S(1)}) custom-call(f32[256,512]{1,0:T(8,128)S(1)} %shard_map.147.refs_0_, bf16[256,1024]{1,0:T(8,128)(2,1)S(1)} %collective-permute-done.8.refs_1_, bf16[512,2048]{1,0:T(8,128)(2,1)S(1)} %get-tuple-element.62.refs_1_.refs_8_.refs_2_, ...), custom_call_target="tpu_custom_call" | custom-call | flops 738197504 | bytes 6291456 | tf_op jit(solution)/shard_map/pallas_call | solution.py:48
  55.9 2.1 %collective-permute-start.2 = (bf16[512,256]{1,0:T(8,128)(2,1)S(1)}, bf16[512,256]{1,0:T(8,128)(2,1)S(1)}, u32[]{:S(2)}, u32[]{:S(2)}) collective-permute-start(bf16[512,256]{1,0:T(8,128)(2,1)S(1)} %get-tuple-element.57), channel_id=1, source_target_pairs={{0,24},{8,0},{16,8},{24,16},{1,25},{9,1},{17,9},{25,17},{2,26},{10... | collective-permute-start | bytes 786440 | tf_op jit(solution)/shard_map/ppermute | solution.py:439
  57.9 2.3 %collective-permute-start.11 = (bf16[256,640]{1,0:T(8,128)(2,1)S(1)}, bf16[256,640]{1,0:T(8,128)(2,1)S(1)}, u32[]{:S(2)}, u32[]{:S(2)}) collective-permute-start(bf16[256,640]{1,0:T(8,128)(2,1)S(1)} %get-tuple-element.75.refs_4_), channel_id=1, source_target_pairs={{0,24},{8,0},{16,8},{24,16},{1,25},{9,1},{17,9},{25,17},{2,26},{10... | collective-permute-start | bytes 983048 | tf_op jit(solution)/shard_map/ppermute | solution.py:439
  60.3 9.7 %collective-permute-start.9 = (bf16[256,640]{1,0:T(8,128)(2,1)S(1)}, bf16[256,640]{1,0:T(8,128)(2,1)S(1)}, u32[]{:S(2)}, u32[]{:S(2)}) collective-permute-start(bf16[256,640]{1,0:T(8,128)(2,1)S(1)} %get-tuple-element.75.refs_4_), channel_id=1, source_target_pairs={{0,8},{8,16},{16,24},{24,0},{1,9},{9,17},{17,25},{25,1},{2,10},{10... | collective-permute-start | bytes 983048 | tf_op jit(solution)/shard_map/ppermute | solution.py:439
  70.0 1.2 %collective-permute-done.19 = f32[16,128]{1,0:T(8,128)S(1)} collective-permute-done((f32[16,128]{1,0:T(8,128)S(1)}, f32[16,128]{1,0:T(8,128)S(1)}, u32[]{:S(2)}, u32[]{:S(2)}) %collective-permute-start.19) | collective-permute-done | bytes 8224 | tf_op jit(solution)/shard_map/ppermute | solution.py:439
  71.2 2.7 %collective-permute-start.17 = (bf16[512,256]{1,0:T(8,128)(2,1)S(1)}, bf16[512,256]{1,0:T(8,128)(2,1)S(1)}, u32[]{:S(2)}, u32[]{:S(2)}) collective-permute-start(bf16[512,256]{1,0:T(8,128)(2,1)S(1)} %get-tuple-element.87), channel_id=1, source_target_pairs={{0,64},{32,96},{64,0},{96,32},{1,65},{33,97},{65,1},{97,33},{2,66}... | collective-permute-start | bytes 786440 | tf_op jit(solution)/shard_map/ppermute | solution.py:439
  73.9 3.3 %collective-permute-start.20 = (f32[16,128]{1,0:T(8,128)S(1)}, f32[16,128]{1,0:T(8,128)S(1)}, u32[]{:S(2)}, u32[]{:S(2)}) collective-permute-start(f32[16,128]{1,0:T(8,128)S(1)} %add.11.refs_1_), channel_id=1, source_target_pairs={{0,2},{2,0},{1,3},{3,1},{4,6},{6,4},{5,7},{7,5},{8,10},{10,8},{9,1... | collective-permute-start | bytes 24584 | tf_op jit(solution)/shard_map/ppermute | solution.py:439
  77.2 1.9 %collective-permute-done.20.refs_2_ = f32[16,128]{1,0:T(8,128)S(1)} collective-permute-done((f32[16,128]{1,0:T(8,128)S(1)}, f32[16,128]{1,0:T(8,128)S(1)}, u32[]{:S(2)}, u32[]{:S(2)}) %collective-permute-start.20) | collective-permute-done | bytes 8224 | tf_op jit(solution)/shard_map/ppermute | solution.py:439
  79.1 1.5 %collective-permute-start.18 = (bf16[512,256]{1,0:T(8,128)(2,1)S(1)}, bf16[512,256]{1,0:T(8,128)(2,1)S(1)}, u32[]{:S(2)}, u32[]{:S(2)}) collective-permute-start(bf16[512,256]{1,0:T(8,128)(2,1)S(1)} %get-tuple-element.88), channel_id=1, source_target_pairs={{0,96},{32,0},{64,32},{96,64},{1,97},{33,1},{65,33},{97,65},{2,98}... | collective-permute-start | bytes 786440 | tf_op jit(solution)/shard_map/ppermute | solution.py:439
  81.2 1.4 %collective-permute-start.22 = (bf16[272,384]{1,0:T(8,128)(2,1)S(1)}, bf16[272,384]{1,0:T(8,128)(2,1)S(1)}, u32[]{:S(2)}, u32[]{:S(2)}) collective-permute-start(bf16[272,384]{1,0:T(8,128)(2,1)S(1)} %get-tuple-element.91.refs_4_), channel_id=1, source_target_pairs={{0,64},{32,96},{64,0},{96,32},{1,65},{33,97},{65,1},{97,33},{2,66}... | collective-permute-start | bytes 626696 | tf_op jit(solution)/shard_map/ppermute | solution.py:439
  82.6 1.4 %collective-permute-start.23 = (bf16[272,384]{1,0:T(8,128)(2,1)S(1)}, bf16[272,384]{1,0:T(8,128)(2,1)S(1)}, u32[]{:S(2)}, u32[]{:S(2)}) collective-permute-start(bf16[272,384]{1,0:T(8,128)(2,1)S(1)} %get-tuple-element.91.refs_4_), channel_id=1, source_target_pairs={{0,96},{32,0},{64,32},{96,64},{1,97},{33,1},{65,33},{97,65},{2,98}... | collective-permute-start | bytes 626696 | tf_op jit(solution)/shard_map/ppermute | solution.py:439
  84.1 1.0 shard_map.149
  85.9 5.4 %collective-permute-done.18.refs_3_ = bf16[512,256]{1,0:T(8,128)(2,1)S(1)} collective-permute-done((bf16[512,256]{1,0:T(8,128)(2,1)S(1)}, bf16[512,256]{1,0:T(8,128)(2,1)S(1)}, u32[]{:S(2)}, u32[]{:S(2)}) %collective-permute-start.18) | collective-permute-done | bytes 262176 | tf_op jit(solution)/shard_map/ppermute | solution.py:439
  91.9 3.4 %collective-permute-done.21.refs_5_ = bf16[272,384]{1,0:T(8,128)(2,1)S(1)} collective-permute-done((bf16[272,384]{1,0:T(8,128)(2,1)S(1)}, bf16[272,384]{1,0:T(8,128)(2,1)S(1)}, u32[]{:S(2)}, u32[]{:S(2)}) %collective-permute-start.21) | collective-permute-done | bytes 208928 | tf_op jit(solution)/shard_map/ppermute | solution.py:439
  95.5 3.1 %collective-permute-done.23.refs_7_ = bf16[272,384]{1,0:T(8,128)(2,1)S(1)} collective-permute-done((bf16[272,384]{1,0:T(8,128)(2,1)S(1)}, bf16[272,384]{1,0:T(8,128)(2,1)S(1)}, u32[]{:S(2)}, u32[]{:S(2)}) %collective-permute-start.23) | collective-permute-done | bytes 208928 | tf_op jit(solution)/shard_map/ppermute | solution.py:439
  99.4 3.0 %collective-permute-start.24 = (bf16[144,384]{1,0:T(8,128)(2,1)S(1)}, bf16[144,384]{1,0:T(8,128)(2,1)S(1)}, u32[]{:S(2)}, u32[]{:S(2)}) collective-permute-start(bf16[144,384]{1,0:T(8,128)(2,1)S(1)} %get-tuple-element.94), channel_id=1, source_target_pairs={{0,8},{8,16},{16,24},{24,0},{1,9},{9,17},{17,25},{25,1},{2,10},{10... | collective-permute-start | bytes 331784 | tf_op jit(solution)/shard_map/ppermute | solution.py:439
  102.5 2.6 %collective-permute-start.26 = (bf16[144,384]{1,0:T(8,128)(2,1)S(1)}, bf16[144,384]{1,0:T(8,128)(2,1)S(1)}, u32[]{:S(2)}, u32[]{:S(2)}) collective-permute-start(bf16[144,384]{1,0:T(8,128)(2,1)S(1)} %get-tuple-element.96), channel_id=1, source_target_pairs={{0,24},{8,0},{16,8},{24,16},{1,25},{9,1},{17,9},{25,17},{2,26},{10... | collective-permute-start | bytes 331784 | tf_op jit(solution)/shard_map/ppermute | solution.py:439
  105.3 1.7 %collective-permute-start.15 = (bf16[64,640]{1,0:T(8,128)(2,1)S(1)}, bf16[64,640]{1,0:T(8,128)(2,1)S(1)}, u32[]{:S(2)}, u32[]{:S(2)}) collective-permute-start(bf16[64,640]{1,0:T(8,128)(2,1)S(1)} %get-tuple-element.81), channel_id=1, source_target_pairs={{0,4},{4,0},{1,5},{5,1},{2,6},{6,2},{3,7},{7,3},{8,12},{12,8},{9,1... | collective-permute-start | bytes 245768 | tf_op jit(solution)/shard_map/ppermute | solution.py:439
  106.9 1.7 %collective-permute-done.25.refs_2_ = bf16[144,384]{1,0:T(8,128)(2,1)S(1)} collective-permute-done((bf16[144,384]{1,0:T(8,128)(2,1)S(1)}, bf16[144,384]{1,0:T(8,128)(2,1)S(1)}, u32[]{:S(2)}, u32[]{:S(2)}) %collective-permute-start.25) | collective-permute-done | bytes 110624 | tf_op jit(solution)/shard_map/ppermute | solution.py:439
  108.7 1.7 %collective-permute-start.27 = (bf16[80,384]{1,0:T(8,128)(2,1)S(1)}, bf16[80,384]{1,0:T(8,128)(2,1)S(1)}, u32[]{:S(2)}, u32[]{:S(2)}) collective-permute-start(bf16[80,384]{1,0:T(8,128)(2,1)S(1)} %get-tuple-element.99), channel_id=1, source_target_pairs={{0,4},{4,0},{1,5},{5,1},{2,6},{6,2},{3,7},{7,3},{8,12},{12,8},{9,1... | collective-permute-start | bytes 184328 | tf_op jit(solution)/shard_map/ppermute | solution.py:439
  111.1 1.9 %collective-permute-done.27.refs_2_ = bf16[80,384]{1,0:T(8,128)(2,1)S(1)} collective-permute-done((bf16[80,384]{1,0:T(8,128)(2,1)S(1)}, bf16[80,384]{1,0:T(8,128)(2,1)S(1)}, u32[]{:S(2)}, u32[]{:S(2)}) %collective-permute-start.27) | collective-permute-done | bytes 61472 | tf_op jit(solution)/shard_map/ppermute | solution.py:439
  (56 shorter events, 7.6 us)
Async XLA Ops:
  0.6 6.6 %copy-start.3 = (s32[1,2048]{1,0:T(1,128)S(1)}, s32[1,2048]{1,0:T(1,128)}, u32[]{:S(2)}) copy-start(s32[1,2048]{1,0:T(1,128)} %refs_1_.4) | copy-start | bytes 24580
  7.1 2.0 %collective-permute-start.3 = (bf16[256,1024]{1,0:T(8,128)(2,1)S(1)}, bf16[256,1024]{1,0:T(8,128)(2,1)S(1)}, u32[]{:S(2)}, u32[]{:S(2)}) collective-permute-start(bf16[256,1024]{1,0:T(8,128)(2,1)S(1)} %get-tuple-element.64), channel_id=1, source_target_pairs={{0,1},{1,0},{2,3},{3,2},{4,5},{5,4},{6,7},{7,6},{8,9},{9,8},{10,11... | collective-permute-start | bytes 1572872 | tf_op jit(solution)/shard_map/ppermute | solution.py:439
  9.3 8.1 %copy-start = (bf16[256,2048]{1,0:T(8,128)(2,1)S(1)}, bf16[256,2048]{1,0:T(8,128)(2,1)}, u32[]{:S(2)}) copy-start(bf16[256,2048]{1,0:T(8,128)(2,1)} %refs_0_.3) | copy-start | bytes 3145732
  9.3 8.1 %copy-start.2 = (bf16[256,2048]{1,0:T(8,128)(2,1)S(1)}, bf16[256,2048]{1,0:T(8,128)(2,1)}, u32[]{:S(2)}) copy-start(bf16[256,2048]{1,0:T(8,128)(2,1)} %refs_1_.5) | copy-start | bytes 3145732
  9.3 8.1 %copy-start.5 = (f32[256]{0:T(256)S(1)}, f32[256]{0:T(256)}, u32[]{:S(2)}) copy-start(f32[256]{0:T(256)} %param.14) | copy-start | bytes 3076
  13.9 3.9 %collective-permute-start.4 = (bf16[256,1024]{1,0:T(8,128)(2,1)S(1)}, bf16[256,1024]{1,0:T(8,128)(2,1)S(1)}, u32[]{:S(2)}, u32[]{:S(2)}) collective-permute-start(bf16[256,1024]{1,0:T(8,128)(2,1)S(1)} %get-tuple-element.66), channel_id=1, source_target_pairs={{0,1},{1,0},{2,3},{3,2},{4,5},{5,4},{6,7},{7,6},{8,9},{9,8},{10,11... | collective-permute-start | bytes 1572872 | tf_op jit(solution)/shard_map/ppermute | solution.py:439
  14.1 15.8 %collective-permute-start.6 = (bf16[256,1024]{1,0:T(8,128)(2,1)S(1)}, bf16[256,1024]{1,0:T(8,128)(2,1)S(1)}, u32[]{:S(2)}, u32[]{:S(2)}) collective-permute-start(bf16[256,1024]{1,0:T(8,128)(2,1)S(1)} %add_convert_fusion.1.refs_9_.refs_0_), channel_id=1, source_target_pairs={{0,2},{2,0},{1,3},{3,1},{4,6},{6,4},{5,7},{7,5},{8,10},{10,8},{9,1... | collective-permute-start | bytes 1572872 | tf_op jit(solution)/shard_map/ppermute | solution.py:439
  30.1 3.4 %collective-permute-start.7 = (bf16[256,1024]{1,0:T(8,128)(2,1)S(1)}, bf16[256,1024]{1,0:T(8,128)(2,1)S(1)}, u32[]{:S(2)}, u32[]{:S(2)}) collective-permute-start(bf16[256,1024]{1,0:T(8,128)(2,1)S(1)} %shard_map.144.refs_0_), channel_id=1, source_target_pairs={{0,1},{1,0},{2,3},{3,2},{4,5},{5,4},{6,7},{7,6},{8,9},{9,8},{10,11... | collective-permute-start | bytes 1572872 | tf_op jit(solution)/shard_map/ppermute | solution.py:439
  30.2 15.8 %collective-permute-start.5 = (bf16[256,1024]{1,0:T(8,128)(2,1)S(1)}, bf16[256,1024]{1,0:T(8,128)(2,1)S(1)}, u32[]{:S(2)}, u32[]{:S(2)}) collective-permute-start(bf16[256,1024]{1,0:T(8,128)(2,1)S(1)} %add_convert_fusion.refs_4_.refs_0_), channel_id=1, source_target_pairs={{0,2},{2,0},{1,3},{3,1},{4,6},{6,4},{5,7},{7,5},{8,10},{10,8},{9,1... | collective-permute-start | bytes 1572872 | tf_op jit(solution)/shard_map/ppermute | solution.py:439
  46.2 7.7 %collective-permute-start.8 = (bf16[256,1024]{1,0:T(8,128)(2,1)S(1)}, bf16[256,1024]{1,0:T(8,128)(2,1)S(1)}, u32[]{:S(2)}, u32[]{:S(2)}) collective-permute-start(bf16[256,1024]{1,0:T(8,128)(2,1)S(1)} %shard_map.146.refs_0_), channel_id=1, source_target_pairs={{0,1},{1,0},{2,3},{3,2},{4,5},{5,4},{6,7},{7,6},{8,9},{9,8},{10,11... | collective-permute-start | bytes 1572872 | tf_op jit(solution)/shard_map/ppermute | solution.py:439
  46.2 11.7 %collective-permute-start.16 = (bf16[512,256]{1,0:T(8,128)(2,1)S(1)}, bf16[512,256]{1,0:T(8,128)(2,1)S(1)}, u32[]{:S(2)}, u32[]{:S(2)}) collective-permute-start(bf16[512,256]{1,0:T(8,128)(2,1)S(1)} %get-tuple-element.86), channel_id=1, source_target_pairs={{0,32},{32,64},{64,96},{96,0},{1,33},{33,65},{65,97},{97,1},{2,34}... | collective-permute-start | bytes 786440 | tf_op jit(solution)/shard_map/ppermute | solution.py:439
  47.9 12.4 %collective-permute-start = (bf16[512,256]{1,0:T(8,128)(2,1)S(1)}, bf16[512,256]{1,0:T(8,128)(2,1)S(1)}, u32[]{:S(2)}, u32[]{:S(2)}) collective-permute-start(bf16[512,256]{1,0:T(8,128)(2,1)S(1)} %get-tuple-element.55), channel_id=1, source_target_pairs={{0,8},{8,16},{16,24},{24,0},{1,9},{9,17},{17,25},{25,1},{2,10},{10... | collective-permute-start | bytes 786440 | tf_op jit(solution)/shard_map/ppermute | solution.py:439
  49.8 20.2 %collective-permute-start.1 = (bf16[512,256]{1,0:T(8,128)(2,1)S(1)}, bf16[512,256]{1,0:T(8,128)(2,1)S(1)}, u32[]{:S(2)}, u32[]{:S(2)}) collective-permute-start(bf16[512,256]{1,0:T(8,128)(2,1)S(1)} %get-tuple-element.56), channel_id=1, source_target_pairs={{0,16},{8,24},{16,0},{24,8},{1,17},{9,25},{17,1},{25,9},{2,18},{10... | collective-permute-start | bytes 786440 | tf_op jit(solution)/shard_map/ppermute | solution.py:439
  55.8 24.8 %collective-permute-start.10 = (bf16[256,640]{1,0:T(8,128)(2,1)S(1)}, bf16[256,640]{1,0:T(8,128)(2,1)S(1)}, u32[]{:S(2)}, u32[]{:S(2)}) collective-permute-start(bf16[256,640]{1,0:T(8,128)(2,1)S(1)} %get-tuple-element.75.refs_4_), channel_id=1, source_target_pairs={{0,16},{8,24},{16,0},{24,8},{1,17},{9,25},{17,1},{25,9},{2,18},{10... | collective-permute-start | bytes 983048 | tf_op jit(solution)/shard_map/ppermute | solution.py:439
  55.9 18.0 %collective-permute-start.2 = (bf16[512,256]{1,0:T(8,128)(2,1)S(1)}, bf16[512,256]{1,0:T(8,128)(2,1)S(1)}, u32[]{:S(2)}, u32[]{:S(2)}) collective-permute-start(bf16[512,256]{1,0:T(8,128)(2,1)S(1)} %get-tuple-element.57), channel_id=1, source_target_pairs={{0,24},{8,0},{16,8},{24,16},{1,25},{9,1},{17,9},{25,17},{2,26},{10... | collective-permute-start | bytes 786440 | tf_op jit(solution)/shard_map/ppermute | solution.py:439
  57.9 23.3 %collective-permute-start.11 = (bf16[256,640]{1,0:T(8,128)(2,1)S(1)}, bf16[256,640]{1,0:T(8,128)(2,1)S(1)}, u32[]{:S(2)}, u32[]{:S(2)}) collective-permute-start(bf16[256,640]{1,0:T(8,128)(2,1)S(1)} %get-tuple-element.75.refs_4_), channel_id=1, source_target_pairs={{0,24},{8,0},{16,8},{24,16},{1,25},{9,1},{17,9},{25,17},{2,26},{10... | collective-permute-start | bytes 983048 | tf_op jit(solution)/shard_map/ppermute | solution.py:439
  60.3 22.3 %collective-permute-start.9 = (bf16[256,640]{1,0:T(8,128)(2,1)S(1)}, bf16[256,640]{1,0:T(8,128)(2,1)S(1)}, u32[]{:S(2)}, u32[]{:S(2)}) collective-permute-start(bf16[256,640]{1,0:T(8,128)(2,1)S(1)} %get-tuple-element.75.refs_4_), channel_id=1, source_target_pairs={{0,8},{8,16},{16,24},{24,0},{1,9},{9,17},{17,25},{25,1},{2,10},{10... | collective-permute-start | bytes 983048 | tf_op jit(solution)/shard_map/ppermute | solution.py:439
  70.0 1.2 %collective-permute-start.19 = (f32[16,128]{1,0:T(8,128)S(1)}, f32[16,128]{1,0:T(8,128)S(1)}, u32[]{:S(2)}, u32[]{:S(2)}) collective-permute-start(f32[16,128]{1,0:T(8,128)S(1)} %get-tuple-element.90), channel_id=1, source_target_pairs={{0,1},{1,0},{2,3},{3,2},{4,5},{5,4},{6,7},{7,6},{8,9},{9,8},{10,11... | collective-permute-start | bytes 24584 | tf_op jit(solution)/shard_map/ppermute | solution.py:439
  71.2 13.9 %collective-permute-start.17 = (bf16[512,256]{1,0:T(8,128)(2,1)S(1)}, bf16[512,256]{1,0:T(8,128)(2,1)S(1)}, u32[]{:S(2)}, u32[]{:S(2)}) collective-permute-start(bf16[512,256]{1,0:T(8,128)(2,1)S(1)} %get-tuple-element.87), channel_id=1, source_target_pairs={{0,64},{32,96},{64,0},{96,32},{1,65},{33,97},{65,1},{97,33},{2,66}... | collective-permute-start | bytes 786440 | tf_op jit(solution)/shard_map/ppermute | solution.py:439
  73.9 5.2 %collective-permute-start.20 = (f32[16,128]{1,0:T(8,128)S(1)}, f32[16,128]{1,0:T(8,128)S(1)}, u32[]{:S(2)}, u32[]{:S(2)}) collective-permute-start(f32[16,128]{1,0:T(8,128)S(1)} %add.11.refs_1_), channel_id=1, source_target_pairs={{0,2},{2,0},{1,3},{3,1},{4,6},{6,4},{5,7},{7,5},{8,10},{10,8},{9,1... | collective-permute-start | bytes 24584 | tf_op jit(solution)/shard_map/ppermute | solution.py:439
  79.1 12.2 %collective-permute-start.18 = (bf16[512,256]{1,0:T(8,128)(2,1)S(1)}, bf16[512,256]{1,0:T(8,128)(2,1)S(1)}, u32[]{:S(2)}, u32[]{:S(2)}) collective-permute-start(bf16[512,256]{1,0:T(8,128)(2,1)S(1)} %get-tuple-element.88), channel_id=1, source_target_pairs={{0,96},{32,0},{64,32},{96,64},{1,97},{33,1},{65,33},{97,65},{2,98}... | collective-permute-start | bytes 786440 | tf_op jit(solution)/shard_map/ppermute | solution.py:439
  80.6 14.7 %collective-permute-start.21 = (bf16[272,384]{1,0:T(8,128)(2,1)S(1)}, bf16[272,384]{1,0:T(8,128)(2,1)S(1)}, u32[]{:S(2)}, u32[]{:S(2)}) collective-permute-start(bf16[272,384]{1,0:T(8,128)(2,1)S(1)} %get-tuple-element.91.refs_4_), channel_id=1, source_target_pairs={{0,32},{32,64},{64,96},{96,0},{1,33},{33,65},{65,97},{97,1},{2,34}... | collective-permute-start | bytes 626696 | tf_op jit(solution)/shard_map/ppermute | solution.py:439
  81.2 14.3 %collective-permute-start.22 = (bf16[272,384]{1,0:T(8,128)(2,1)S(1)}, bf16[272,384]{1,0:T(8,128)(2,1)S(1)}, u32[]{:S(2)}, u32[]{:S(2)}) collective-permute-start(bf16[272,384]{1,0:T(8,128)(2,1)S(1)} %get-tuple-element.91.refs_4_), channel_id=1, source_target_pairs={{0,64},{32,96},{64,0},{96,32},{1,65},{33,97},{65,1},{97,33},{2,66}... | collective-permute-start | bytes 626696 | tf_op jit(solution)/shard_map/ppermute | solution.py:439
  82.6 16.0 %collective-permute-start.23 = (bf16[272,384]{1,0:T(8,128)(2,1)S(1)}, bf16[272,384]{1,0:T(8,128)(2,1)S(1)}, u32[]{:S(2)}, u32[]{:S(2)}) collective-permute-start(bf16[272,384]{1,0:T(8,128)(2,1)S(1)} %get-tuple-element.91.refs_4_), channel_id=1, source_target_pairs={{0,96},{32,0},{64,32},{96,64},{1,97},{33,1},{65,33},{97,65},{2,98}... | collective-permute-start | bytes 626696 | tf_op jit(solution)/shard_map/ppermute | solution.py:439
  85.1 17.5 %collective-permute-start.12 = (bf16[128,640]{1,0:T(8,128)(2,1)S(1)}, bf16[128,640]{1,0:T(8,128)(2,1)S(1)}, u32[]{:S(2)}, u32[]{:S(2)}) collective-permute-start(bf16[128,640]{1,0:T(8,128)(2,1)S(1)} %get-tuple-element.77), channel_id=1, source_target_pairs={{0,32},{32,64},{64,96},{96,0},{1,33},{33,65},{65,97},{97,1},{2,34}... | collective-permute-start | bytes 491528 | tf_op jit(solution)/shard_map/ppermute | solution.py:439
  91.3 13.9 %collective-permute-start.13 = (bf16[128,640]{1,0:T(8,128)(2,1)S(1)}, bf16[128,640]{1,0:T(8,128)(2,1)S(1)}, u32[]{:S(2)}, u32[]{:S(2)}) collective-permute-start(bf16[128,640]{1,0:T(8,128)(2,1)S(1)} %get-tuple-element.78), channel_id=1, source_target_pairs={{0,64},{32,96},{64,0},{96,32},{1,65},{33,97},{65,1},{97,33},{2,66}... | collective-permute-start | bytes 491528 | tf_op jit(solution)/shard_map/ppermute | solution.py:439
  95.3 9.8 %collective-permute-start.14 = (bf16[128,640]{1,0:T(8,128)(2,1)S(1)}, bf16[128,640]{1,0:T(8,128)(2,1)S(1)}, u32[]{:S(2)}, u32[]{:S(2)}) collective-permute-start(bf16[128,640]{1,0:T(8,128)(2,1)S(1)} %get-tuple-element.79), channel_id=1, source_target_pairs={{0,96},{32,0},{64,32},{96,64},{1,97},{33,1},{65,33},{97,65},{2,98}... | collective-permute-start | bytes 491528 | tf_op jit(solution)/shard_map/ppermute | solution.py:439
  99.4 7.6 %collective-permute-start.24 = (bf16[144,384]{1,0:T(8,128)(2,1)S(1)}, bf16[144,384]{1,0:T(8,128)(2,1)S(1)}, u32[]{:S(2)}, u32[]{:S(2)}) collective-permute-start(bf16[144,384]{1,0:T(8,128)(2,1)S(1)} %get-tuple-element.94), channel_id=1, source_target_pairs={{0,8},{8,16},{16,24},{24,0},{1,9},{9,17},{17,25},{25,1},{2,10},{10... | collective-permute-start | bytes 331784 | tf_op jit(solution)/shard_map/ppermute | solution.py:439
  102.4 6.3 %collective-permute-start.25 = (bf16[144,384]{1,0:T(8,128)(2,1)S(1)}, bf16[144,384]{1,0:T(8,128)(2,1)S(1)}, u32[]{:S(2)}, u32[]{:S(2)}) collective-permute-start(bf16[144,384]{1,0:T(8,128)(2,1)S(1)} %get-tuple-element.95), channel_id=1, source_target_pairs={{0,16},{8,24},{16,0},{24,8},{1,17},{9,25},{17,1},{25,9},{2,18},{10... | collective-permute-start | bytes 331784 | tf_op jit(solution)/shard_map/ppermute | solution.py:439
  102.5 6.1 %collective-permute-start.26 = (bf16[144,384]{1,0:T(8,128)(2,1)S(1)}, bf16[144,384]{1,0:T(8,128)(2,1)S(1)}, u32[]{:S(2)}, u32[]{:S(2)}) collective-permute-start(bf16[144,384]{1,0:T(8,128)(2,1)S(1)} %get-tuple-element.96), channel_id=1, source_target_pairs={{0,24},{8,0},{16,8},{24,16},{1,25},{9,1},{17,9},{25,17},{2,26},{10... | collective-permute-start | bytes 331784 | tf_op jit(solution)/shard_map/ppermute | solution.py:439
  105.3 5.2 %collective-permute-start.15 = (bf16[64,640]{1,0:T(8,128)(2,1)S(1)}, bf16[64,640]{1,0:T(8,128)(2,1)S(1)}, u32[]{:S(2)}, u32[]{:S(2)}) collective-permute-start(bf16[64,640]{1,0:T(8,128)(2,1)S(1)} %get-tuple-element.81), channel_id=1, source_target_pairs={{0,4},{4,0},{1,5},{5,1},{2,6},{6,2},{3,7},{7,3},{8,12},{12,8},{9,1... | collective-permute-start | bytes 245768 | tf_op jit(solution)/shard_map/ppermute | solution.py:439
  108.7 4.3 %collective-permute-start.27 = (bf16[80,384]{1,0:T(8,128)(2,1)S(1)}, bf16[80,384]{1,0:T(8,128)(2,1)S(1)}, u32[]{:S(2)}, u32[]{:S(2)}) collective-permute-start(bf16[80,384]{1,0:T(8,128)(2,1)S(1)} %get-tuple-element.99), channel_id=1, source_target_pairs={{0,4},{4,0},{1,5},{5,1},{2,6},{6,2},{3,7},{7,3},{8,12},{12,8},{9,1... | collective-permute-start | bytes 184328 | tf_op jit(solution)/shard_map/ppermute | solution.py:439
  (2 other events, 3.1 us)

commit v4 on v3

--- a/solution.py
+++ b/solution.py
@@ -371,16 +371,18 @@
 
 
 def estimate_b_body(*refs):
-    y_parts, sums, outs, sum_out = refs[4:8], refs[8], refs[9:13], refs[13]
+    y_parts, sums, keep, send, sum_out = refs[4:8], refs[8], refs[9], refs[10], refs[11]
     length = refs[0].shape[1]
-    group = outs[0].shape[0]
+    group = keep.shape[0]
+    rows = group // 4
     total = in_pairs(sums[...], *(read_sums(y[length:, :]) for y in y_parts[1:]))
     sum_out[...] = total
     whole = rows_times(refs[:4], y_parts)
-    for step, out in enumerate(outs):
-        out[:group, :] = whole[step * group : (step + 1) * group, :].astype(out.dtype)
-        if step > 0:
-            out[group:, :] = pieces_of(total, out.shape[1])
+    for step in range(4):
+        at = slice(step * rows, (step + 1) * rows)
+        keep[at, :] = whole[2 * step * rows : (2 * step + 1) * rows, :]
+        send[at, :] = whole[(2 * step + 1) * rows : (2 * step + 2) * rows, :].astype(bf16)
+    send[group:, :] = pieces_of(total, send.shape[1])
 
 
 def middle_a_body(a0, a1, a2, a3, keep, send):
@@ -390,34 +392,35 @@
     send[...] = a[rows:, :].astype(bf16)
 
 
-def middle_b_body(b0, b1, b2, b3, sums, keep, send, sum_out):
-    rows = keep.shape[0]
-    group = 2 * rows
-    b = b0[...] + sum(r[:group, :].astype(f32) for r in (b1, b2, b3))
-    keep[...] = b[:rows, :]
-    send[:rows, :] = b[rows:, :].astype(bf16)
-    total = in_pairs(sums[...], *(read_sums(r[group:, :]) for r in (b1, b2, b3)))
+def middle_b_body(keep, came, sums, b0, b1, b2, b3, sum_out):
+    group = keep.shape[0]
+    rows = group // 4
+    whole = keep[...] + came[:group, :].astype(f32)
+    total = sums[...] + read_sums(came[group:, :])
     sum_out[...] = total
-    send[rows:, :] = pieces_of(total, send.shape[1])
-
-
-def final_a_body(keep, came, sign, diag_query, more_out):
-    feat = diag_query.shape[1]
-    more = more_out.shape[1]
-    a = keep[...] + came[...].astype(f32)
-    diag_query[...] = sign[...] * a[:, :feat]
-    more_out[...] = sign[:, :more] * a[:, feat:]
-
-
-def final_b_body(more_in, keep, came, sums, sign, diag_key, mean_out, *, count):
-    rows = diag_key.shape[0]
-    more = more_in.shape[1]
-    diag_key[:, :more] = more_in[...]
-    diag_key[:, more:] = sign[:, more:] * (keep[...] + came[:rows, :].astype(f32))
-    total = sums[...] + read_sums(came[rows:, :])
+    b0[...] = whole[:rows, :]
+    for step, out in ((1, b1), (2, b2), (3, b3)):
+        out[:rows, :] = whole[step * rows : (step + 1) * rows, :].astype(bf16)
+        out[rows:, :] = pieces_of(total, out.shape[1])
+
+
+def final_b_body(b0, b1, b2, b3, sums, sign, tail, mean_out, *, count):
+    rows, rest = b0.shape
+    signs = sign[:, sign.shape[1] - rest :]
+    tail[...] = signs * (b0[...] + sum(r[:rows, :].astype(f32) for r in (b1, b2, b3)))
+    total = in_pairs(sums[...], *(read_sums(r[rows:, :]) for r in (b1, b2, b3)))
     lane = lax.broadcasted_iota(i32, (1, total.shape[1]), 1)
     for i in range(2):
         mean_out[i] = jnp.sum(jnp.where(lane == i, total[0:1, :], 0.0)) * (1.0 / count)
+
+
+def final_a_body(keep, came, sign, tail, diag_query, diag_key):
+    feat = diag_query.shape[1]
+    more = keep.shape[1] - feat
+    a = keep[...] + came[...].astype(f32)
+    diag_query[...] = sign[...] * a[:, :feat]
+    diag_key[:, :more] = sign[:, :more] * a[:, feat:]
+    diag_key[:, more:] = tail[...]
 
 
 def flip(value, moves):
@@ -547,36 +550,35 @@
         [VMEM] * 8,
         (), product, 3 * MIB, 24,
     )(*xq, *ya_in)
-    part, keep = shape((group + 16, rest), bf16), shape((group, rest), f32)
-    *b, sums = call(
+    side = [xor("yl", 1)]
+    keep_b, send_b, sums = call(
         estimate_b_body,
-        (keep, part, part, part, small_sums),
+        (shape((4 * rows, rest), f32), shape((4 * rows + 16, rest), bf16), small_sums),
         [VMEM] * 9,
         (), product, 3 * MIB, 24,
     )(*xk, *yb_in, sums)
+    came_b = flip(send_b, side)
     a_in = [flip(part, where) for part, where in zip(a[1:], along_x)]
+    part = shape((rows + 16, rest), bf16)
+    *b, sums = call(
+        middle_b_body,
+        (shape((rows, rest), f32), part, part, part, small_sums),
+        [VMEM] * 3,
+        (), 0, MIB, 16,
+    )(keep_b, came_b, sums)
     b_in = [flip(part, where) for part, where in zip(b[1:], along_z)]
     keep_a, send_a = call(
         middle_a_body, (shape((rows, cut), f32), shape((rows, cut), bf16)), [VMEM] * 4, (), 0, MIB, 16
     )(a[0], *a_in)
-    keep_b, send_b, sums = call(
-        middle_b_body,
-        (shape((rows, rest), f32), shape((rows + 16, rest), bf16), small_sums),
-        [VMEM] * 5,
+    came_a = flip(send_a, side)
+    tail, mean = call(
+        functools.partial(final_b_body, count=groups * entries),
+        (shape((rows, rest), f32), shape((2,), f32)),
+        [VMEM] * 6,
         (), 0, MIB, 16,
-    )(b[0], *b_in, sums)
-    side = [xor("yl", 1)]
+    )(b[0], *b_in, sums, sign)
     block = shape((rows, feat), f32)
-    came_a, came_b = flip(send_a, side), flip(send_b, side)
-    diag_query, more = call(
-        final_a_body, (block, shape((rows, cut - feat), f32)), [VMEM] * 3, (), 0, MIB, 16
-    )(keep_a, came_a, sign)
-    diag_key, mean = call(
-        functools.partial(final_b_body, count=groups * entries),
-        (block, shape((2,), f32)),
-        [VMEM] * 5,
-        (), 0, MIB, 16,
-    )(more, keep_b, came_b, sums, sign)
+    diag_query, diag_key = call(final_a_body, (block, block), [VMEM] * 4, (), 0, MIB, 16)(keep_a, came_a, sign, tail)
     return diag_query, diag_key, mean
 
 

time: 116 us -> 118 us (1.017); the launches traced: 114 us -> 118 us
  waiting for transfers between devices: 41.2 us -> 49.8 us
  starting transfers between devices: 50.1 us -> 45.7 us
    ppermute x28, waiting for transfers between devices: 41.2 us -> 49.8 us  [flip(): lax.ppermute(value, axes if len(axes) > 1 else axes[0], [(i, target(i)) f...]
    ppermute x28, starting transfers between devices: 50.1 us -> 45.7 us  [flip(): lax.ppermute(value, axes if len(axes) > 1 else axes[0], [(i, target(i)) f...]
  transfers between devices with their start and end apart: 28 -> 28, of which waited for: 10 -> 14; matrix products, arithmetic and copies ran while one was open for 0% -> 0% of each run, Pallas kernels for 8% -> 8%
where the time goes in v4:
time: 118 us
  waiting for transfers between devices  49.8 us (42%)
  starting transfers between devices  45.7 us (39%)
  Pallas kernels  21.2 us (18%)
    ppermute x28, waiting for transfers between devices, flip(): lax.ppermute(value, axes if len(axes) > 1 else axes[0], [(i, target(i)) f...  49.8 us
    ppermute x28, starting transfers between devices, flip(): lax.ppermute(value, axes if len(axes) > 1 else axes[0], [(i, target(i)) f...  45.7 us
    pallas_call x17, Pallas kernels, run(): return kernel(*args, *after)  21.2 us
  transfers between devices with their start and end apart: 28, of which 14 were waited for; matrix products, arithmetic and copies ran while one was open for 0% of the time, Pallas kernels for 8%

profile of v4, /device:TPU:0, one launch (start us, length us, event | category | flops | bytes accessed | tf_op | source)
XLA Modules:
  0.0 117.9 jit_solution(12216420840283205300)
XLA Ops:
  0.6 6.5 %shard_map.139 = (bf16[256,2048]{1,0:T(8,128)(2,1)S(1)}, bf16[256,512]{1,0:T(8,128)(2,1)S(1)}, bf16[256,512]{1,0:T(8,128)(2,1)S(1)}, bf16[256,512]{1,0:T(8,128)(...) custom-call(bf16[256,2048]{1,0:T(8,128)(2,1)} %refs_0_.3, ...), custom_call_target="tpu_custom_call" | custom-call | flops 2415919104 | bytes 12582912 | tf_op jit(solution)/shard_map/pallas_call | solution.py:48
  9.3 4.5 %shard_map.142 = (bf16[256,512]{1,0:T(8,128)(2,1)S(1)}, bf16[256,512]{1,0:T(8,128)(2,1)S(1)}, f32[256,512]{1,0:T(8,128)S(1)}, f32[4,256,256]{2,1,0:T(8,128)S(1)}...) custom-call(bf16[256,2048]{1,0:T(8,128)(2,1)S(1)} %get-tuple-element.53.refs_0_, s32[1,2048]{1,0:T(1,128)S(1)} %copy-done.3, ...), custom_call_target="tpu_custom_call" | custom-call | flops 1342177280 | bytes 8388608 | tf_op jit(solution)/shard_map/pallas_call | solution.py:48
  14.1 3.3 %collective-permute-start.6 = (bf16[256,1024]{1,0:T(8,128)(2,1)S(1)}, bf16[256,1024]{1,0:T(8,128)(2,1)S(1)}, u32[]{:S(2)}, u32[]{:S(2)}) collective-permute-start(bf16[256,1024]{1,0:T(8,128)(2,1)S(1)} %add_convert_fusion.1.refs_9_.refs_0_), channel_id=1, source_target_pairs={{0,2},{2,0},{1,3},{3,1},{4,6},{6,4},{5,7},{7,5},{8,10},{10,8},{9,1... | collective-permute-start | bytes 1572872 | tf_op jit(solution)/shard_map/ppermute | solution.py:442
  17.9 11.9 %collective-permute-done.6.refs_1_ = bf16[256,1024]{1,0:T(8,128)(2,1)S(1)} collective-permute-done((bf16[256,1024]{1,0:T(8,128)(2,1)S(1)}, bf16[256,1024]{1,0:T(8,128)(2,1)S(1)}, u32[]{:S(2)}, u32[]{:S(2)}) %collective-permute-start.6) | collective-permute-done | bytes 524320 | tf_op jit(solution)/shard_map/ppermute | solution.py:442
  30.2 3.3 %collective-permute-start.5 = (bf16[256,1024]{1,0:T(8,128)(2,1)S(1)}, bf16[256,1024]{1,0:T(8,128)(2,1)S(1)}, u32[]{:S(2)}, u32[]{:S(2)}) collective-permute-start(bf16[256,1024]{1,0:T(8,128)(2,1)S(1)} %add_convert_fusion.refs_4_.refs_0_), channel_id=1, source_target_pairs={{0,2},{2,0},{1,3},{3,1},{4,6},{6,4},{5,7},{7,5},{8,10},{10,8},{9,1... | collective-permute-start | bytes 1572872 | tf_op jit(solution)/shard_map/ppermute | solution.py:442
  33.5 2.8 %shard_map.145 = (f32[256,512]{1,0:T(8,128)S(1)}, f32[256,512]{1,0:T(8,128)S(1)}) custom-call(bf16[256,1024]{1,0:T(8,128)(2,1)S(1)} %shard_map.144.refs_0_, bf16[256,1024]{1,0:T(8,128)(2,1)S(1)} %collective-permute-done.7.refs_1_, bf16[512,2048]{1,0:T(8,128)(2,1)S(1)} %get-tuple-element.62.refs_1_.refs_8_.refs_2_, ...), custom_call_target="tpu_custom_call" | custom-call | flops 872415232 | bytes 6291456 | tf_op jit(solution)/shard_map/pallas_call | solution.py:48
  36.3 9.7 %collective-permute-done.5.refs_1_ = bf16[256,1024]{1,0:T(8,128)(2,1)S(1)} collective-permute-done((bf16[256,1024]{1,0:T(8,128)(2,1)S(1)}, bf16[256,1024]{1,0:T(8,128)(2,1)S(1)}, u32[]{:S(2)}, u32[]{:S(2)}) %collective-permute-start.5) | collective-permute-done | bytes 524320 | tf_op jit(solution)/shard_map/ppermute | solution.py:442
  46.2 1.6 %collective-permute-start.16 = (bf16[512,256]{1,0:T(8,128)(2,1)S(1)}, bf16[512,256]{1,0:T(8,128)(2,1)S(1)}, u32[]{:S(2)}, u32[]{:S(2)}) collective-permute-start(bf16[512,256]{1,0:T(8,128)(2,1)S(1)} %get-tuple-element.84), channel_id=1, source_target_pairs={{0,32},{32,64},{64,96},{96,0},{1,33},{33,65},{65,97},{97,1},{2,34}... | collective-permute-start | bytes 786440 | tf_op jit(solution)/shard_map/ppermute | solution.py:442
  47.9 2.7 %collective-permute-start.17 = (bf16[512,256]{1,0:T(8,128)(2,1)S(1)}, bf16[512,256]{1,0:T(8,128)(2,1)S(1)}, u32[]{:S(2)}, u32[]{:S(2)}) collective-permute-start(bf16[512,256]{1,0:T(8,128)(2,1)S(1)} %get-tuple-element.85), channel_id=1, source_target_pairs={{0,64},{32,96},{64,0},{96,32},{1,65},{33,97},{65,1},{97,33},{2,66}... | collective-permute-start | bytes 786440 | tf_op jit(solution)/shard_map/ppermute | solution.py:442
  50.6 1.4 %collective-permute-start.18 = (bf16[512,256]{1,0:T(8,128)(2,1)S(1)}, bf16[512,256]{1,0:T(8,128)(2,1)S(1)}, u32[]{:S(2)}, u32[]{:S(2)}) collective-permute-start(bf16[512,256]{1,0:T(8,128)(2,1)S(1)} %get-tuple-element.86), channel_id=1, source_target_pairs={{0,96},{32,0},{64,32},{96,64},{1,97},{33,1},{65,33},{97,65},{2,98}... | collective-permute-start | bytes 786440 | tf_op jit(solution)/shard_map/ppermute | solution.py:442
  52.0 1.9 %collective-permute-start = (bf16[512,256]{1,0:T(8,128)(2,1)S(1)}, bf16[512,256]{1,0:T(8,128)(2,1)S(1)}, u32[]{:S(2)}, u32[]{:S(2)}) collective-permute-start(bf16[512,256]{1,0:T(8,128)(2,1)S(1)} %get-tuple-element.55), channel_id=1, source_target_pairs={{0,8},{8,16},{16,24},{24,0},{1,9},{9,17},{17,25},{25,1},{2,10},{10... | collective-permute-start | bytes 786440 | tf_op jit(solution)/shard_map/ppermute | solution.py:442
  54.4 2.0 %shard_map.148 = (bf16[256,640]{1,0:T(8,128)(2,1)S(1)}, bf16[256,384]{1,0:T(8,128)(2,1)S(1)}, f32[16,128]{1,0:T(8,128)S(1)}) custom-call(f32[256,512]{1,0:T(8,128)S(1)} %shard_map.147.refs_0_, bf16[256,1024]{1,0:T(8,128)(2,1)S(1)} %collective-permute-done.8.refs_1_, bf16[512,2048]{1,0:T(8,128)(2,1)S(1)} %get-tuple-element.62.refs_1_.refs_8_.refs_2_, ...), custom_call_target="tpu_custom_call" | custom-call | flops 738197504 | bytes 6291456 | tf_op jit(solution)/shard_map/pallas_call | solution.py:48
  57.6 3.2 %collective-permute-start.20 = (f32[16,128]{1,0:T(8,128)S(1)}, f32[16,128]{1,0:T(8,128)S(1)}, u32[]{:S(2)}, u32[]{:S(2)}) collective-permute-start(f32[16,128]{1,0:T(8,128)S(1)} %add.11.refs_1_), channel_id=1, source_target_pairs={{0,2},{2,0},{1,3},{3,1},{4,6},{6,4},{5,7},{7,5},{8,10},{10,8},{9,1... | collective-permute-start | bytes 24584 | tf_op jit(solution)/shard_map/ppermute | solution.py:442
  60.8 2.0 %collective-permute-done.20.refs_2_ = f32[16,128]{1,0:T(8,128)S(1)} collective-permute-done((f32[16,128]{1,0:T(8,128)S(1)}, f32[16,128]{1,0:T(8,128)S(1)}, u32[]{:S(2)}, u32[]{:S(2)}) %collective-permute-start.20) | collective-permute-done | bytes 8224 | tf_op jit(solution)/shard_map/ppermute | solution.py:442
  64.3 1.9 %collective-permute-start.23 = (bf16[272,384]{1,0:T(8,128)(2,1)S(1)}, bf16[272,384]{1,0:T(8,128)(2,1)S(1)}, u32[]{:S(2)}, u32[]{:S(2)}) collective-permute-start(bf16[272,384]{1,0:T(8,128)(2,1)S(1)} %get-tuple-element.89.refs_4_), channel_id=1, source_target_pairs={{0,96},{32,0},{64,32},{96,64},{1,97},{33,1},{65,33},{97,65},{2,98}... | collective-permute-start | bytes 626696 | tf_op jit(solution)/shard_map/ppermute | solution.py:442
  66.2 3.6 %collective-permute-start.10 = (bf16[256,640]{1,0:T(8,128)(2,1)S(1)}, bf16[256,640]{1,0:T(8,128)(2,1)S(1)}, u32[]{:S(2)}, u32[]{:S(2)}) collective-permute-start(bf16[256,640]{1,0:T(8,128)(2,1)S(1)} %get-tuple-element.75.refs_4_), channel_id=1, source_target_pairs={{0,16},{8,24},{16,0},{24,8},{1,17},{9,25},{17,1},{25,9},{2,18},{10... | collective-permute-start | bytes 983048 | tf_op jit(solution)/shard_map/ppermute | solution.py:442
  70.8 4.1 %collective-permute-done.21.refs_5_ = bf16[272,384]{1,0:T(8,128)(2,1)S(1)} collective-permute-done((bf16[272,384]{1,0:T(8,128)(2,1)S(1)}, bf16[272,384]{1,0:T(8,128)(2,1)S(1)}, u32[]{:S(2)}, u32[]{:S(2)}) %collective-permute-start.21) | collective-permute-done | bytes 208928 | tf_op jit(solution)/shard_map/ppermute | solution.py:442
  74.9 1.9 %collective-permute-start.9 = (bf16[256,640]{1,0:T(8,128)(2,1)S(1)}, bf16[256,640]{1,0:T(8,128)(2,1)S(1)}, u32[]{:S(2)}, u32[]{:S(2)}) collective-permute-start(bf16[256,640]{1,0:T(8,128)(2,1)S(1)} %get-tuple-element.75.refs_4_), channel_id=1, source_target_pairs={{0,8},{8,16},{16,24},{24,0},{1,9},{9,17},{17,25},{25,1},{2,10},{10... | collective-permute-start | bytes 983048 | tf_op jit(solution)/shard_map/ppermute | solution.py:442
  76.9 1.7 %collective-permute-start.1 = (bf16[512,256]{1,0:T(8,128)(2,1)S(1)}, bf16[512,256]{1,0:T(8,128)(2,1)S(1)}, u32[]{:S(2)}, u32[]{:S(2)}) collective-permute-start(bf16[512,256]{1,0:T(8,128)(2,1)S(1)} %get-tuple-element.56), channel_id=1, source_target_pairs={{0,16},{8,24},{16,0},{24,8},{1,17},{9,25},{17,1},{25,9},{2,18},{10... | collective-permute-start | bytes 786440 | tf_op jit(solution)/shard_map/ppermute | solution.py:442
  78.5 2.6 %collective-permute-start.2 = (bf16[512,256]{1,0:T(8,128)(2,1)S(1)}, bf16[512,256]{1,0:T(8,128)(2,1)S(1)}, u32[]{:S(2)}, u32[]{:S(2)}) collective-permute-start(bf16[512,256]{1,0:T(8,128)(2,1)S(1)} %get-tuple-element.57), channel_id=1, source_target_pairs={{0,24},{8,0},{16,8},{24,16},{1,25},{9,1},{17,9},{25,17},{2,26},{10... | collective-permute-start | bytes 786440 | tf_op jit(solution)/shard_map/ppermute | solution.py:442
  81.9 9.2 %collective-permute-done.1.refs_2_ = bf16[512,256]{1,0:T(8,128)(2,1)S(1)} collective-permute-done((bf16[512,256]{1,0:T(8,128)(2,1)S(1)}, bf16[512,256]{1,0:T(8,128)(2,1)S(1)}, u32[]{:S(2)}, u32[]{:S(2)}) %collective-permute-start.1) | collective-permute-done | bytes 262176 | tf_op jit(solution)/shard_map/ppermute | solution.py:442
  91.1 1.3 %collective-permute-start.24 = (bf16[272,384]{1,0:T(8,128)(2,1)S(1)}, bf16[272,384]{1,0:T(8,128)(2,1)S(1)}, u32[]{:S(2)}, u32[]{:S(2)}) collective-permute-start(bf16[272,384]{1,0:T(8,128)(2,1)S(1)} %get-tuple-element.92), channel_id=1, source_target_pairs={{0,4},{4,0},{1,5},{5,1},{2,6},{6,2},{3,7},{7,3},{8,12},{12,8},{9,1... | collective-permute-start | bytes 626696 | tf_op jit(solution)/shard_map/ppermute | solution.py:442
  92.3 1.5 %collective-permute-done.2.refs_3_ = bf16[512,256]{1,0:T(8,128)(2,1)S(1)} collective-permute-done((bf16[512,256]{1,0:T(8,128)(2,1)S(1)}, bf16[512,256]{1,0:T(8,128)(2,1)S(1)}, u32[]{:S(2)}, u32[]{:S(2)}) %collective-permute-start.2) | collective-permute-done | bytes 262176 | tf_op jit(solution)/shard_map/ppermute | solution.py:442
  96.1 2.4 %collective-permute-start.13 = (bf16[128,640]{1,0:T(8,128)(2,1)S(1)}, bf16[128,640]{1,0:T(8,128)(2,1)S(1)}, u32[]{:S(2)}, u32[]{:S(2)}) collective-permute-start(bf16[128,640]{1,0:T(8,128)(2,1)S(1)} %get-tuple-element.78), channel_id=1, source_target_pairs={{0,64},{32,96},{64,0},{96,32},{1,65},{33,97},{65,1},{97,33},{2,66}... | collective-permute-start | bytes 491528 | tf_op jit(solution)/shard_map/ppermute | solution.py:442
  98.5 1.6 %collective-permute-start.14 = (bf16[128,640]{1,0:T(8,128)(2,1)S(1)}, bf16[128,640]{1,0:T(8,128)(2,1)S(1)}, u32[]{:S(2)}, u32[]{:S(2)}) collective-permute-start(bf16[128,640]{1,0:T(8,128)(2,1)S(1)} %get-tuple-element.79), channel_id=1, source_target_pairs={{0,96},{32,0},{64,32},{96,64},{1,97},{33,1},{65,33},{97,65},{2,98}... | collective-permute-start | bytes 491528 | tf_op jit(solution)/shard_map/ppermute | solution.py:442
  100.1 3.1 %collective-permute-done.12.refs_1_ = bf16[128,640]{1,0:T(8,128)(2,1)S(1)} collective-permute-done((bf16[128,640]{1,0:T(8,128)(2,1)S(1)}, bf16[128,640]{1,0:T(8,128)(2,1)S(1)}, u32[]{:S(2)}, u32[]{:S(2)}) %collective-permute-start.12) | collective-permute-done | bytes 163872 | tf_op jit(solution)/shard_map/ppermute | solution.py:442
  103.2 1.8 %collective-permute-done.13.refs_2_ = bf16[128,640]{1,0:T(8,128)(2,1)S(1)} collective-permute-done((bf16[128,640]{1,0:T(8,128)(2,1)S(1)}, bf16[128,640]{1,0:T(8,128)(2,1)S(1)}, u32[]{:S(2)}, u32[]{:S(2)}) %collective-permute-start.13) | collective-permute-done | bytes 163872 | tf_op jit(solution)/shard_map/ppermute | solution.py:442
  105.3 1.7 %collective-permute-start.15 = (bf16[64,640]{1,0:T(8,128)(2,1)S(1)}, bf16[64,640]{1,0:T(8,128)(2,1)S(1)}, u32[]{:S(2)}, u32[]{:S(2)}) collective-permute-start(bf16[64,640]{1,0:T(8,128)(2,1)S(1)} %get-tuple-element.81), channel_id=1, source_target_pairs={{0,4},{4,0},{1,5},{5,1},{2,6},{6,2},{3,7},{7,3},{8,12},{12,8},{9,1... | collective-permute-start | bytes 245768 | tf_op jit(solution)/shard_map/ppermute | solution.py:442
  107.0 2.1 %collective-permute-start.25 = (bf16[80,384]{1,0:T(8,128)(2,1)S(1)}, bf16[80,384]{1,0:T(8,128)(2,1)S(1)}, u32[]{:S(2)}, u32[]{:S(2)}) collective-permute-start(bf16[80,384]{1,0:T(8,128)(2,1)S(1)} %get-tuple-element.95), channel_id=1, source_target_pairs={{0,8},{8,16},{16,24},{24,0},{1,9},{9,17},{17,25},{25,1},{2,10},{10... | collective-permute-start | bytes 184328 | tf_op jit(solution)/shard_map/ppermute | solution.py:442
  109.2 3.1 %collective-permute-start.26 = (bf16[80,384]{1,0:T(8,128)(2,1)S(1)}, bf16[80,384]{1,0:T(8,128)(2,1)S(1)}, u32[]{:S(2)}, u32[]{:S(2)}) collective-permute-start(bf16[80,384]{1,0:T(8,128)(2,1)S(1)} %get-tuple-element.96), channel_id=1, source_target_pairs={{0,16},{8,24},{16,0},{24,8},{1,17},{9,25},{17,1},{25,9},{2,18},{10... | collective-permute-start | bytes 184328 | tf_op jit(solution)/shard_map/ppermute | solution.py:442
  113.4 1.7 %collective-permute-done.26.refs_2_ = bf16[80,384]{1,0:T(8,128)(2,1)S(1)} collective-permute-done((bf16[80,384]{1,0:T(8,128)(2,1)S(1)}, bf16[80,384]{1,0:T(8,128)(2,1)S(1)}, u32[]{:S(2)}, u32[]{:S(2)}) %collective-permute-start.26) | collective-permute-done | bytes 61472 | tf_op jit(solution)/shard_map/ppermute | solution.py:442
  115.1 1.4 %collective-permute-done.27.refs_3_ = bf16[80,384]{1,0:T(8,128)(2,1)S(1)} collective-permute-done((bf16[80,384]{1,0:T(8,128)(2,1)S(1)}, bf16[80,384]{1,0:T(8,128)(2,1)S(1)}, u32[]{:S(2)}, u32[]{:S(2)}) %collective-permute-start.27) | collective-permute-done | bytes 61472 | tf_op jit(solution)/shard_map/ppermute | solution.py:442
  (56 shorter events, 13.5 us)
Async XLA Ops:
  0.6 6.6 %copy-start.3 = (s32[1,2048]{1,0:T(1,128)S(1)}, s32[1,2048]{1,0:T(1,128)}, u32[]{:S(2)}) copy-start(s32[1,2048]{1,0:T(1,128)} %refs_1_.4) | copy-start | bytes 24580
  7.1 2.0 %collective-permute-start.3 = (bf16[256,1024]{1,0:T(8,128)(2,1)S(1)}, bf16[256,1024]{1,0:T(8,128)(2,1)S(1)}, u32[]{:S(2)}, u32[]{:S(2)}) collective-permute-start(bf16[256,1024]{1,0:T(8,128)(2,1)S(1)} %get-tuple-element.64), channel_id=1, source_target_pairs={{0,1},{1,0},{2,3},{3,2},{4,5},{5,4},{6,7},{7,6},{8,9},{9,8},{10,11... | collective-permute-start | bytes 1572872 | tf_op jit(solution)/shard_map/ppermute | solution.py:442
  9.3 8.1 %copy-start = (bf16[256,2048]{1,0:T(8,128)(2,1)S(1)}, bf16[256,2048]{1,0:T(8,128)(2,1)}, u32[]{:S(2)}) copy-start(bf16[256,2048]{1,0:T(8,128)(2,1)} %refs_0_.3) | copy-start | bytes 3145732
  9.3 8.1 %copy-start.2 = (bf16[256,2048]{1,0:T(8,128)(2,1)S(1)}, bf16[256,2048]{1,0:T(8,128)(2,1)}, u32[]{:S(2)}) copy-start(bf16[256,2048]{1,0:T(8,128)(2,1)} %refs_1_.5) | copy-start | bytes 3145732
  9.3 8.1 %copy-start.5 = (f32[256]{0:T(256)S(1)}, f32[256]{0:T(256)}, u32[]{:S(2)}) copy-start(f32[256]{0:T(256)} %param.14) | copy-start | bytes 3076
  13.9 3.9 %collective-permute-start.4 = (bf16[256,1024]{1,0:T(8,128)(2,1)S(1)}, bf16[256,1024]{1,0:T(8,128)(2,1)S(1)}, u32[]{:S(2)}, u32[]{:S(2)}) collective-permute-start(bf16[256,1024]{1,0:T(8,128)(2,1)S(1)} %get-tuple-element.66), channel_id=1, source_target_pairs={{0,1},{1,0},{2,3},{3,2},{4,5},{5,4},{6,7},{7,6},{8,9},{9,8},{10,11... | collective-permute-start | bytes 1572872 | tf_op jit(solution)/shard_map/ppermute | solution.py:442
  14.1 15.8 %collective-permute-start.6 = (bf16[256,1024]{1,0:T(8,128)(2,1)S(1)}, bf16[256,1024]{1,0:T(8,128)(2,1)S(1)}, u32[]{:S(2)}, u32[]{:S(2)}) collective-permute-start(bf16[256,1024]{1,0:T(8,128)(2,1)S(1)} %add_convert_fusion.1.refs_9_.refs_0_), channel_id=1, source_target_pairs={{0,2},{2,0},{1,3},{3,1},{4,6},{6,4},{5,7},{7,5},{8,10},{10,8},{9,1... | collective-permute-start | bytes 1572872 | tf_op jit(solution)/shard_map/ppermute | solution.py:442
  30.1 3.4 %collective-permute-start.7 = (bf16[256,1024]{1,0:T(8,128)(2,1)S(1)}, bf16[256,1024]{1,0:T(8,128)(2,1)S(1)}, u32[]{:S(2)}, u32[]{:S(2)}) collective-permute-start(bf16[256,1024]{1,0:T(8,128)(2,1)S(1)} %shard_map.144.refs_0_), channel_id=1, source_target_pairs={{0,1},{1,0},{2,3},{3,2},{4,5},{5,4},{6,7},{7,6},{8,9},{9,8},{10,11... | collective-permute-start | bytes 1572872 | tf_op jit(solution)/shard_map/ppermute | solution.py:442
  30.2 15.8 %collective-permute-start.5 = (bf16[256,1024]{1,0:T(8,128)(2,1)S(1)}, bf16[256,1024]{1,0:T(8,128)(2,1)S(1)}, u32[]{:S(2)}, u32[]{:S(2)}) collective-permute-start(bf16[256,1024]{1,0:T(8,128)(2,1)S(1)} %add_convert_fusion.refs_4_.refs_0_), channel_id=1, source_target_pairs={{0,2},{2,0},{1,3},{3,1},{4,6},{6,4},{5,7},{7,5},{8,10},{10,8},{9,1... | collective-permute-start | bytes 1572872 | tf_op jit(solution)/shard_map/ppermute | solution.py:442
  46.2 8.3 %collective-permute-start.8 = (bf16[256,1024]{1,0:T(8,128)(2,1)S(1)}, bf16[256,1024]{1,0:T(8,128)(2,1)S(1)}, u32[]{:S(2)}, u32[]{:S(2)}) collective-permute-start(bf16[256,1024]{1,0:T(8,128)(2,1)S(1)} %shard_map.146.refs_0_), channel_id=1, source_target_pairs={{0,1},{1,0},{2,3},{3,2},{4,5},{5,4},{6,7},{7,6},{8,9},{9,8},{10,11... | collective-permute-start | bytes 1572872 | tf_op jit(solution)/shard_map/ppermute | solution.py:442
  46.2 17.2 %collective-permute-start.16 = (bf16[512,256]{1,0:T(8,128)(2,1)S(1)}, bf16[512,256]{1,0:T(8,128)(2,1)S(1)}, u32[]{:S(2)}, u32[]{:S(2)}) collective-permute-start(bf16[512,256]{1,0:T(8,128)(2,1)S(1)} %get-tuple-element.84), channel_id=1, source_target_pairs={{0,32},{32,64},{64,96},{96,0},{1,33},{33,65},{65,97},{97,1},{2,34}... | collective-permute-start | bytes 786440 | tf_op jit(solution)/shard_map/ppermute | solution.py:442
  47.9 16.4 %collective-permute-start.17 = (bf16[512,256]{1,0:T(8,128)(2,1)S(1)}, bf16[512,256]{1,0:T(8,128)(2,1)S(1)}, u32[]{:S(2)}, u32[]{:S(2)}) collective-permute-start(bf16[512,256]{1,0:T(8,128)(2,1)S(1)} %get-tuple-element.85), channel_id=1, source_target_pairs={{0,64},{32,96},{64,0},{96,32},{1,65},{33,97},{65,1},{97,33},{2,66}... | collective-permute-start | bytes 786440 | tf_op jit(solution)/shard_map/ppermute | solution.py:442
  50.6 15.6 %collective-permute-start.18 = (bf16[512,256]{1,0:T(8,128)(2,1)S(1)}, bf16[512,256]{1,0:T(8,128)(2,1)S(1)}, u32[]{:S(2)}, u32[]{:S(2)}) collective-permute-start(bf16[512,256]{1,0:T(8,128)(2,1)S(1)} %get-tuple-element.86), channel_id=1, source_target_pairs={{0,96},{32,0},{64,32},{96,64},{1,97},{33,1},{65,33},{97,65},{2,98}... | collective-permute-start | bytes 786440 | tf_op jit(solution)/shard_map/ppermute | solution.py:442
  52.0 17.8 %collective-permute-start = (bf16[512,256]{1,0:T(8,128)(2,1)S(1)}, bf16[512,256]{1,0:T(8,128)(2,1)S(1)}, u32[]{:S(2)}, u32[]{:S(2)}) collective-permute-start(bf16[512,256]{1,0:T(8,128)(2,1)S(1)} %get-tuple-element.55), channel_id=1, source_target_pairs={{0,8},{8,16},{16,24},{24,0},{1,9},{9,17},{17,25},{25,1},{2,10},{10... | collective-permute-start | bytes 786440 | tf_op jit(solution)/shard_map/ppermute | solution.py:442
  56.4 1.2 %collective-permute-start.19 = (f32[16,128]{1,0:T(8,128)S(1)}, f32[16,128]{1,0:T(8,128)S(1)}, u32[]{:S(2)}, u32[]{:S(2)}) collective-permute-start(f32[16,128]{1,0:T(8,128)S(1)} %get-tuple-element.88), channel_id=1, source_target_pairs={{0,1},{1,0},{2,3},{3,2},{4,5},{5,4},{6,7},{7,6},{8,9},{9,8},{10,11... | collective-permute-start | bytes 24584 | tf_op jit(solution)/shard_map/ppermute | solution.py:442
  57.6 5.2 %collective-permute-start.20 = (f32[16,128]{1,0:T(8,128)S(1)}, f32[16,128]{1,0:T(8,128)S(1)}, u32[]{:S(2)}, u32[]{:S(2)}) collective-permute-start(f32[16,128]{1,0:T(8,128)S(1)} %add.11.refs_1_), channel_id=1, source_target_pairs={{0,2},{2,0},{1,3},{3,1},{4,6},{6,4},{5,7},{7,5},{8,10},{10,8},{9,1... | collective-permute-start | bytes 24584 | tf_op jit(solution)/shard_map/ppermute | solution.py:442
  62.8 12.1 %collective-permute-start.21 = (bf16[272,384]{1,0:T(8,128)(2,1)S(1)}, bf16[272,384]{1,0:T(8,128)(2,1)S(1)}, u32[]{:S(2)}, u32[]{:S(2)}) collective-permute-start(bf16[272,384]{1,0:T(8,128)(2,1)S(1)} %get-tuple-element.89.refs_4_), channel_id=1, source_target_pairs={{0,32},{32,64},{64,96},{96,0},{1,33},{33,65},{65,97},{97,1},{2,34}... | collective-permute-start | bytes 626696 | tf_op jit(solution)/shard_map/ppermute | solution.py:442
  63.5 13.4 %collective-permute-start.22 = (bf16[272,384]{1,0:T(8,128)(2,1)S(1)}, bf16[272,384]{1,0:T(8,128)(2,1)S(1)}, u32[]{:S(2)}, u32[]{:S(2)}) collective-permute-start(bf16[272,384]{1,0:T(8,128)(2,1)S(1)} %get-tuple-element.89.refs_4_), channel_id=1, source_target_pairs={{0,64},{32,96},{64,0},{96,32},{1,65},{33,97},{65,1},{97,33},{2,66}... | collective-permute-start | bytes 626696 | tf_op jit(solution)/shard_map/ppermute | solution.py:442
  64.3 14.2 %collective-permute-start.23 = (bf16[272,384]{1,0:T(8,128)(2,1)S(1)}, bf16[272,384]{1,0:T(8,128)(2,1)S(1)}, u32[]{:S(2)}, u32[]{:S(2)}) collective-permute-start(bf16[272,384]{1,0:T(8,128)(2,1)S(1)} %get-tuple-element.89.refs_4_), channel_id=1, source_target_pairs={{0,96},{32,0},{64,32},{96,64},{1,97},{33,1},{65,33},{97,65},{2,98}... | collective-permute-start | bytes 626696 | tf_op jit(solution)/shard_map/ppermute | solution.py:442
  66.2 27.6 %collective-permute-start.10 = (bf16[256,640]{1,0:T(8,128)(2,1)S(1)}, bf16[256,640]{1,0:T(8,128)(2,1)S(1)}, u32[]{:S(2)}, u32[]{:S(2)}) collective-permute-start(bf16[256,640]{1,0:T(8,128)(2,1)S(1)} %get-tuple-element.75.refs_4_), channel_id=1, source_target_pairs={{0,16},{8,24},{16,0},{24,8},{1,17},{9,25},{17,1},{25,9},{2,18},{10... | collective-permute-start | bytes 983048 | tf_op jit(solution)/shard_map/ppermute | solution.py:442
  69.8 24.0 %collective-permute-start.11 = (bf16[256,640]{1,0:T(8,128)(2,1)S(1)}, bf16[256,640]{1,0:T(8,128)(2,1)S(1)}, u32[]{:S(2)}, u32[]{:S(2)}) collective-permute-start(bf16[256,640]{1,0:T(8,128)(2,1)S(1)} %get-tuple-element.75.refs_4_), channel_id=1, source_target_pairs={{0,24},{8,0},{16,8},{24,16},{1,25},{9,1},{17,9},{25,17},{2,26},{10... | collective-permute-start | bytes 983048 | tf_op jit(solution)/shard_map/ppermute | solution.py:442
  74.9 18.9 %collective-permute-start.9 = (bf16[256,640]{1,0:T(8,128)(2,1)S(1)}, bf16[256,640]{1,0:T(8,128)(2,1)S(1)}, u32[]{:S(2)}, u32[]{:S(2)}) collective-permute-start(bf16[256,640]{1,0:T(8,128)(2,1)S(1)} %get-tuple-element.75.refs_4_), channel_id=1, source_target_pairs={{0,8},{8,16},{16,24},{24,0},{1,9},{9,17},{17,25},{25,1},{2,10},{10... | collective-permute-start | bytes 983048 | tf_op jit(solution)/shard_map/ppermute | solution.py:442
  76.9 14.2 %collective-permute-start.1 = (bf16[512,256]{1,0:T(8,128)(2,1)S(1)}, bf16[512,256]{1,0:T(8,128)(2,1)S(1)}, u32[]{:S(2)}, u32[]{:S(2)}) collective-permute-start(bf16[512,256]{1,0:T(8,128)(2,1)S(1)} %get-tuple-element.56), channel_id=1, source_target_pairs={{0,16},{8,24},{16,0},{24,8},{1,17},{9,25},{17,1},{25,9},{2,18},{10... | collective-permute-start | bytes 786440 | tf_op jit(solution)/shard_map/ppermute | solution.py:442
  78.5 15.3 %collective-permute-start.2 = (bf16[512,256]{1,0:T(8,128)(2,1)S(1)}, bf16[512,256]{1,0:T(8,128)(2,1)S(1)}, u32[]{:S(2)}, u32[]{:S(2)}) collective-permute-start(bf16[512,256]{1,0:T(8,128)(2,1)S(1)} %get-tuple-element.57), channel_id=1, source_target_pairs={{0,24},{8,0},{16,8},{24,16},{1,25},{9,1},{17,9},{25,17},{2,26},{10... | collective-permute-start | bytes 786440 | tf_op jit(solution)/shard_map/ppermute | solution.py:442
  91.1 15.9 %collective-permute-start.24 = (bf16[272,384]{1,0:T(8,128)(2,1)S(1)}, bf16[272,384]{1,0:T(8,128)(2,1)S(1)}, u32[]{:S(2)}, u32[]{:S(2)}) collective-permute-start(bf16[272,384]{1,0:T(8,128)(2,1)S(1)} %get-tuple-element.92), channel_id=1, source_target_pairs={{0,4},{4,0},{1,5},{5,1},{2,6},{6,2},{3,7},{7,3},{8,12},{12,8},{9,1... | collective-permute-start | bytes 626696 | tf_op jit(solution)/shard_map/ppermute | solution.py:442
  94.9 8.4 %collective-permute-start.12 = (bf16[128,640]{1,0:T(8,128)(2,1)S(1)}, bf16[128,640]{1,0:T(8,128)(2,1)S(1)}, u32[]{:S(2)}, u32[]{:S(2)}) collective-permute-start(bf16[128,640]{1,0:T(8,128)(2,1)S(1)} %get-tuple-element.77), channel_id=1, source_target_pairs={{0,32},{32,64},{64,96},{96,0},{1,33},{33,65},{65,97},{97,1},{2,34}... | collective-permute-start | bytes 491528 | tf_op jit(solution)/shard_map/ppermute | solution.py:442
  96.1 8.9 %collective-permute-start.13 = (bf16[128,640]{1,0:T(8,128)(2,1)S(1)}, bf16[128,640]{1,0:T(8,128)(2,1)S(1)}, u32[]{:S(2)}, u32[]{:S(2)}) collective-permute-start(bf16[128,640]{1,0:T(8,128)(2,1)S(1)} %get-tuple-element.78), channel_id=1, source_target_pairs={{0,64},{32,96},{64,0},{96,32},{1,65},{33,97},{65,1},{97,33},{2,66}... | collective-permute-start | bytes 491528 | tf_op jit(solution)/shard_map/ppermute | solution.py:442
  98.5 6.7 %collective-permute-start.14 = (bf16[128,640]{1,0:T(8,128)(2,1)S(1)}, bf16[128,640]{1,0:T(8,128)(2,1)S(1)}, u32[]{:S(2)}, u32[]{:S(2)}) collective-permute-start(bf16[128,640]{1,0:T(8,128)(2,1)S(1)} %get-tuple-element.79), channel_id=1, source_target_pairs={{0,96},{32,0},{64,32},{96,64},{1,97},{33,1},{65,33},{97,65},{2,98}... | collective-permute-start | bytes 491528 | tf_op jit(solution)/shard_map/ppermute | solution.py:442
  105.3 11.8 %collective-permute-start.15 = (bf16[64,640]{1,0:T(8,128)(2,1)S(1)}, bf16[64,640]{1,0:T(8,128)(2,1)S(1)}, u32[]{:S(2)}, u32[]{:S(2)}) collective-permute-start(bf16[64,640]{1,0:T(8,128)(2,1)S(1)} %get-tuple-element.81), channel_id=1, source_target_pairs={{0,4},{4,0},{1,5},{5,1},{2,6},{6,2},{3,7},{7,3},{8,12},{12,8},{9,1... | collective-permute-start | bytes 245768 | tf_op jit(solution)/shard_map/ppermute | solution.py:442
  107.0 6.4 %collective-permute-start.25 = (bf16[80,384]{1,0:T(8,128)(2,1)S(1)}, bf16[80,384]{1,0:T(8,128)(2,1)S(1)}, u32[]{:S(2)}, u32[]{:S(2)}) collective-permute-start(bf16[80,384]{1,0:T(8,128)(2,1)S(1)} %get-tuple-element.95), channel_id=1, source_target_pairs={{0,8},{8,16},{16,24},{24,0},{1,9},{9,17},{17,25},{25,1},{2,10},{10... | collective-permute-start | bytes 184328 | tf_op jit(solution)/shard_map/ppermute | solution.py:442
  109.2 6.0 %collective-permute-start.26 = (bf16[80,384]{1,0:T(8,128)(2,1)S(1)}, bf16[80,384]{1,0:T(8,128)(2,1)S(1)}, u32[]{:S(2)}, u32[]{:S(2)}) collective-permute-start(bf16[80,384]{1,0:T(8,128)(2,1)S(1)} %get-tuple-element.96), channel_id=1, source_target_pairs={{0,16},{8,24},{16,0},{24,8},{1,17},{9,25},{17,1},{25,9},{2,18},{10... | collective-permute-start | bytes 184328 | tf_op jit(solution)/shard_map/ppermute | solution.py:442
  112.3 4.2 %collective-permute-start.27 = (bf16[80,384]{1,0:T(8,128)(2,1)S(1)}, bf16[80,384]{1,0:T(8,128)(2,1)S(1)}, u32[]{:S(2)}, u32[]{:S(2)}) collective-permute-start(bf16[80,384]{1,0:T(8,128)(2,1)S(1)} %get-tuple-element.97), channel_id=1, source_target_pairs={{0,24},{8,0},{16,8},{24,16},{1,25},{9,1},{17,9},{25,17},{2,26},{10... | collective-permute-start | bytes 184328 | tf_op jit(solution)/shard_map/ppermute | solution.py:442
  (2 other events, 3.1 us)

commit v5 on v4

--- a/solution.py
+++ b/solution.py
@@ -362,22 +362,26 @@
     return sum(dot(a[...], b[:length, :]) for a, b in zip(x_parts, y_parts))
 
 
-def estimate_a_body(*refs):
-    outs = refs[8:]
+def part_body(*refs):
+    count = len(refs) // 2
+    refs[-1][...] = rows_times(refs[:count], refs[count:-1])
+
+
+def estimate_a_body(before, x_last, y_last, *outs):
     group = outs[0].shape[0]
-    whole = rows_times(refs[:4], refs[4:8])
+    whole = before[...] + rows_times([x_last], [y_last])
     for step, out in enumerate(outs):
         out[...] = whole[step * group : (step + 1) * group, :].astype(out.dtype)
 
 
 def estimate_b_body(*refs):
-    y_parts, sums, keep, send, sum_out = refs[4:8], refs[8], refs[9], refs[10], refs[11]
-    length = refs[0].shape[1]
+    before, x_parts, y_parts, (sums, keep, send, sum_out) = refs[0], refs[1:3], refs[3:6], refs[6:]
+    length = x_parts[0].shape[1]
     group = keep.shape[0]
     rows = group // 4
-    total = in_pairs(sums[...], *(read_sums(y[length:, :]) for y in y_parts[1:]))
+    total = in_pairs(sums[...], *(read_sums(y[length:, :]) for y in y_parts))
     sum_out[...] = total
-    whole = rows_times(refs[:4], y_parts)
+    whole = before[...] + rows_times(x_parts, y_parts[1:])
     for step in range(4):
         at = slice(step * rows, (step + 1) * rows)
         keep[at, :] = whole[2 * step * rows : (2 * step + 1) * rows, :]
@@ -543,20 +547,27 @@
     yb_in = [yb] + [flip(yb, where) for where in along_x]
 
     group = 2 * rows
+    near_first = (0, 1, 3)
+    part_a = call(part_body, shape((4 * group, cut), f32), [VMEM] * 6, (), 3 * product // 4, 3 * MIB, 16)(
+        *(xq[i] for i in near_first), *(ya_in[i] for i in near_first)
+    )
+    part_b = call(part_body, shape((4 * group, rest), f32), [VMEM] * 4, (), product // 2, 3 * MIB, 16, (part_a,))(
+        *xk[:2], *yb_in[:2]
+    )
     part, keep = shape((group, cut), bf16), shape((group, cut), f32)
     a = call(
         estimate_a_body,
         (keep, part, part, part),
-        [VMEM] * 8,
-        (), product, 3 * MIB, 24,
-    )(*xq, *ya_in)
+        [VMEM] * 3,
+        (), product // 4, 3 * MIB, 24,
+    )(part_a, xq[2], ya_in[2])
     side = [xor("yl", 1)]
     keep_b, send_b, sums = call(
         estimate_b_body,
         (shape((4 * rows, rest), f32), shape((4 * rows + 16, rest), bf16), small_sums),
-        [VMEM] * 9,
-        (), product, 3 * MIB, 24,
-    )(*xk, *yb_in, sums)
+        [VMEM] * 7,
+        (), product // 2, 3 * MIB, 24, (a[0],),
+    )(part_b, *xk[2:], *yb_in[1:], sums)
     came_b = flip(send_b, side)
     a_in = [flip(part, where) for part, where in zip(a[1:], along_x)]
     part = shape((rows + 16, rest), bf16)

time: 118 us -> 125 us (1.059)
  waiting for transfers between devices: 49.8 us -> 59.8 us
  starting transfers between devices: 45.7 us -> 42.2 us
    ppermute x28, waiting for transfers between devices: 49.8 us -> 59.8 us  [flip(): lax.ppermute(value, axes if len(axes) > 1 else axes[0], [(i, target(i)) f...]
    ppermute x28, starting transfers between devices: 45.7 us -> 42.2 us  [flip(): lax.ppermute(value, axes if len(axes) > 1 else axes[0], [(i, target(i)) f...]
    pallas_call x17 -> x19, Pallas kernels: 21.2 us -> 21.5 us  [run(): return kernel(*args, *after)]
  transfers between devices with their start and end apart: 28 -> 28, of which waited for: 14 -> 15; matrix products, arithmetic and copies ran while one was open for 0% -> 0% of each run, Pallas kernels for 8% -> 7%
where the time goes in v5:
time: 125 us
  waiting for transfers between devices  59.8 us (48%)
  starting transfers between devices  42.2 us (34%)
  Pallas kernels  21.5 us (17%)
    ppermute x28, waiting for transfers between devices, flip(): lax.ppermute(value, axes if len(axes) > 1 else axes[0], [(i, target(i)) f...  59.8 us
    ppermute x28, starting transfers between devices, flip(): lax.ppermute(value, axes if len(axes) > 1 else axes[0], [(i, target(i)) f...  42.2 us
    pallas_call x19, Pallas kernels, run(): return kernel(*args, *after)  21.5 us
  transfers between devices with their start and end apart: 28, of which 15 were waited for; matrix products, arithmetic and copies ran while one was open for 0% of the time, Pallas kernels for 7%

profile of v5, /device:TPU:0, one launch (start us, length us, event | category | flops | bytes accessed | tf_op | source)
XLA Modules:
  0.0 124.8 jit_solution(4985946460338706814)
XLA Ops:
  0.6 6.5 %shard_map.139 = (bf16[256,2048]{1,0:T(8,128)(2,1)S(1)}, bf16[256,512]{1,0:T(8,128)(2,1)S(1)}, bf16[256,512]{1,0:T(8,128)(2,1)S(1)}, bf16[256,512]{1,0:T(8,128)(...) custom-call(bf16[256,2048]{1,0:T(8,128)(2,1)} %refs_0_.3, ...), custom_call_target="tpu_custom_call" | custom-call | flops 2415919104 | bytes 12582912 | tf_op jit(solution)/shard_map/pallas_call | solution.py:48
  9.3 4.5 %shard_map.142 = (bf16[256,512]{1,0:T(8,128)(2,1)S(1)}, bf16[256,512]{1,0:T(8,128)(2,1)S(1)}, f32[256,512]{1,0:T(8,128)S(1)}, f32[4,256,256]{2,1,0:T(8,128)S(1)}...) custom-call(bf16[256,2048]{1,0:T(8,128)(2,1)S(1)} %get-tuple-element.53.refs_0_, s32[1,2048]{1,0:T(1,128)S(1)} %copy-done.3, ...), custom_call_target="tpu_custom_call" | custom-call | flops 1342177280 | bytes 8388608 | tf_op jit(solution)/shard_map/pallas_call | solution.py:48
  14.1 3.3 %collective-permute-start.5 = (bf16[256,1024]{1,0:T(8,128)(2,1)S(1)}, bf16[256,1024]{1,0:T(8,128)(2,1)S(1)}, u32[]{:S(2)}, u32[]{:S(2)}) collective-permute-start(bf16[256,1024]{1,0:T(8,128)(2,1)S(1)} %add_convert_fusion.1.refs_9_.refs_0_), channel_id=1, source_target_pairs={{0,2},{2,0},{1,3},{3,1},{4,6},{6,4},{5,7},{7,5},{8,10},{10,8},{9,1... | collective-permute-start | bytes 1572872 | tf_op jit(solution)/shard_map/ppermute | solution.py:446
  18.0 11.9 %collective-permute-done.5.refs_1_ = bf16[256,1024]{1,0:T(8,128)(2,1)S(1)} collective-permute-done((bf16[256,1024]{1,0:T(8,128)(2,1)S(1)}, bf16[256,1024]{1,0:T(8,128)(2,1)S(1)}, u32[]{:S(2)}, u32[]{:S(2)}) %collective-permute-start.5) | collective-permute-done | bytes 524320 | tf_op jit(solution)/shard_map/ppermute | solution.py:446
  30.2 3.3 %collective-permute-start.4 = (bf16[256,1024]{1,0:T(8,128)(2,1)S(1)}, bf16[256,1024]{1,0:T(8,128)(2,1)S(1)}, u32[]{:S(2)}, u32[]{:S(2)}) collective-permute-start(bf16[256,1024]{1,0:T(8,128)(2,1)S(1)} %add_convert_fusion.refs_4_.refs_0_), channel_id=1, source_target_pairs={{0,2},{2,0},{1,3},{3,1},{4,6},{6,4},{5,7},{7,5},{8,10},{10,8},{9,1... | collective-permute-start | bytes 1572872 | tf_op jit(solution)/shard_map/ppermute | solution.py:446
  33.5 2.8 %shard_map.145 = (f32[256,512]{1,0:T(8,128)S(1)}, f32[256,512]{1,0:T(8,128)S(1)}) custom-call(bf16[256,1024]{1,0:T(8,128)(2,1)S(1)} %shard_map.144.refs_0_, bf16[256,1024]{1,0:T(8,128)(2,1)S(1)} %collective-permute-done.6.refs_1_, bf16[512,2048]{1,0:T(8,128)(2,1)S(1)} %get-tuple-element.61.refs_1_.refs_8_.refs_2_, ...), custom_call_target="tpu_custom_call" | custom-call | flops 872415232 | bytes 6291456 | tf_op jit(solution)/shard_map/pallas_call | solution.py:48
  36.3 9.7 %collective-permute-done.4.refs_1_ = bf16[256,1024]{1,0:T(8,128)(2,1)S(1)} collective-permute-done((bf16[256,1024]{1,0:T(8,128)(2,1)S(1)}, bf16[256,1024]{1,0:T(8,128)(2,1)S(1)}, u32[]{:S(2)}, u32[]{:S(2)}) %collective-permute-start.4) | collective-permute-done | bytes 524320 | tf_op jit(solution)/shard_map/ppermute | solution.py:446
  46.3 2.0 %collective-permute-start = (bf16[512,256]{1,0:T(8,128)(2,1)S(1)}, bf16[512,256]{1,0:T(8,128)(2,1)S(1)}, u32[]{:S(2)}, u32[]{:S(2)}) collective-permute-start(bf16[512,256]{1,0:T(8,128)(2,1)S(1)} %get-tuple-element.55), channel_id=1, source_target_pairs={{0,8},{8,16},{16,24},{24,0},{1,9},{9,17},{17,25},{25,1},{2,10},{10... | collective-permute-start | bytes 786440 | tf_op jit(solution)/shard_map/ppermute | solution.py:446
  48.3 2.4 %collective-permute-start.1 = (bf16[512,256]{1,0:T(8,128)(2,1)S(1)}, bf16[512,256]{1,0:T(8,128)(2,1)S(1)}, u32[]{:S(2)}, u32[]{:S(2)}) collective-permute-start(bf16[512,256]{1,0:T(8,128)(2,1)S(1)} %get-tuple-element.56), channel_id=1, source_target_pairs={{0,24},{8,0},{16,8},{24,16},{1,25},{9,1},{17,9},{25,17},{2,26},{10... | collective-permute-start | bytes 786440 | tf_op jit(solution)/shard_map/ppermute | solution.py:446
  51.2 2.0 %shard_map.148 = (bf16[256,640]{1,0:T(8,128)(2,1)S(1)}, bf16[256,384]{1,0:T(8,128)(2,1)S(1)}, f32[16,128]{1,0:T(8,128)S(1)}) custom-call(f32[256,512]{1,0:T(8,128)S(1)} %shard_map.147.refs_0_, bf16[256,1024]{1,0:T(8,128)(2,1)S(1)} %collective-permute-done.7.refs_1_, bf16[512,2048]{1,0:T(8,128)(2,1)S(1)} %get-tuple-element.61.refs_1_.refs_8_.refs_2_, ...), custom_call_target="tpu_custom_call" | custom-call | flops 738197504 | bytes 6291456 | tf_op jit(solution)/shard_map/pallas_call | solution.py:48
  53.2 3.2 %collective-permute-start.9 = (bf16[256,640]{1,0:T(8,128)(2,1)S(1)}, bf16[256,640]{1,0:T(8,128)(2,1)S(1)}, u32[]{:S(2)}, u32[]{:S(2)}) collective-permute-start(bf16[256,640]{1,0:T(8,128)(2,1)S(1)} %get-tuple-element.74.refs_3_), channel_id=1, source_target_pairs={{0,24},{8,0},{16,8},{24,16},{1,25},{9,1},{17,9},{25,17},{2,26},{10... | collective-permute-start | bytes 983048 | tf_op jit(solution)/shard_map/ppermute | solution.py:446
  57.6 1.5 %collective-permute-start.16 = (bf16[512,256]{1,0:T(8,128)(2,1)S(1)}, bf16[512,256]{1,0:T(8,128)(2,1)S(1)}, u32[]{:S(2)}, u32[]{:S(2)}) collective-permute-start(bf16[512,256]{1,0:T(8,128)(2,1)S(1)} %get-tuple-element.84), channel_id=1, source_target_pairs={{0,32},{32,64},{64,96},{96,0},{1,33},{33,65},{65,97},{97,1},{2,34}... | collective-permute-start | bytes 786440 | tf_op jit(solution)/shard_map/ppermute | solution.py:446
  59.1 3.5 %collective-permute-start.10 = (bf16[512,256]{1,0:T(8,128)(2,1)S(1)}, bf16[512,256]{1,0:T(8,128)(2,1)S(1)}, u32[]{:S(2)}, u32[]{:S(2)}) collective-permute-start(bf16[512,256]{1,0:T(8,128)(2,1)S(1)} %get-tuple-element.75), channel_id=1, source_target_pairs={{0,16},{8,24},{16,0},{24,8},{1,17},{9,25},{17,1},{25,9},{2,18},{10... | collective-permute-start | bytes 786440 | tf_op jit(solution)/shard_map/ppermute | solution.py:446
  62.6 5.0 %collective-permute-done.16.refs_1_ = bf16[512,256]{1,0:T(8,128)(2,1)S(1)} collective-permute-done((bf16[512,256]{1,0:T(8,128)(2,1)S(1)}, bf16[512,256]{1,0:T(8,128)(2,1)S(1)}, u32[]{:S(2)}, u32[]{:S(2)}) %collective-permute-start.16) | collective-permute-done | bytes 262176 | tf_op jit(solution)/shard_map/ppermute | solution.py:446
  67.5 3.2 %collective-permute-start.18 = (f32[16,128]{1,0:T(8,128)S(1)}, f32[16,128]{1,0:T(8,128)S(1)}, u32[]{:S(2)}, u32[]{:S(2)}) collective-permute-start(f32[16,128]{1,0:T(8,128)S(1)} %add.11.refs_1_), channel_id=1, source_target_pairs={{0,2},{2,0},{1,3},{3,1},{4,6},{6,4},{5,7},{7,5},{8,10},{10,8},{9,1... | collective-permute-start | bytes 24584 | tf_op jit(solution)/shard_map/ppermute | solution.py:446
  70.7 7.4 %collective-permute-done.10.refs_1_ = bf16[512,256]{1,0:T(8,128)(2,1)S(1)} collective-permute-done((bf16[512,256]{1,0:T(8,128)(2,1)S(1)}, bf16[512,256]{1,0:T(8,128)(2,1)S(1)}, u32[]{:S(2)}, u32[]{:S(2)}) %collective-permute-start.10) | collective-permute-done | bytes 262176 | tf_op jit(solution)/shard_map/ppermute | solution.py:446
  78.2 3.0 %collective-permute-start.20 = (bf16[512,256]{1,0:T(8,128)(2,1)S(1)}, bf16[512,256]{1,0:T(8,128)(2,1)S(1)}, u32[]{:S(2)}, u32[]{:S(2)}) collective-permute-start(bf16[512,256]{1,0:T(8,128)(2,1)S(1)} %get-tuple-element.88), channel_id=1, source_target_pairs={{0,64},{32,96},{64,0},{96,32},{1,65},{33,97},{65,1},{97,33},{2,66}... | collective-permute-start | bytes 786440 | tf_op jit(solution)/shard_map/ppermute | solution.py:446
  81.2 1.1 collective-permute-start.21
  82.4 1.0 collective-permute-start.19
  84.1 2.5 %collective-permute-start.23 = (bf16[272,384]{1,0:T(8,128)(2,1)S(1)}, bf16[272,384]{1,0:T(8,128)(2,1)S(1)}, u32[]{:S(2)}, u32[]{:S(2)}) collective-permute-start(bf16[272,384]{1,0:T(8,128)(2,1)S(1)} %get-tuple-element.87.refs_2_), channel_id=1, source_target_pairs={{0,96},{32,0},{64,32},{96,64},{1,97},{33,1},{65,33},{97,65},{2,98}... | collective-permute-start | bytes 626696 | tf_op jit(solution)/shard_map/ppermute | solution.py:446
  87.8 5.6 %collective-permute-done.19.refs_3_ = bf16[272,384]{1,0:T(8,128)(2,1)S(1)} collective-permute-done((bf16[272,384]{1,0:T(8,128)(2,1)S(1)}, bf16[272,384]{1,0:T(8,128)(2,1)S(1)}, u32[]{:S(2)}, u32[]{:S(2)}) %collective-permute-start.19) | collective-permute-done | bytes 208928 | tf_op jit(solution)/shard_map/ppermute | solution.py:446
  94.6 1.8 %collective-permute-done.22.refs_4_ = bf16[272,384]{1,0:T(8,128)(2,1)S(1)} collective-permute-done((bf16[272,384]{1,0:T(8,128)(2,1)S(1)}, bf16[272,384]{1,0:T(8,128)(2,1)S(1)}, u32[]{:S(2)}, u32[]{:S(2)}) %collective-permute-start.22) | collective-permute-done | bytes 208928 | tf_op jit(solution)/shard_map/ppermute | solution.py:446
  96.4 5.8 %collective-permute-done.23.refs_5_ = bf16[272,384]{1,0:T(8,128)(2,1)S(1)} collective-permute-done((bf16[272,384]{1,0:T(8,128)(2,1)S(1)}, bf16[272,384]{1,0:T(8,128)(2,1)S(1)}, u32[]{:S(2)}, u32[]{:S(2)}) %collective-permute-start.23) | collective-permute-done | bytes 208928 | tf_op jit(solution)/shard_map/ppermute | solution.py:446
  102.6 1.7 %collective-permute-start.24 = (bf16[272,384]{1,0:T(8,128)(2,1)S(1)}, bf16[272,384]{1,0:T(8,128)(2,1)S(1)}, u32[]{:S(2)}, u32[]{:S(2)}) collective-permute-start(bf16[272,384]{1,0:T(8,128)(2,1)S(1)} %get-tuple-element.92), channel_id=1, source_target_pairs={{0,4},{4,0},{1,5},{5,1},{2,6},{6,2},{3,7},{7,3},{8,12},{12,8},{9,1... | collective-permute-start | bytes 626696 | tf_op jit(solution)/shard_map/ppermute | solution.py:446
  104.3 1.3 %collective-permute-start.12 = (bf16[128,640]{1,0:T(8,128)(2,1)S(1)}, bf16[128,640]{1,0:T(8,128)(2,1)S(1)}, u32[]{:S(2)}, u32[]{:S(2)}) collective-permute-start(bf16[128,640]{1,0:T(8,128)(2,1)S(1)} %get-tuple-element.77), channel_id=1, source_target_pairs={{0,32},{32,64},{64,96},{96,0},{1,33},{33,65},{65,97},{97,1},{2,34}... | collective-permute-start | bytes 491528 | tf_op jit(solution)/shard_map/ppermute | solution.py:446
  105.6 2.7 %collective-permute-start.13 = (bf16[128,640]{1,0:T(8,128)(2,1)S(1)}, bf16[128,640]{1,0:T(8,128)(2,1)S(1)}, u32[]{:S(2)}, u32[]{:S(2)}) collective-permute-start(bf16[128,640]{1,0:T(8,128)(2,1)S(1)} %get-tuple-element.78), channel_id=1, source_target_pairs={{0,64},{32,96},{64,0},{96,32},{1,65},{33,97},{65,1},{97,33},{2,66}... | collective-permute-start | bytes 491528 | tf_op jit(solution)/shard_map/ppermute | solution.py:446
  108.9 2.1 %collective-permute-done.12.refs_1_ = bf16[128,640]{1,0:T(8,128)(2,1)S(1)} collective-permute-done((bf16[128,640]{1,0:T(8,128)(2,1)S(1)}, bf16[128,640]{1,0:T(8,128)(2,1)S(1)}, u32[]{:S(2)}, u32[]{:S(2)}) %collective-permute-start.12) | collective-permute-done | bytes 163872 | tf_op jit(solution)/shard_map/ppermute | solution.py:446
  111.0 4.6 %collective-permute-done.13.refs_2_ = bf16[128,640]{1,0:T(8,128)(2,1)S(1)} collective-permute-done((bf16[128,640]{1,0:T(8,128)(2,1)S(1)}, bf16[128,640]{1,0:T(8,128)(2,1)S(1)}, u32[]{:S(2)}, u32[]{:S(2)}) %collective-permute-start.13) | collective-permute-done | bytes 163872 | tf_op jit(solution)/shard_map/ppermute | solution.py:446
  117.3 1.6 %collective-permute-start.26 = (bf16[80,384]{1,0:T(8,128)(2,1)S(1)}, bf16[80,384]{1,0:T(8,128)(2,1)S(1)}, u32[]{:S(2)}, u32[]{:S(2)}) collective-permute-start(bf16[80,384]{1,0:T(8,128)(2,1)S(1)} %get-tuple-element.96), channel_id=1, source_target_pairs={{0,16},{8,24},{16,0},{24,8},{1,17},{9,25},{17,1},{25,9},{2,18},{10... | collective-permute-start | bytes 184328 | tf_op jit(solution)/shard_map/ppermute | solution.py:446
  118.9 1.2 collective-permute-start.27
  120.0 1.8 %collective-permute-done.25.refs_1_ = bf16[80,384]{1,0:T(8,128)(2,1)S(1)} collective-permute-done((bf16[80,384]{1,0:T(8,128)(2,1)S(1)}, bf16[80,384]{1,0:T(8,128)(2,1)S(1)}, u32[]{:S(2)}, u32[]{:S(2)}) %collective-permute-start.25) | collective-permute-done | bytes 61472 | tf_op jit(solution)/shard_map/ppermute | solution.py:446
  121.9 1.2 collective-permute-done.26.refs_2_
  (58 shorter events, 12.6 us)
Async XLA Ops:
  0.6 6.6 %copy-start.3 = (s32[1,2048]{1,0:T(1,128)S(1)}, s32[1,2048]{1,0:T(1,128)}, u32[]{:S(2)}) copy-start(s32[1,2048]{1,0:T(1,128)} %refs_1_.4) | copy-start | bytes 24580
  7.1 2.0 %collective-permute-start.2 = (bf16[256,1024]{1,0:T(8,128)(2,1)S(1)}, bf16[256,1024]{1,0:T(8,128)(2,1)S(1)}, u32[]{:S(2)}, u32[]{:S(2)}) collective-permute-start(bf16[256,1024]{1,0:T(8,128)(2,1)S(1)} %get-tuple-element.63), channel_id=1, source_target_pairs={{0,1},{1,0},{2,3},{3,2},{4,5},{5,4},{6,7},{7,6},{8,9},{9,8},{10,11... | collective-permute-start | bytes 1572872 | tf_op jit(solution)/shard_map/ppermute | solution.py:446
  9.3 8.1 %copy-start = (bf16[256,2048]{1,0:T(8,128)(2,1)S(1)}, bf16[256,2048]{1,0:T(8,128)(2,1)}, u32[]{:S(2)}) copy-start(bf16[256,2048]{1,0:T(8,128)(2,1)} %refs_0_.3) | copy-start | bytes 3145732
  9.3 8.1 %copy-start.2 = (bf16[256,2048]{1,0:T(8,128)(2,1)S(1)}, bf16[256,2048]{1,0:T(8,128)(2,1)}, u32[]{:S(2)}) copy-start(bf16[256,2048]{1,0:T(8,128)(2,1)} %refs_1_.5) | copy-start | bytes 3145732
  9.3 8.1 %copy-start.5 = (f32[256]{0:T(256)S(1)}, f32[256]{0:T(256)}, u32[]{:S(2)}) copy-start(f32[256]{0:T(256)} %param.14) | copy-start | bytes 3076
  13.9 3.9 %collective-permute-start.3 = (bf16[256,1024]{1,0:T(8,128)(2,1)S(1)}, bf16[256,1024]{1,0:T(8,128)(2,1)S(1)}, u32[]{:S(2)}, u32[]{:S(2)}) collective-permute-start(bf16[256,1024]{1,0:T(8,128)(2,1)S(1)} %get-tuple-element.65), channel_id=1, source_target_pairs={{0,1},{1,0},{2,3},{3,2},{4,5},{5,4},{6,7},{7,6},{8,9},{9,8},{10,11... | collective-permute-start | bytes 1572872 | tf_op jit(solution)/shard_map/ppermute | solution.py:446
  14.1 15.8 %collective-permute-start.5 = (bf16[256,1024]{1,0:T(8,128)(2,1)S(1)}, bf16[256,1024]{1,0:T(8,128)(2,1)S(1)}, u32[]{:S(2)}, u32[]{:S(2)}) collective-permute-start(bf16[256,1024]{1,0:T(8,128)(2,1)S(1)} %add_convert_fusion.1.refs_9_.refs_0_), channel_id=1, source_target_pairs={{0,2},{2,0},{1,3},{3,1},{4,6},{6,4},{5,7},{7,5},{8,10},{10,8},{9,1... | collective-permute-start | bytes 1572872 | tf_op jit(solution)/shard_map/ppermute | solution.py:446
  30.1 3.4 %collective-permute-start.6 = (bf16[256,1024]{1,0:T(8,128)(2,1)S(1)}, bf16[256,1024]{1,0:T(8,128)(2,1)S(1)}, u32[]{:S(2)}, u32[]{:S(2)}) collective-permute-start(bf16[256,1024]{1,0:T(8,128)(2,1)S(1)} %shard_map.144.refs_0_), channel_id=1, source_target_pairs={{0,1},{1,0},{2,3},{3,2},{4,5},{5,4},{6,7},{7,6},{8,9},{9,8},{10,11... | collective-permute-start | bytes 1572872 | tf_op jit(solution)/shard_map/ppermute | solution.py:446
  30.2 15.8 %collective-permute-start.4 = (bf16[256,1024]{1,0:T(8,128)(2,1)S(1)}, bf16[256,1024]{1,0:T(8,128)(2,1)S(1)}, u32[]{:S(2)}, u32[]{:S(2)}) collective-permute-start(bf16[256,1024]{1,0:T(8,128)(2,1)S(1)} %add_convert_fusion.refs_4_.refs_0_), channel_id=1, source_target_pairs={{0,2},{2,0},{1,3},{3,1},{4,6},{6,4},{5,7},{7,5},{8,10},{10,8},{9,1... | collective-permute-start | bytes 1572872 | tf_op jit(solution)/shard_map/ppermute | solution.py:446
  46.2 5.0 %collective-permute-start.7 = (bf16[256,1024]{1,0:T(8,128)(2,1)S(1)}, bf16[256,1024]{1,0:T(8,128)(2,1)S(1)}, u32[]{:S(2)}, u32[]{:S(2)}) collective-permute-start(bf16[256,1024]{1,0:T(8,128)(2,1)S(1)} %shard_map.146.refs_0_), channel_id=1, source_target_pairs={{0,1},{1,0},{2,3},{3,2},{4,5},{5,4},{6,7},{7,6},{8,9},{9,8},{10,11... | collective-permute-start | bytes 1572872 | tf_op jit(solution)/shard_map/ppermute | solution.py:446
  46.3 11.3 %collective-permute-start = (bf16[512,256]{1,0:T(8,128)(2,1)S(1)}, bf16[512,256]{1,0:T(8,128)(2,1)S(1)}, u32[]{:S(2)}, u32[]{:S(2)}) collective-permute-start(bf16[512,256]{1,0:T(8,128)(2,1)S(1)} %get-tuple-element.55), channel_id=1, source_target_pairs={{0,8},{8,16},{16,24},{24,0},{1,9},{9,17},{17,25},{25,1},{2,10},{10... | collective-permute-start | bytes 786440 | tf_op jit(solution)/shard_map/ppermute | solution.py:446
  48.3 9.3 %collective-permute-start.1 = (bf16[512,256]{1,0:T(8,128)(2,1)S(1)}, bf16[512,256]{1,0:T(8,128)(2,1)S(1)}, u32[]{:S(2)}, u32[]{:S(2)}) collective-permute-start(bf16[512,256]{1,0:T(8,128)(2,1)S(1)} %get-tuple-element.56), channel_id=1, source_target_pairs={{0,24},{8,0},{16,8},{24,16},{1,25},{9,1},{17,9},{25,17},{2,26},{10... | collective-permute-start | bytes 786440 | tf_op jit(solution)/shard_map/ppermute | solution.py:446
  53.1 29.2 %collective-permute-start.8 = (bf16[256,640]{1,0:T(8,128)(2,1)S(1)}, bf16[256,640]{1,0:T(8,128)(2,1)S(1)}, u32[]{:S(2)}, u32[]{:S(2)}) collective-permute-start(bf16[256,640]{1,0:T(8,128)(2,1)S(1)} %get-tuple-element.74.refs_3_), channel_id=1, source_target_pairs={{0,8},{8,16},{16,24},{24,0},{1,9},{9,17},{17,25},{25,1},{2,10},{10... | collective-permute-start | bytes 983048 | tf_op jit(solution)/shard_map/ppermute | solution.py:446
  53.2 30.2 %collective-permute-start.9 = (bf16[256,640]{1,0:T(8,128)(2,1)S(1)}, bf16[256,640]{1,0:T(8,128)(2,1)S(1)}, u32[]{:S(2)}, u32[]{:S(2)}) collective-permute-start(bf16[256,640]{1,0:T(8,128)(2,1)S(1)} %get-tuple-element.74.refs_3_), channel_id=1, source_target_pairs={{0,24},{8,0},{16,8},{24,16},{1,25},{9,1},{17,9},{25,17},{2,26},{10... | collective-permute-start | bytes 983048 | tf_op jit(solution)/shard_map/ppermute | solution.py:446
  56.4 27.7 %collective-permute-start.11 = (bf16[256,640]{1,0:T(8,128)(2,1)S(1)}, bf16[256,640]{1,0:T(8,128)(2,1)S(1)}, u32[]{:S(2)}, u32[]{:S(2)}) collective-permute-start(bf16[256,640]{1,0:T(8,128)(2,1)S(1)} %get-tuple-element.74.refs_3_), channel_id=1, source_target_pairs={{0,16},{8,24},{16,0},{24,8},{1,17},{9,25},{17,1},{25,9},{2,18},{10... | collective-permute-start | bytes 983048 | tf_op jit(solution)/shard_map/ppermute | solution.py:446
  57.6 1.5 %collective-permute-start.17 = (f32[16,128]{1,0:T(8,128)S(1)}, f32[16,128]{1,0:T(8,128)S(1)}, u32[]{:S(2)}, u32[]{:S(2)}) collective-permute-start(f32[16,128]{1,0:T(8,128)S(1)} %get-tuple-element.86), channel_id=1, source_target_pairs={{0,1},{1,0},{2,3},{3,2},{4,5},{5,4},{6,7},{7,6},{8,9},{9,8},{10,11... | collective-permute-start | bytes 24584 | tf_op jit(solution)/shard_map/ppermute | solution.py:446
  57.6 9.9 %collective-permute-start.16 = (bf16[512,256]{1,0:T(8,128)(2,1)S(1)}, bf16[512,256]{1,0:T(8,128)(2,1)S(1)}, u32[]{:S(2)}, u32[]{:S(2)}) collective-permute-start(bf16[512,256]{1,0:T(8,128)(2,1)S(1)} %get-tuple-element.84), channel_id=1, source_target_pairs={{0,32},{32,64},{64,96},{96,0},{1,33},{33,65},{65,97},{97,1},{2,34}... | collective-permute-start | bytes 786440 | tf_op jit(solution)/shard_map/ppermute | solution.py:446
  59.1 19.1 %collective-permute-start.10 = (bf16[512,256]{1,0:T(8,128)(2,1)S(1)}, bf16[512,256]{1,0:T(8,128)(2,1)S(1)}, u32[]{:S(2)}, u32[]{:S(2)}) collective-permute-start(bf16[512,256]{1,0:T(8,128)(2,1)S(1)} %get-tuple-element.75), channel_id=1, source_target_pairs={{0,16},{8,24},{16,0},{24,8},{1,17},{9,25},{17,1},{25,9},{2,18},{10... | collective-permute-start | bytes 786440 | tf_op jit(solution)/shard_map/ppermute | solution.py:446
  67.5 13.7 %collective-permute-start.18 = (f32[16,128]{1,0:T(8,128)S(1)}, f32[16,128]{1,0:T(8,128)S(1)}, u32[]{:S(2)}, u32[]{:S(2)}) collective-permute-start(f32[16,128]{1,0:T(8,128)S(1)} %add.11.refs_1_), channel_id=1, source_target_pairs={{0,2},{2,0},{1,3},{3,1},{4,6},{6,4},{5,7},{7,5},{8,10},{10,8},{9,1... | collective-permute-start | bytes 24584 | tf_op jit(solution)/shard_map/ppermute | solution.py:446
  78.2 15.6 %collective-permute-start.20 = (bf16[512,256]{1,0:T(8,128)(2,1)S(1)}, bf16[512,256]{1,0:T(8,128)(2,1)S(1)}, u32[]{:S(2)}, u32[]{:S(2)}) collective-permute-start(bf16[512,256]{1,0:T(8,128)(2,1)S(1)} %get-tuple-element.88), channel_id=1, source_target_pairs={{0,64},{32,96},{64,0},{96,32},{1,65},{33,97},{65,1},{97,33},{2,66}... | collective-permute-start | bytes 786440 | tf_op jit(solution)/shard_map/ppermute | solution.py:446
  81.2 13.4 %collective-permute-start.21 = (bf16[512,256]{1,0:T(8,128)(2,1)S(1)}, bf16[512,256]{1,0:T(8,128)(2,1)S(1)}, u32[]{:S(2)}, u32[]{:S(2)}) collective-permute-start(bf16[512,256]{1,0:T(8,128)(2,1)S(1)} %get-tuple-element.89), channel_id=1, source_target_pairs={{0,96},{32,0},{64,32},{96,64},{1,97},{33,1},{65,33},{97,65},{2,98}... | collective-permute-start | bytes 786440 | tf_op jit(solution)/shard_map/ppermute | solution.py:446
  82.4 11.0 %collective-permute-start.19 = (bf16[272,384]{1,0:T(8,128)(2,1)S(1)}, bf16[272,384]{1,0:T(8,128)(2,1)S(1)}, u32[]{:S(2)}, u32[]{:S(2)}) collective-permute-start(bf16[272,384]{1,0:T(8,128)(2,1)S(1)} %get-tuple-element.87.refs_2_), channel_id=1, source_target_pairs={{0,32},{32,64},{64,96},{96,0},{1,33},{33,65},{65,97},{97,1},{2,34}... | collective-permute-start | bytes 626696 | tf_op jit(solution)/shard_map/ppermute | solution.py:446
  83.3 13.1 %collective-permute-start.22 = (bf16[272,384]{1,0:T(8,128)(2,1)S(1)}, bf16[272,384]{1,0:T(8,128)(2,1)S(1)}, u32[]{:S(2)}, u32[]{:S(2)}) collective-permute-start(bf16[272,384]{1,0:T(8,128)(2,1)S(1)} %get-tuple-element.87.refs_2_), channel_id=1, source_target_pairs={{0,64},{32,96},{64,0},{96,32},{1,65},{33,97},{65,1},{97,33},{2,66}... | collective-permute-start | bytes 626696 | tf_op jit(solution)/shard_map/ppermute | solution.py:446
  84.1 18.1 %collective-permute-start.23 = (bf16[272,384]{1,0:T(8,128)(2,1)S(1)}, bf16[272,384]{1,0:T(8,128)(2,1)S(1)}, u32[]{:S(2)}, u32[]{:S(2)}) collective-permute-start(bf16[272,384]{1,0:T(8,128)(2,1)S(1)} %get-tuple-element.87.refs_2_), channel_id=1, source_target_pairs={{0,96},{32,0},{64,32},{96,64},{1,97},{33,1},{65,33},{97,65},{2,98}... | collective-permute-start | bytes 626696 | tf_op jit(solution)/shard_map/ppermute | solution.py:446
  102.6 13.7 %collective-permute-start.24 = (bf16[272,384]{1,0:T(8,128)(2,1)S(1)}, bf16[272,384]{1,0:T(8,128)(2,1)S(1)}, u32[]{:S(2)}, u32[]{:S(2)}) collective-permute-start(bf16[272,384]{1,0:T(8,128)(2,1)S(1)} %get-tuple-element.92), channel_id=1, source_target_pairs={{0,4},{4,0},{1,5},{5,1},{2,6},{6,2},{3,7},{7,3},{8,12},{12,8},{9,1... | collective-permute-start | bytes 626696 | tf_op jit(solution)/shard_map/ppermute | solution.py:446
  104.3 6.7 %collective-permute-start.12 = (bf16[128,640]{1,0:T(8,128)(2,1)S(1)}, bf16[128,640]{1,0:T(8,128)(2,1)S(1)}, u32[]{:S(2)}, u32[]{:S(2)}) collective-permute-start(bf16[128,640]{1,0:T(8,128)(2,1)S(1)} %get-tuple-element.77), channel_id=1, source_target_pairs={{0,32},{32,64},{64,96},{96,0},{1,33},{33,65},{65,97},{97,1},{2,34}... | collective-permute-start | bytes 491528 | tf_op jit(solution)/shard_map/ppermute | solution.py:446
  105.6 10.1 %collective-permute-start.13 = (bf16[128,640]{1,0:T(8,128)(2,1)S(1)}, bf16[128,640]{1,0:T(8,128)(2,1)S(1)}, u32[]{:S(2)}, u32[]{:S(2)}) collective-permute-start(bf16[128,640]{1,0:T(8,128)(2,1)S(1)} %get-tuple-element.78), channel_id=1, source_target_pairs={{0,64},{32,96},{64,0},{96,32},{1,65},{33,97},{65,1},{97,33},{2,66}... | collective-permute-start | bytes 491528 | tf_op jit(solution)/shard_map/ppermute | solution.py:446
  108.4 7.3 %collective-permute-start.14 = (bf16[128,640]{1,0:T(8,128)(2,1)S(1)}, bf16[128,640]{1,0:T(8,128)(2,1)S(1)}, u32[]{:S(2)}, u32[]{:S(2)}) collective-permute-start(bf16[128,640]{1,0:T(8,128)(2,1)S(1)} %get-tuple-element.79), channel_id=1, source_target_pairs={{0,96},{32,0},{64,32},{96,64},{1,97},{33,1},{65,33},{97,65},{2,98}... | collective-permute-start | bytes 491528 | tf_op jit(solution)/shard_map/ppermute | solution.py:446
  115.8 8.3 %collective-permute-start.15 = (bf16[64,640]{1,0:T(8,128)(2,1)S(1)}, bf16[64,640]{1,0:T(8,128)(2,1)S(1)}, u32[]{:S(2)}, u32[]{:S(2)}) collective-permute-start(bf16[64,640]{1,0:T(8,128)(2,1)S(1)} %get-tuple-element.81), channel_id=1, source_target_pairs={{0,4},{4,0},{1,5},{5,1},{2,6},{6,2},{3,7},{7,3},{8,12},{12,8},{9,1... | collective-permute-start | bytes 245768 | tf_op jit(solution)/shard_map/ppermute | solution.py:446
  116.3 5.5 %collective-permute-start.25 = (bf16[80,384]{1,0:T(8,128)(2,1)S(1)}, bf16[80,384]{1,0:T(8,128)(2,1)S(1)}, u32[]{:S(2)}, u32[]{:S(2)}) collective-permute-start(bf16[80,384]{1,0:T(8,128)(2,1)S(1)} %get-tuple-element.95), channel_id=1, source_target_pairs={{0,8},{8,16},{16,24},{24,0},{1,9},{9,17},{17,25},{25,1},{2,10},{10... | collective-permute-start | bytes 184328 | tf_op jit(solution)/shard_map/ppermute | solution.py:446
  117.3 5.7 %collective-permute-start.26 = (bf16[80,384]{1,0:T(8,128)(2,1)S(1)}, bf16[80,384]{1,0:T(8,128)(2,1)S(1)}, u32[]{:S(2)}, u32[]{:S(2)}) collective-permute-start(bf16[80,384]{1,0:T(8,128)(2,1)S(1)} %get-tuple-element.96), channel_id=1, source_target_pairs={{0,16},{8,24},{16,0},{24,8},{1,17},{9,25},{17,1},{25,9},{2,18},{10... | collective-permute-start | bytes 184328 | tf_op jit(solution)/shard_map/ppermute | solution.py:446
  118.9 4.5 %collective-permute-start.27 = (bf16[80,384]{1,0:T(8,128)(2,1)S(1)}, bf16[80,384]{1,0:T(8,128)(2,1)S(1)}, u32[]{:S(2)}, u32[]{:S(2)}) collective-permute-start(bf16[80,384]{1,0:T(8,128)(2,1)S(1)} %get-tuple-element.97), channel_id=1, source_target_pairs={{0,24},{8,0},{16,8},{24,16},{1,25},{9,1},{17,9},{25,17},{2,26},{10... | collective-permute-start | bytes 184328 | tf_op jit(solution)/shard_map/ppermute | solution.py:446
  (2 other events, 3.1 us)

commit v6 on v5

--- a/solution.py
+++ b/solution.py
@@ -121,14 +121,19 @@
     sources = (tok_hbm, gain_hbm, wq_hbm, wk_hbm, table_hbm, seg_hbm, wv_hbm, wo_hbm)
     places = (tok, gain, wq, wk, table, seg, wv, wo)
     copies = [pltpu.make_async_copy(s, d, sems.at[i]) for i, (s, d) in enumerate(zip(sources, places))]
-    for copy in copies[:3]:
-        copy.start()
+    for i in (5, 0, 1, 2):
+        copies[i].start()
     length = tok.shape[0]
     heads = q_out.shape[1] // HEAD_DIM
     half = send_out.shape[1]
+    copies[5].wait()
+    document = jnp.broadcast_to(seg[...].astype(f32), (length, length))
+    row = lax.broadcasted_iota(i32, (length, length), 0)
+    col = lax.broadcasted_iota(i32, (length, length), 1)
+    allowed = (row >= col) & (document == document.T)
     copies[0].wait()
-    for copy in copies[3:]:
-        copy.start()
+    for i in (3, 4, 6, 7):
+        copies[i].start()
     copies[1].wait()
     tokens = tok[...].astype(f32)
     inverse = lax.rsqrt(jnp.mean(tokens * tokens, axis=1, keepdims=True) + EPSILON)
@@ -138,14 +143,10 @@
     query = dot(normed, wq[...])
     copies[3].wait()
     keys = dot(normed, wk[...])
-    for copy in copies[4:7]:
-        copy.wait()
+    copies[4].wait()
+    copies[6].wait()
     values = dot(normed, wv[...]).astype(bf16)
     v_out[...] = values
-    document = jnp.broadcast_to(seg[...].astype(f32), (length, length))
-    row = lax.broadcasted_iota(i32, (length, length), 0)
-    col = lax.broadcasted_iota(i32, (length, length), 1)
-    allowed = (row >= col) & (document == document.T)
     attended = []
     for h in range(heads):
         q = rotate(query[:, head(h)], table[:length], table[length:])

time: 125 us -> 125 us (level)
  no operation moved by 1% of the time
where the time goes in v6:
time: 125 us
  waiting for transfers between devices  59.8 us (48%)
  starting transfers between devices  42.2 us (34%)
  Pallas kernels  21.5 us (17%)
    ppermute x28, waiting for transfers between devices, flip(): lax.ppermute(value, axes if len(axes) > 1 else axes[0], [(i, target(i)) f...  59.8 us
    ppermute x28, starting transfers between devices, flip(): lax.ppermute(value, axes if len(axes) > 1 else axes[0], [(i, target(i)) f...  42.2 us
    pallas_call x19, Pallas kernels, run(): return kernel(*args, *after)  21.5 us
  transfers between devices with their start and end apart: 28, of which 15 were waited for; matrix products, arithmetic and copies ran while one was open for 0% of the time, Pallas kernels for 7%

profile of v6, /device:TPU:0, one launch (start us, length us, event | category | flops | bytes accessed | tf_op | source)
XLA Modules:
  0.0 124.8 jit_solution(3507564417754869118)
XLA Ops:
  0.6 6.5 %shard_map.139 = (bf16[256,2048]{1,0:T(8,128)(2,1)S(1)}, bf16[256,512]{1,0:T(8,128)(2,1)S(1)}, bf16[256,512]{1,0:T(8,128)(2,1)S(1)}, bf16[256,512]{1,0:T(8,128)(...) custom-call(bf16[256,2048]{1,0:T(8,128)(2,1)} %refs_0_.3, ...), custom_call_target="tpu_custom_call" | custom-call | flops 2415919104 | bytes 12582912 | tf_op jit(solution)/shard_map/pallas_call | solution.py:48
  9.3 4.5 %shard_map.142 = (bf16[256,512]{1,0:T(8,128)(2,1)S(1)}, bf16[256,512]{1,0:T(8,128)(2,1)S(1)}, f32[256,512]{1,0:T(8,128)S(1)}, f32[4,256,256]{2,1,0:T(8,128)S(1)}...) custom-call(bf16[256,2048]{1,0:T(8,128)(2,1)S(1)} %get-tuple-element.53.refs_0_, s32[1,2048]{1,0:T(1,128)S(1)} %copy-done.3, ...), custom_call_target="tpu_custom_call" | custom-call | flops 1342177280 | bytes 8388608 | tf_op jit(solution)/shard_map/pallas_call | solution.py:48
  14.1 3.3 %collective-permute-start.5 = (bf16[256,1024]{1,0:T(8,128)(2,1)S(1)}, bf16[256,1024]{1,0:T(8,128)(2,1)S(1)}, u32[]{:S(2)}, u32[]{:S(2)}) collective-permute-start(bf16[256,1024]{1,0:T(8,128)(2,1)S(1)} %add_convert_fusion.1.refs_9_.refs_0_), channel_id=1, source_target_pairs={{0,2},{2,0},{1,3},{3,1},{4,6},{6,4},{5,7},{7,5},{8,10},{10,8},{9,1... | collective-permute-start | bytes 1572872 | tf_op jit(solution)/shard_map/ppermute | solution.py:447
  18.0 11.9 %collective-permute-done.5.refs_1_ = bf16[256,1024]{1,0:T(8,128)(2,1)S(1)} collective-permute-done((bf16[256,1024]{1,0:T(8,128)(2,1)S(1)}, bf16[256,1024]{1,0:T(8,128)(2,1)S(1)}, u32[]{:S(2)}, u32[]{:S(2)}) %collective-permute-start.5) | collective-permute-done | bytes 524320 | tf_op jit(solution)/shard_map/ppermute | solution.py:447
  30.2 3.3 %collective-permute-start.4 = (bf16[256,1024]{1,0:T(8,128)(2,1)S(1)}, bf16[256,1024]{1,0:T(8,128)(2,1)S(1)}, u32[]{:S(2)}, u32[]{:S(2)}) collective-permute-start(bf16[256,1024]{1,0:T(8,128)(2,1)S(1)} %add_convert_fusion.refs_4_.refs_0_), channel_id=1, source_target_pairs={{0,2},{2,0},{1,3},{3,1},{4,6},{6,4},{5,7},{7,5},{8,10},{10,8},{9,1... | collective-permute-start | bytes 1572872 | tf_op jit(solution)/shard_map/ppermute | solution.py:447
  33.5 2.8 %shard_map.145 = (f32[256,512]{1,0:T(8,128)S(1)}, f32[256,512]{1,0:T(8,128)S(1)}) custom-call(bf16[256,1024]{1,0:T(8,128)(2,1)S(1)} %shard_map.144.refs_0_, bf16[256,1024]{1,0:T(8,128)(2,1)S(1)} %collective-permute-done.6.refs_1_, bf16[512,2048]{1,0:T(8,128)(2,1)S(1)} %get-tuple-element.61.refs_1_.refs_8_.refs_2_, ...), custom_call_target="tpu_custom_call" | custom-call | flops 872415232 | bytes 6291456 | tf_op jit(solution)/shard_map/pallas_call | solution.py:48
  36.3 9.7 %collective-permute-done.4.refs_1_ = bf16[256,1024]{1,0:T(8,128)(2,1)S(1)} collective-permute-done((bf16[256,1024]{1,0:T(8,128)(2,1)S(1)}, bf16[256,1024]{1,0:T(8,128)(2,1)S(1)}, u32[]{:S(2)}, u32[]{:S(2)}) %collective-permute-start.4) | collective-permute-done | bytes 524320 | tf_op jit(solution)/shard_map/ppermute | solution.py:447
  46.3 2.0 %collective-permute-start = (bf16[512,256]{1,0:T(8,128)(2,1)S(1)}, bf16[512,256]{1,0:T(8,128)(2,1)S(1)}, u32[]{:S(2)}, u32[]{:S(2)}) collective-permute-start(bf16[512,256]{1,0:T(8,128)(2,1)S(1)} %get-tuple-element.55), channel_id=1, source_target_pairs={{0,8},{8,16},{16,24},{24,0},{1,9},{9,17},{17,25},{25,1},{2,10},{10... | collective-permute-start | bytes 786440 | tf_op jit(solution)/shard_map/ppermute | solution.py:447
  48.3 2.4 %collective-permute-start.1 = (bf16[512,256]{1,0:T(8,128)(2,1)S(1)}, bf16[512,256]{1,0:T(8,128)(2,1)S(1)}, u32[]{:S(2)}, u32[]{:S(2)}) collective-permute-start(bf16[512,256]{1,0:T(8,128)(2,1)S(1)} %get-tuple-element.56), channel_id=1, source_target_pairs={{0,24},{8,0},{16,8},{24,16},{1,25},{9,1},{17,9},{25,17},{2,26},{10... | collective-permute-start | bytes 786440 | tf_op jit(solution)/shard_map/ppermute | solution.py:447
  51.2 2.0 %shard_map.148 = (bf16[256,640]{1,0:T(8,128)(2,1)S(1)}, bf16[256,384]{1,0:T(8,128)(2,1)S(1)}, f32[16,128]{1,0:T(8,128)S(1)}) custom-call(f32[256,512]{1,0:T(8,128)S(1)} %shard_map.147.refs_0_, bf16[256,1024]{1,0:T(8,128)(2,1)S(1)} %collective-permute-done.7.refs_1_, bf16[512,2048]{1,0:T(8,128)(2,1)S(1)} %get-tuple-element.61.refs_1_.refs_8_.refs_2_, ...), custom_call_target="tpu_custom_call" | custom-call | flops 738197504 | bytes 6291456 | tf_op jit(solution)/shard_map/pallas_call | solution.py:48
  53.2 3.2 %collective-permute-start.9 = (bf16[256,640]{1,0:T(8,128)(2,1)S(1)}, bf16[256,640]{1,0:T(8,128)(2,1)S(1)}, u32[]{:S(2)}, u32[]{:S(2)}) collective-permute-start(bf16[256,640]{1,0:T(8,128)(2,1)S(1)} %get-tuple-element.74.refs_3_), channel_id=1, source_target_pairs={{0,24},{8,0},{16,8},{24,16},{1,25},{9,1},{17,9},{25,17},{2,26},{10... | collective-permute-start | bytes 983048 | tf_op jit(solution)/shard_map/ppermute | solution.py:447
  57.6 1.5 %collective-permute-start.16 = (bf16[512,256]{1,0:T(8,128)(2,1)S(1)}, bf16[512,256]{1,0:T(8,128)(2,1)S(1)}, u32[]{:S(2)}, u32[]{:S(2)}) collective-permute-start(bf16[512,256]{1,0:T(8,128)(2,1)S(1)} %get-tuple-element.84), channel_id=1, source_target_pairs={{0,32},{32,64},{64,96},{96,0},{1,33},{33,65},{65,97},{97,1},{2,34}... | collective-permute-start | bytes 786440 | tf_op jit(solution)/shard_map/ppermute | solution.py:447
  59.1 3.5 %collective-permute-start.10 = (bf16[512,256]{1,0:T(8,128)(2,1)S(1)}, bf16[512,256]{1,0:T(8,128)(2,1)S(1)}, u32[]{:S(2)}, u32[]{:S(2)}) collective-permute-start(bf16[512,256]{1,0:T(8,128)(2,1)S(1)} %get-tuple-element.75), channel_id=1, source_target_pairs={{0,16},{8,24},{16,0},{24,8},{1,17},{9,25},{17,1},{25,9},{2,18},{10... | collective-permute-start | bytes 786440 | tf_op jit(solution)/shard_map/ppermute | solution.py:447
  62.6 4.9 %collective-permute-done.16.refs_1_ = bf16[512,256]{1,0:T(8,128)(2,1)S(1)} collective-permute-done((bf16[512,256]{1,0:T(8,128)(2,1)S(1)}, bf16[512,256]{1,0:T(8,128)(2,1)S(1)}, u32[]{:S(2)}, u32[]{:S(2)}) %collective-permute-start.16) | collective-permute-done | bytes 262176 | tf_op jit(solution)/shard_map/ppermute | solution.py:447
  67.5 3.2 %collective-permute-start.18 = (f32[16,128]{1,0:T(8,128)S(1)}, f32[16,128]{1,0:T(8,128)S(1)}, u32[]{:S(2)}, u32[]{:S(2)}) collective-permute-start(f32[16,128]{1,0:T(8,128)S(1)} %add.11.refs_1_), channel_id=1, source_target_pairs={{0,2},{2,0},{1,3},{3,1},{4,6},{6,4},{5,7},{7,5},{8,10},{10,8},{9,1... | collective-permute-start | bytes 24584 | tf_op jit(solution)/shard_map/ppermute | solution.py:447
  70.7 7.4 %collective-permute-done.10.refs_1_ = bf16[512,256]{1,0:T(8,128)(2,1)S(1)} collective-permute-done((bf16[512,256]{1,0:T(8,128)(2,1)S(1)}, bf16[512,256]{1,0:T(8,128)(2,1)S(1)}, u32[]{:S(2)}, u32[]{:S(2)}) %collective-permute-start.10) | collective-permute-done | bytes 262176 | tf_op jit(solution)/shard_map/ppermute | solution.py:447
  78.2 3.0 %collective-permute-start.20 = (bf16[512,256]{1,0:T(8,128)(2,1)S(1)}, bf16[512,256]{1,0:T(8,128)(2,1)S(1)}, u32[]{:S(2)}, u32[]{:S(2)}) collective-permute-start(bf16[512,256]{1,0:T(8,128)(2,1)S(1)} %get-tuple-element.88), channel_id=1, source_target_pairs={{0,64},{32,96},{64,0},{96,32},{1,65},{33,97},{65,1},{97,33},{2,66}... | collective-permute-start | bytes 786440 | tf_op jit(solution)/shard_map/ppermute | solution.py:447
  81.2 1.1 collective-permute-start.21
  82.4 0.9 collective-permute-start.19
  84.1 2.5 %collective-permute-start.23 = (bf16[272,384]{1,0:T(8,128)(2,1)S(1)}, bf16[272,384]{1,0:T(8,128)(2,1)S(1)}, u32[]{:S(2)}, u32[]{:S(2)}) collective-permute-start(bf16[272,384]{1,0:T(8,128)(2,1)S(1)} %get-tuple-element.87.refs_2_), channel_id=1, source_target_pairs={{0,96},{32,0},{64,32},{96,64},{1,97},{33,1},{65,33},{97,65},{2,98}... | collective-permute-start | bytes 626696 | tf_op jit(solution)/shard_map/ppermute | solution.py:447
  87.8 5.6 %collective-permute-done.19.refs_3_ = bf16[272,384]{1,0:T(8,128)(2,1)S(1)} collective-permute-done((bf16[272,384]{1,0:T(8,128)(2,1)S(1)}, bf16[272,384]{1,0:T(8,128)(2,1)S(1)}, u32[]{:S(2)}, u32[]{:S(2)}) %collective-permute-start.19) | collective-permute-done | bytes 208928 | tf_op jit(solution)/shard_map/ppermute | solution.py:447
  94.6 1.8 %collective-permute-done.22.refs_4_ = bf16[272,384]{1,0:T(8,128)(2,1)S(1)} collective-permute-done((bf16[272,384]{1,0:T(8,128)(2,1)S(1)}, bf16[272,384]{1,0:T(8,128)(2,1)S(1)}, u32[]{:S(2)}, u32[]{:S(2)}) %collective-permute-start.22) | collective-permute-done | bytes 208928 | tf_op jit(solution)/shard_map/ppermute | solution.py:447
  96.4 5.8 %collective-permute-done.23.refs_5_ = bf16[272,384]{1,0:T(8,128)(2,1)S(1)} collective-permute-done((bf16[272,384]{1,0:T(8,128)(2,1)S(1)}, bf16[272,384]{1,0:T(8,128)(2,1)S(1)}, u32[]{:S(2)}, u32[]{:S(2)}) %collective-permute-start.23) | collective-permute-done | bytes 208928 | tf_op jit(solution)/shard_map/ppermute | solution.py:447
  102.6 1.7 %collective-permute-start.24 = (bf16[272,384]{1,0:T(8,128)(2,1)S(1)}, bf16[272,384]{1,0:T(8,128)(2,1)S(1)}, u32[]{:S(2)}, u32[]{:S(2)}) collective-permute-start(bf16[272,384]{1,0:T(8,128)(2,1)S(1)} %get-tuple-element.92), channel_id=1, source_target_pairs={{0,4},{4,0},{1,5},{5,1},{2,6},{6,2},{3,7},{7,3},{8,12},{12,8},{9,1... | collective-permute-start | bytes 626696 | tf_op jit(solution)/shard_map/ppermute | solution.py:447
  104.3 1.3 %collective-permute-start.12 = (bf16[128,640]{1,0:T(8,128)(2,1)S(1)}, bf16[128,640]{1,0:T(8,128)(2,1)S(1)}, u32[]{:S(2)}, u32[]{:S(2)}) collective-permute-start(bf16[128,640]{1,0:T(8,128)(2,1)S(1)} %get-tuple-element.77), channel_id=1, source_target_pairs={{0,32},{32,64},{64,96},{96,0},{1,33},{33,65},{65,97},{97,1},{2,34}... | collective-permute-start | bytes 491528 | tf_op jit(solution)/shard_map/ppermute | solution.py:447
  105.6 2.7 %collective-permute-start.13 = (bf16[128,640]{1,0:T(8,128)(2,1)S(1)}, bf16[128,640]{1,0:T(8,128)(2,1)S(1)}, u32[]{:S(2)}, u32[]{:S(2)}) collective-permute-start(bf16[128,640]{1,0:T(8,128)(2,1)S(1)} %get-tuple-element.78), channel_id=1, source_target_pairs={{0,64},{32,96},{64,0},{96,32},{1,65},{33,97},{65,1},{97,33},{2,66}... | collective-permute-start | bytes 491528 | tf_op jit(solution)/shard_map/ppermute | solution.py:447
  108.9 2.1 %collective-permute-done.12.refs_1_ = bf16[128,640]{1,0:T(8,128)(2,1)S(1)} collective-permute-done((bf16[128,640]{1,0:T(8,128)(2,1)S(1)}, bf16[128,640]{1,0:T(8,128)(2,1)S(1)}, u32[]{:S(2)}, u32[]{:S(2)}) %collective-permute-start.12) | collective-permute-done | bytes 163872 | tf_op jit(solution)/shard_map/ppermute | solution.py:447
  111.0 4.6 %collective-permute-done.13.refs_2_ = bf16[128,640]{1,0:T(8,128)(2,1)S(1)} collective-permute-done((bf16[128,640]{1,0:T(8,128)(2,1)S(1)}, bf16[128,640]{1,0:T(8,128)(2,1)S(1)}, u32[]{:S(2)}, u32[]{:S(2)}) %collective-permute-start.13) | collective-permute-done | bytes 163872 | tf_op jit(solution)/shard_map/ppermute | solution.py:447
  117.3 1.6 %collective-permute-start.26 = (bf16[80,384]{1,0:T(8,128)(2,1)S(1)}, bf16[80,384]{1,0:T(8,128)(2,1)S(1)}, u32[]{:S(2)}, u32[]{:S(2)}) collective-permute-start(bf16[80,384]{1,0:T(8,128)(2,1)S(1)} %get-tuple-element.96), channel_id=1, source_target_pairs={{0,16},{8,24},{16,0},{24,8},{1,17},{9,25},{17,1},{25,9},{2,18},{10... | collective-permute-start | bytes 184328 | tf_op jit(solution)/shard_map/ppermute | solution.py:447
  118.9 1.2 collective-permute-start.27
  120.0 1.8 %collective-permute-done.25.refs_1_ = bf16[80,384]{1,0:T(8,128)(2,1)S(1)} collective-permute-done((bf16[80,384]{1,0:T(8,128)(2,1)S(1)}, bf16[80,384]{1,0:T(8,128)(2,1)S(1)}, u32[]{:S(2)}, u32[]{:S(2)}) %collective-permute-start.25) | collective-permute-done | bytes 61472 | tf_op jit(solution)/shard_map/ppermute | solution.py:447
  121.9 1.2 collective-permute-done.26.refs_2_
  (58 shorter events, 12.6 us)
Async XLA Ops:
  0.6 6.6 %copy-start.3 = (s32[1,2048]{1,0:T(1,128)S(1)}, s32[1,2048]{1,0:T(1,128)}, u32[]{:S(2)}) copy-start(s32[1,2048]{1,0:T(1,128)} %refs_1_.4) | copy-start | bytes 24580
  7.1 2.0 %collective-permute-start.2 = (bf16[256,1024]{1,0:T(8,128)(2,1)S(1)}, bf16[256,1024]{1,0:T(8,128)(2,1)S(1)}, u32[]{:S(2)}, u32[]{:S(2)}) collective-permute-start(bf16[256,1024]{1,0:T(8,128)(2,1)S(1)} %get-tuple-element.63), channel_id=1, source_target_pairs={{0,1},{1,0},{2,3},{3,2},{4,5},{5,4},{6,7},{7,6},{8,9},{9,8},{10,11... | collective-permute-start | bytes 1572872 | tf_op jit(solution)/shard_map/ppermute | solution.py:447
  9.3 8.1 %copy-start = (bf16[256,2048]{1,0:T(8,128)(2,1)S(1)}, bf16[256,2048]{1,0:T(8,128)(2,1)}, u32[]{:S(2)}) copy-start(bf16[256,2048]{1,0:T(8,128)(2,1)} %refs_0_.3) | copy-start | bytes 3145732
  9.3 8.1 %copy-start.2 = (bf16[256,2048]{1,0:T(8,128)(2,1)S(1)}, bf16[256,2048]{1,0:T(8,128)(2,1)}, u32[]{:S(2)}) copy-start(bf16[256,2048]{1,0:T(8,128)(2,1)} %refs_1_.5) | copy-start | bytes 3145732
  9.3 8.1 %copy-start.5 = (f32[256]{0:T(256)S(1)}, f32[256]{0:T(256)}, u32[]{:S(2)}) copy-start(f32[256]{0:T(256)} %param.14) | copy-start | bytes 3076
  13.9 3.9 %collective-permute-start.3 = (bf16[256,1024]{1,0:T(8,128)(2,1)S(1)}, bf16[256,1024]{1,0:T(8,128)(2,1)S(1)}, u32[]{:S(2)}, u32[]{:S(2)}) collective-permute-start(bf16[256,1024]{1,0:T(8,128)(2,1)S(1)} %get-tuple-element.65), channel_id=1, source_target_pairs={{0,1},{1,0},{2,3},{3,2},{4,5},{5,4},{6,7},{7,6},{8,9},{9,8},{10,11... | collective-permute-start | bytes 1572872 | tf_op jit(solution)/shard_map/ppermute | solution.py:447
  14.1 15.8 %collective-permute-start.5 = (bf16[256,1024]{1,0:T(8,128)(2,1)S(1)}, bf16[256,1024]{1,0:T(8,128)(2,1)S(1)}, u32[]{:S(2)}, u32[]{:S(2)}) collective-permute-start(bf16[256,1024]{1,0:T(8,128)(2,1)S(1)} %add_convert_fusion.1.refs_9_.refs_0_), channel_id=1, source_target_pairs={{0,2},{2,0},{1,3},{3,1},{4,6},{6,4},{5,7},{7,5},{8,10},{10,8},{9,1... | collective-permute-start | bytes 1572872 | tf_op jit(solution)/shard_map/ppermute | solution.py:447
  30.1 3.4 %collective-permute-start.6 = (bf16[256,1024]{1,0:T(8,128)(2,1)S(1)}, bf16[256,1024]{1,0:T(8,128)(2,1)S(1)}, u32[]{:S(2)}, u32[]{:S(2)}) collective-permute-start(bf16[256,1024]{1,0:T(8,128)(2,1)S(1)} %shard_map.144.refs_0_), channel_id=1, source_target_pairs={{0,1},{1,0},{2,3},{3,2},{4,5},{5,4},{6,7},{7,6},{8,9},{9,8},{10,11... | collective-permute-start | bytes 1572872 | tf_op jit(solution)/shard_map/ppermute | solution.py:447
  30.2 15.8 %collective-permute-start.4 = (bf16[256,1024]{1,0:T(8,128)(2,1)S(1)}, bf16[256,1024]{1,0:T(8,128)(2,1)S(1)}, u32[]{:S(2)}, u32[]{:S(2)}) collective-permute-start(bf16[256,1024]{1,0:T(8,128)(2,1)S(1)} %add_convert_fusion.refs_4_.refs_0_), channel_id=1, source_target_pairs={{0,2},{2,0},{1,3},{3,1},{4,6},{6,4},{5,7},{7,5},{8,10},{10,8},{9,1... | collective-permute-start | bytes 1572872 | tf_op jit(solution)/shard_map/ppermute | solution.py:447
  46.2 5.0 %collective-permute-start.7 = (bf16[256,1024]{1,0:T(8,128)(2,1)S(1)}, bf16[256,1024]{1,0:T(8,128)(2,1)S(1)}, u32[]{:S(2)}, u32[]{:S(2)}) collective-permute-start(bf16[256,1024]{1,0:T(8,128)(2,1)S(1)} %shard_map.146.refs_0_), channel_id=1, source_target_pairs={{0,1},{1,0},{2,3},{3,2},{4,5},{5,4},{6,7},{7,6},{8,9},{9,8},{10,11... | collective-permute-start | bytes 1572872 | tf_op jit(solution)/shard_map/ppermute | solution.py:447
  46.3 11.3 %collective-permute-start = (bf16[512,256]{1,0:T(8,128)(2,1)S(1)}, bf16[512,256]{1,0:T(8,128)(2,1)S(1)}, u32[]{:S(2)}, u32[]{:S(2)}) collective-permute-start(bf16[512,256]{1,0:T(8,128)(2,1)S(1)} %get-tuple-element.55), channel_id=1, source_target_pairs={{0,8},{8,16},{16,24},{24,0},{1,9},{9,17},{17,25},{25,1},{2,10},{10... | collective-permute-start | bytes 786440 | tf_op jit(solution)/shard_map/ppermute | solution.py:447
  48.3 9.3 %collective-permute-start.1 = (bf16[512,256]{1,0:T(8,128)(2,1)S(1)}, bf16[512,256]{1,0:T(8,128)(2,1)S(1)}, u32[]{:S(2)}, u32[]{:S(2)}) collective-permute-start(bf16[512,256]{1,0:T(8,128)(2,1)S(1)} %get-tuple-element.56), channel_id=1, source_target_pairs={{0,24},{8,0},{16,8},{24,16},{1,25},{9,1},{17,9},{25,17},{2,26},{10... | collective-permute-start | bytes 786440 | tf_op jit(solution)/shard_map/ppermute | solution.py:447
  53.1 29.2 %collective-permute-start.8 = (bf16[256,640]{1,0:T(8,128)(2,1)S(1)}, bf16[256,640]{1,0:T(8,128)(2,1)S(1)}, u32[]{:S(2)}, u32[]{:S(2)}) collective-permute-start(bf16[256,640]{1,0:T(8,128)(2,1)S(1)} %get-tuple-element.74.refs_3_), channel_id=1, source_target_pairs={{0,8},{8,16},{16,24},{24,0},{1,9},{9,17},{17,25},{25,1},{2,10},{10... | collective-permute-start | bytes 983048 | tf_op jit(solution)/shard_map/ppermute | solution.py:447
  53.2 30.2 %collective-permute-start.9 = (bf16[256,640]{1,0:T(8,128)(2,1)S(1)}, bf16[256,640]{1,0:T(8,128)(2,1)S(1)}, u32[]{:S(2)}, u32[]{:S(2)}) collective-permute-start(bf16[256,640]{1,0:T(8,128)(2,1)S(1)} %get-tuple-element.74.refs_3_), channel_id=1, source_target_pairs={{0,24},{8,0},{16,8},{24,16},{1,25},{9,1},{17,9},{25,17},{2,26},{10... | collective-permute-start | bytes 983048 | tf_op jit(solution)/shard_map/ppermute | solution.py:447
  56.4 27.7 %collective-permute-start.11 = (bf16[256,640]{1,0:T(8,128)(2,1)S(1)}, bf16[256,640]{1,0:T(8,128)(2,1)S(1)}, u32[]{:S(2)}, u32[]{:S(2)}) collective-permute-start(bf16[256,640]{1,0:T(8,128)(2,1)S(1)} %get-tuple-element.74.refs_3_), channel_id=1, source_target_pairs={{0,16},{8,24},{16,0},{24,8},{1,17},{9,25},{17,1},{25,9},{2,18},{10... | collective-permute-start | bytes 983048 | tf_op jit(solution)/shard_map/ppermute | solution.py:447
  57.6 1.5 %collective-permute-start.17 = (f32[16,128]{1,0:T(8,128)S(1)}, f32[16,128]{1,0:T(8,128)S(1)}, u32[]{:S(2)}, u32[]{:S(2)}) collective-permute-start(f32[16,128]{1,0:T(8,128)S(1)} %get-tuple-element.86), channel_id=1, source_target_pairs={{0,1},{1,0},{2,3},{3,2},{4,5},{5,4},{6,7},{7,6},{8,9},{9,8},{10,11... | collective-permute-start | bytes 24584 | tf_op jit(solution)/shard_map/ppermute | solution.py:447
  57.6 9.9 %collective-permute-start.16 = (bf16[512,256]{1,0:T(8,128)(2,1)S(1)}, bf16[512,256]{1,0:T(8,128)(2,1)S(1)}, u32[]{:S(2)}, u32[]{:S(2)}) collective-permute-start(bf16[512,256]{1,0:T(8,128)(2,1)S(1)} %get-tuple-element.84), channel_id=1, source_target_pairs={{0,32},{32,64},{64,96},{96,0},{1,33},{33,65},{65,97},{97,1},{2,34}... | collective-permute-start | bytes 786440 | tf_op jit(solution)/shard_map/ppermute | solution.py:447
  59.1 19.1 %collective-permute-start.10 = (bf16[512,256]{1,0:T(8,128)(2,1)S(1)}, bf16[512,256]{1,0:T(8,128)(2,1)S(1)}, u32[]{:S(2)}, u32[]{:S(2)}) collective-permute-start(bf16[512,256]{1,0:T(8,128)(2,1)S(1)} %get-tuple-element.75), channel_id=1, source_target_pairs={{0,16},{8,24},{16,0},{24,8},{1,17},{9,25},{17,1},{25,9},{2,18},{10... | collective-permute-start | bytes 786440 | tf_op jit(solution)/shard_map/ppermute | solution.py:447
  67.5 13.7 %collective-permute-start.18 = (f32[16,128]{1,0:T(8,128)S(1)}, f32[16,128]{1,0:T(8,128)S(1)}, u32[]{:S(2)}, u32[]{:S(2)}) collective-permute-start(f32[16,128]{1,0:T(8,128)S(1)} %add.11.refs_1_), channel_id=1, source_target_pairs={{0,2},{2,0},{1,3},{3,1},{4,6},{6,4},{5,7},{7,5},{8,10},{10,8},{9,1... | collective-permute-start | bytes 24584 | tf_op jit(solution)/shard_map/ppermute | solution.py:447
  78.2 15.6 %collective-permute-start.20 = (bf16[512,256]{1,0:T(8,128)(2,1)S(1)}, bf16[512,256]{1,0:T(8,128)(2,1)S(1)}, u32[]{:S(2)}, u32[]{:S(2)}) collective-permute-start(bf16[512,256]{1,0:T(8,128)(2,1)S(1)} %get-tuple-element.88), channel_id=1, source_target_pairs={{0,64},{32,96},{64,0},{96,32},{1,65},{33,97},{65,1},{97,33},{2,66}... | collective-permute-start | bytes 786440 | tf_op jit(solution)/shard_map/ppermute | solution.py:447
  81.2 13.4 %collective-permute-start.21 = (bf16[512,256]{1,0:T(8,128)(2,1)S(1)}, bf16[512,256]{1,0:T(8,128)(2,1)S(1)}, u32[]{:S(2)}, u32[]{:S(2)}) collective-permute-start(bf16[512,256]{1,0:T(8,128)(2,1)S(1)} %get-tuple-element.89), channel_id=1, source_target_pairs={{0,96},{32,0},{64,32},{96,64},{1,97},{33,1},{65,33},{97,65},{2,98}... | collective-permute-start | bytes 786440 | tf_op jit(solution)/shard_map/ppermute | solution.py:447
  82.4 10.9 %collective-permute-start.19 = (bf16[272,384]{1,0:T(8,128)(2,1)S(1)}, bf16[272,384]{1,0:T(8,128)(2,1)S(1)}, u32[]{:S(2)}, u32[]{:S(2)}) collective-permute-start(bf16[272,384]{1,0:T(8,128)(2,1)S(1)} %get-tuple-element.87.refs_2_), channel_id=1, source_target_pairs={{0,32},{32,64},{64,96},{96,0},{1,33},{33,65},{65,97},{97,1},{2,34}... | collective-permute-start | bytes 626696 | tf_op jit(solution)/shard_map/ppermute | solution.py:447
  83.3 13.1 %collective-permute-start.22 = (bf16[272,384]{1,0:T(8,128)(2,1)S(1)}, bf16[272,384]{1,0:T(8,128)(2,1)S(1)}, u32[]{:S(2)}, u32[]{:S(2)}) collective-permute-start(bf16[272,384]{1,0:T(8,128)(2,1)S(1)} %get-tuple-element.87.refs_2_), channel_id=1, source_target_pairs={{0,64},{32,96},{64,0},{96,32},{1,65},{33,97},{65,1},{97,33},{2,66}... | collective-permute-start | bytes 626696 | tf_op jit(solution)/shard_map/ppermute | solution.py:447
  84.1 18.1 %collective-permute-start.23 = (bf16[272,384]{1,0:T(8,128)(2,1)S(1)}, bf16[272,384]{1,0:T(8,128)(2,1)S(1)}, u32[]{:S(2)}, u32[]{:S(2)}) collective-permute-start(bf16[272,384]{1,0:T(8,128)(2,1)S(1)} %get-tuple-element.87.refs_2_), channel_id=1, source_target_pairs={{0,96},{32,0},{64,32},{96,64},{1,97},{33,1},{65,33},{97,65},{2,98}... | collective-permute-start | bytes 626696 | tf_op jit(solution)/shard_map/ppermute | solution.py:447
  102.6 13.7 %collective-permute-start.24 = (bf16[272,384]{1,0:T(8,128)(2,1)S(1)}, bf16[272,384]{1,0:T(8,128)(2,1)S(1)}, u32[]{:S(2)}, u32[]{:S(2)}) collective-permute-start(bf16[272,384]{1,0:T(8,128)(2,1)S(1)} %get-tuple-element.92), channel_id=1, source_target_pairs={{0,4},{4,0},{1,5},{5,1},{2,6},{6,2},{3,7},{7,3},{8,12},{12,8},{9,1... | collective-permute-start | bytes 626696 | tf_op jit(solution)/shard_map/ppermute | solution.py:447
  104.3 6.7 %collective-permute-start.12 = (bf16[128,640]{1,0:T(8,128)(2,1)S(1)}, bf16[128,640]{1,0:T(8,128)(2,1)S(1)}, u32[]{:S(2)}, u32[]{:S(2)}) collective-permute-start(bf16[128,640]{1,0:T(8,128)(2,1)S(1)} %get-tuple-element.77), channel_id=1, source_target_pairs={{0,32},{32,64},{64,96},{96,0},{1,33},{33,65},{65,97},{97,1},{2,34}... | collective-permute-start | bytes 491528 | tf_op jit(solution)/shard_map/ppermute | solution.py:447
  105.6 10.1 %collective-permute-start.13 = (bf16[128,640]{1,0:T(8,128)(2,1)S(1)}, bf16[128,640]{1,0:T(8,128)(2,1)S(1)}, u32[]{:S(2)}, u32[]{:S(2)}) collective-permute-start(bf16[128,640]{1,0:T(8,128)(2,1)S(1)} %get-tuple-element.78), channel_id=1, source_target_pairs={{0,64},{32,96},{64,0},{96,32},{1,65},{33,97},{65,1},{97,33},{2,66}... | collective-permute-start | bytes 491528 | tf_op jit(solution)/shard_map/ppermute | solution.py:447
  108.4 7.3 %collective-permute-start.14 = (bf16[128,640]{1,0:T(8,128)(2,1)S(1)}, bf16[128,640]{1,0:T(8,128)(2,1)S(1)}, u32[]{:S(2)}, u32[]{:S(2)}) collective-permute-start(bf16[128,640]{1,0:T(8,128)(2,1)S(1)} %get-tuple-element.79), channel_id=1, source_target_pairs={{0,96},{32,0},{64,32},{96,64},{1,97},{33,1},{65,33},{97,65},{2,98}... | collective-permute-start | bytes 491528 | tf_op jit(solution)/shard_map/ppermute | solution.py:447
  115.8 8.3 %collective-permute-start.15 = (bf16[64,640]{1,0:T(8,128)(2,1)S(1)}, bf16[64,640]{1,0:T(8,128)(2,1)S(1)}, u32[]{:S(2)}, u32[]{:S(2)}) collective-permute-start(bf16[64,640]{1,0:T(8,128)(2,1)S(1)} %get-tuple-element.81), channel_id=1, source_target_pairs={{0,4},{4,0},{1,5},{5,1},{2,6},{6,2},{3,7},{7,3},{8,12},{12,8},{9,1... | collective-permute-start | bytes 245768 | tf_op jit(solution)/shard_map/ppermute | solution.py:447
  116.3 5.5 %collective-permute-start.25 = (bf16[80,384]{1,0:T(8,128)(2,1)S(1)}, bf16[80,384]{1,0:T(8,128)(2,1)S(1)}, u32[]{:S(2)}, u32[]{:S(2)}) collective-permute-start(bf16[80,384]{1,0:T(8,128)(2,1)S(1)} %get-tuple-element.95), channel_id=1, source_target_pairs={{0,8},{8,16},{16,24},{24,0},{1,9},{9,17},{17,25},{25,1},{2,10},{10... | collective-permute-start | bytes 184328 | tf_op jit(solution)/shard_map/ppermute | solution.py:447
  117.3 5.7 %collective-permute-start.26 = (bf16[80,384]{1,0:T(8,128)(2,1)S(1)}, bf16[80,384]{1,0:T(8,128)(2,1)S(1)}, u32[]{:S(2)}, u32[]{:S(2)}) collective-permute-start(bf16[80,384]{1,0:T(8,128)(2,1)S(1)} %get-tuple-element.96), channel_id=1, source_target_pairs={{0,16},{8,24},{16,0},{24,8},{1,17},{9,25},{17,1},{25,9},{2,18},{10... | collective-permute-start | bytes 184328 | tf_op jit(solution)/shard_map/ppermute | solution.py:447
  118.9 4.5 %collective-permute-start.27 = (bf16[80,384]{1,0:T(8,128)(2,1)S(1)}, bf16[80,384]{1,0:T(8,128)(2,1)S(1)}, u32[]{:S(2)}, u32[]{:S(2)}) collective-permute-start(bf16[80,384]{1,0:T(8,128)(2,1)S(1)} %get-tuple-element.97), channel_id=1, source_target_pairs={{0,24},{8,0},{16,8},{24,16},{1,25},{9,1},{17,9},{25,17},{2,26},{10... | collective-permute-start | bytes 184328 | tf_op jit(solution)/shard_map/ppermute | solution.py:447
  (2 other events, 3.1 us)
